TPU v7x, 128 devices: a whole 4x4x4 slice. The times are simulated.
128 devices in a mesh: orow: 16 (over z, x), ocol: 8 (over y, core).
Axes of the slice: x: 4, y: 4, z: 4, core: 2. Of those that a mesh axis runs over, the one named last changes fastest.
Arguments:
- integrals: bfloat16 [2304, 32, 384], P('ocol', 'orow'), may hold values from -0.29882812 to 0.29882812
- occ_count: int32 [16], replicated, may hold values from 1 to 2
- occ_energy: float32 [32], replicated, may hold values from -2 to -0.5
- vir_energy: float32 [384], replicated, may hold values from 0.3 to 2.5
- task_iblock: int32 [64, 1], replicated, may hold values from 0 to 15; in each aligned block of 64 rows (0 to 63, 64 to 127, ...) at most 8 rows name the same one
- task_jblock: int32 [64], replicated, may hold values from 0 to 15
Outputs:
- gamma_out: float32 [2304, 32, 384], P('ocol', 'orow')
- density: float32 [384, 384], replicated
Inputs may be any that keep to these rules, and one draw needn't show every extreme that they name: `task_iblock`: no first block is named by more than 8 tasks, and some first block by exactly 8.
All inputs are finite; a program needn't handle non-finite values.
Results may differ from a plain program's by a relative error of at most 0.0019.
Values may be sent and summed in bfloat16 or wider, within the bound.
No kernel may reach another device: no remote copies, remote signals or barrier semaphores. Data moves between devices by JAX's collectives and lax.ppermute only.
A program may use at most 128 MiB of HBM per device.

v0:
```python
import jax
import jax.numpy as jnp
from jax import lax
from jax.experimental import pallas as pl
from jax.experimental.pallas import tpu as pltpu
from jax.sharding import Mesh
from jax.sharding import PartitionSpec as P


AXES = ("z", "x", "y", "c")
OROW = ("z", "x")
OCOL = ("y", "c")
BF16 = jnp.bfloat16
F32 = jnp.float32
ANY = pl.BlockSpec(memory_space=pl.ANY)
SMEM = pl.BlockSpec(memory_space=pltpu.SMEM)


def move(x, axis, s):
    n = lax.axis_size(axis)
    return lax.ppermute(x, axis, [(i, (i + s) % n) for i in range(n)])


def swap(x):
    return lax.ppermute(x, "c", [(0, 1), (1, 0)])


def to_plane():
    pairs = []
    for z in range(4):
        for x in range(4):
            for y in range(4):
                for c in range(2):
                    source = ((z * 4 + x) * 4 + y) * 2 + c
                    target = (((2 * (z // 2) + c) * 4 + (x + y) % 4) * 4 + x) * 2 + z % 2
                    pairs.append((source, target))
    return pairs


def turn_kernel(slot_ref, *refs):
    pieces, out_ref, held, sem = refs[:8], refs[8], refs[9], refs[10]
    rows = pieces[0].shape[1]
    copies = [
        pltpu.make_async_copy(
            piece, held.at[:, pl.ds(pl.multiple_of(slot_ref[n] * rows, rows), rows), :], sem.at[n]
        )
        for n, piece in enumerate(pieces)
    ]
    for copy in copies:
        copy.start()
    for copy in copies:
        copy.wait()
    v = held.shape[2]
    for i in range(2):
        out_ref[i * v : (i + 1) * v, :] = held[i].T


def amp_kernel(place_ref, scal_ref, left_ref, row_ref, col_ref, *refs):
    sets_a, sets_b = refs[0:4], refs[4:8]
    ampt_ref, dens_ref, right_ref = refs[8:11]
    held, k_ref, amp_ref, sem, out_sem = refs[11:]
    rows, v = sets_a[0].shape[1:]

    def piece(source, slot, h, half):
        at = pl.ds(pl.multiple_of(slot * rows, rows), rows)
        return pltpu.make_async_copy(
            source, held.at[h, at, half * v : (half + 1) * v], sem.at[h]
        )

    for s in range(4):
        for t in range(4):
            for source, zs, xs, half in ((sets_a[s], s, t, 0), (sets_b[s], t, s, 1)):
                zz = place_ref[zs]
                piece(
                    source.at[t], 2 * place_ref[4 + xs] + lax.rem(zz, 2), zz // 2, half
                ).start()
    for h in range(2):
        for _ in range(16):
            piece(sets_a[0].at[0], 0, h, 0).wait()
        copy_out = pltpu.make_async_copy(held.at[h], right_ref.at[h], out_sem.at[h])
        copy_out.start()
        k_ref[...] = jnp.dot(left_ref[...], held[h], preferred_element_type=F32)
        for i in range(2):
            for j in range(2):
                a, b = slice(i * v, (i + 1) * v), slice(j * v, (j + 1) * v)
                k = k_ref[a, b]
                kt = k.T
                pair = scal_ref[i] + scal_ref[2 + 2 * h + j]
                both = scal_ref[10 + i] * scal_ref[12 + 2 * h + j]
                delta = (pair - col_ref[...]) - row_ref[...]
                amp_ref[a, b] = (both * ((2.0 * k - kt) / delta)).astype(BF16)
                ampt_ref[h, b, a] = (both * ((2.0 * kt - k) / delta)).astype(BF16)
        part = None
        for i in range(2):
            a = slice(i * v, (i + 1) * v)
            prod = jnp.dot(amp_ref[a, :], ampt_ref[h, :, a], preferred_element_type=F32)
            part = prod if part is None else part + prod
        part = scal_ref[6 + h] * part
        if h == 0:
            dens_ref[...] = part
        else:
            dens_ref[...] += part
    for h in range(2):
        pltpu.make_async_copy(held.at[h], right_ref.at[h], out_sem.at[h]).wait()


def gamma_kernel(slot_ref, scal_ref, mine_ref, other_ref, ampt_ref, keep_ref, give_ref):
    for right_ref, out_ref in ((other_ref, give_ref), (mine_ref, keep_ref)):
        total = scal_ref[8] * jnp.dot(right_ref[0], ampt_ref[0], preferred_element_type=F32)
        out_ref[0] = total + scal_ref[9] * jnp.dot(
            right_ref[1], ampt_ref[1], preferred_element_type=F32
        )


def swap_bits(x, axis, bits):
    return lax.ppermute(x, axis, [(i, i ^ bits) for i in range(lax.axis_size(axis))])


def halves_of(x, second):
    low, high = jnp.split(x, 2)
    return jnp.where(second, high, low), jnp.where(second, low, high)


def joined(mine, other, second):
    return jnp.where(
        second, jnp.concatenate([other, mine]), jnp.concatenate([mine, other])
    )


def local(integrals, occ_count, occ_energy, vir_energy, task_iblock, task_jblock):
    rows, orbitals, v = integrals.shape
    z, x, y, c = (lax.axis_index(a) for a in AXES)
    my_row = z * 4 + x
    steps = jnp.arange(4)
    shard = jnp.swapaxes(integrals, 0, 1)

    planed = lax.ppermute(shard, AXES, to_plane())
    shard, planed = lax.optimization_barrier((shard, planed))
    around = [shard] + [move(shard, "y", s) for s in (1, 2, 3)]
    across = [swap(p) for p in around]
    first_a = jnp.stack([planed[0]] + [move(planed[0], "x", s) for s in (1, 2, 3)])
    first_b = jnp.stack([planed[1]] + [move(planed[1], "z", s) for s in (1, 2, 3)])
    sets_a = [first_a] + [move(first_a, "z", s) for s in (1, 2, 3)]
    sets_b = [first_b] + [move(first_b, "x", s) for s in (1, 2, 3)]

    ys = (y - steps) % 4
    slots = jnp.concatenate([2 * ys + c, 2 * ys + 1 - c]).astype(jnp.int32)
    place = jnp.concatenate([(z - steps) % 4, (x - steps - y) % 4]).astype(jnp.int32)
    blocks = 4 * (2 * jnp.arange(2) + c) + y
    first, second = task_iblock[:, 0], task_jblock
    ours = ((first == my_row)[:, None] & (second[:, None] == blocks[None])).sum(0)
    theirs = ((second == my_row)[:, None] & (first[:, None] == blocks[None])).sum(0)
    energy = occ_energy.reshape(-1, orbitals)
    used = jnp.arange(orbitals)[None, :] < occ_count[:, None]
    scal = jnp.concatenate(
        [
            energy[my_row],
            energy[blocks].reshape(-1),
            ours.astype(F32),
            (ours + theirs).astype(F32),
            used[my_row].astype(F32),
            used[blocks].reshape(-1).astype(F32),
        ]
    )

    left = pl.pallas_call(
        turn_kernel,
        in_specs=[SMEM] + [ANY] * 8,
        out_specs=pl.BlockSpec(memory_space=pltpu.VMEM),
        out_shape=jax.ShapeDtypeStruct((2 * v, 8 * rows), BF16),
        scratch_shapes=[pltpu.VMEM((2, 8 * rows, v), BF16), pltpu.SemaphoreType.DMA((8,))],
        cost_estimate=pl.CostEstimate(flops=0, bytes_accessed=7_000_000, transcendentals=0),
        name="turn",
    )(slots, *around, *across)

    vmem = pl.BlockSpec(memory_space=pltpu.VMEM)
    ampt, dens, right = pl.pallas_call(
        amp_kernel,
        in_specs=[SMEM, SMEM, vmem, vmem, vmem] + [ANY] * 8,
        out_specs=[vmem, vmem, ANY],
        out_shape=[
            jax.ShapeDtypeStruct((2, 2 * v, 2 * v), BF16),
            jax.ShapeDtypeStruct((v, v), F32),
            jax.ShapeDtypeStruct((2, 8 * rows, 2 * v), BF16),
        ],
        scratch_shapes=[
            pltpu.VMEM((2, 8 * rows, 2 * v), BF16),
            pltpu.VMEM((2 * v, 2 * v), F32),
            pltpu.VMEM((2 * v, 2 * v), BF16),
            pltpu.SemaphoreType.DMA((2,)),
            pltpu.SemaphoreType.DMA((2,)),
        ],
        cost_estimate=pl.CostEstimate(
            flops=6_200_000_000, bytes_accessed=20_000_000, transcendentals=0
        ),
        name="amplitudes",
    )(place, scal, left, vir_energy.reshape(1, -1), vir_energy.reshape(-1, 1), *sets_a, *sets_b)

    def gamma_parts(ends):
        at = 2 * ((y + jnp.array(ends)) % 4)
        slot = jnp.stack([at + c, at + 1 - c]).astype(jnp.int32)
        width = 2 * v
        return pl.pallas_call(
            gamma_kernel,
            grid_spec=pltpu.PrefetchScalarGridSpec(
                num_scalar_prefetch=1,
                grid=(len(ends),),
                in_specs=[
                    SMEM,
                    pl.BlockSpec((2, rows, width), lambda n, slot: (0, slot[0, n], 0)),
                    pl.BlockSpec((2, rows, width), lambda n, slot: (0, slot[1, n], 0)),
                    pl.BlockSpec((2, width, width), lambda n, slot: (0, 0, 0)),
                ],
                out_specs=[pl.BlockSpec((1, rows, width), lambda n, slot: (n, 0, 0))] * 2,
            ),
            out_shape=[jax.ShapeDtypeStruct((len(ends), rows, width), F32)] * 2,
            cost_estimate=pl.CostEstimate(
                flops=1_360_000_000 * len(ends), bytes_accessed=10_000_000, transcendentals=0
            ),
        )(slot, scal, right, right, ampt)

    low, high = halves_of(dens, c == 1)
    dens_got = swap(high)
    keep, give = gamma_parts((2, 1))
    got = swap(give)
    keep_near, give_near = gamma_parts((3, 0))
    got_near = swap(give_near)
    to_far, to_next = (keep[0] + got[0]).astype(BF16), (keep[1] + got[1]).astype(BF16)
    far = move(to_far, "y", 2)
    next_one = move(to_next, "y", 1)
    to_last = (keep_near[0] + got_near[0]).astype(BF16)
    last_one = move(to_last, "y", 3)
    gamma = keep_near[1] + got_near[1]
    gamma = gamma + next_one.astype(F32) + last_one.astype(F32) + far.astype(F32)
    gamma_out = gamma.reshape(rows, orbitals, v)

    own = low + dens_got
    upper, odd = y // 2 == 1, y % 2 == 1
    for bits, second in ((3, upper), (1, odd)):
        own, sent = halves_of(own, second)
        got = swap_bits(sent, "y", bits)
        own = own + got
    for axis in ("x", "z"):
        for bits in (1, 3):
            got = swap_bits(own, axis, bits)
            own = own + got
    own = own / task_iblock.shape[0]
    for bits, second in ((1, odd), (3, upper)):
        got = swap_bits(own, "y", bits)
        own = joined(own, got, second)
    got = swap(own)
    density = joined(own, got, c == 1)
    return gamma_out, density


def solution(mesh):
    finer = Mesh(mesh.devices.reshape(4, 4, 4, 2), AXES)
    placed = (P(OCOL, OROW, None), P(), P(), P(), P(), P())
    return jax.shard_map(
        local, mesh=finer, in_specs=placed, out_specs=(P(OCOL, OROW, None), P()), check_vma=False
    )
```

profile of v0, /device:TPU:0, one launch (start us, length us, event | category | flops | bytes accessed | tf_op | source)
XLA Modules:
  0.0 192.4 jit_solution(4901431362107497534)
XLA Ops:
  9.5 13.7 %collective-permute-start.9 = (bf16[288,384]{1,0:T(8,128)(2,1)S(1)}, bf16[288,384]{1,0:T(8,128)(2,1)S(1)}, u32[]{:S(2)}, u32[]{:S(2)}) collective-permute-start(bf16[288,384]{1,0:T(8,128)(2,1)S(1)} %get-tuple-element.29), channel_id=1, source_target_pairs={{0,16},{8,24},{16,0},{24,8},{1,17},{9,25},{17,1},{25,9},{2,18},{10... | collective-permute-start | bytes 663560 | tf_op jit(solution)/shard_map/ppermute | solution.py:21
  30.8 3.3 %collective-permute-done.10 = bf16[288,384]{1,0:T(8,128)(2,1)S(1)} collective-permute-done((bf16[288,384]{1,0:T(8,128)(2,1)S(1)}, bf16[288,384]{1,0:T(8,128)(2,1)S(1)}, u32[]{:S(2)}, u32[]{:S(2)}) %collective-permute-start.10) | collective-permute-done | bytes 221216 | tf_op jit(solution)/shard_map/ppermute | solution.py:21
  35.1 3.6 %collective-permute-start.15 = (bf16[288,384]{1,0:T(8,128)(2,1)S(1)}, bf16[288,384]{1,0:T(8,128)(2,1)S(1)}, u32[]{:S(2)}, u32[]{:S(2)}) collective-permute-start(bf16[288,384]{1,0:T(8,128)(2,1)S(1)} %get-tuple-element.30), channel_id=1, source_target_pairs={{0,64},{32,96},{64,0},{96,32},{1,65},{33,97},{65,1},{97,33},{2,66}... | collective-permute-start | bytes 663560 | tf_op jit(solution)/shard_map/ppermute | solution.py:21
  39.1 5.8 %collective-permute-done.15 = bf16[288,384]{1,0:T(8,128)(2,1)S(1)} collective-permute-done((bf16[288,384]{1,0:T(8,128)(2,1)S(1)}, bf16[288,384]{1,0:T(8,128)(2,1)S(1)}, u32[]{:S(2)}, u32[]{:S(2)}) %collective-permute-start.15) | collective-permute-done | bytes 221216 | tf_op jit(solution)/shard_map/ppermute | solution.py:21
  45.7 5.2 %collective-permute-done.16 = bf16[288,384]{1,0:T(8,128)(2,1)S(1)} collective-permute-done((bf16[288,384]{1,0:T(8,128)(2,1)S(1)}, bf16[288,384]{1,0:T(8,128)(2,1)S(1)}, u32[]{:S(2)}, u32[]{:S(2)}) %collective-permute-start.16) | collective-permute-done | bytes 221216 | tf_op jit(solution)/shard_map/ppermute | solution.py:21
  55.0 3.1 %collective-permute-start.12 = (bf16[4,288,384]{2,1,0:T(8,128)(2,1)S(1)}, bf16[4,288,384]{2,1,0:T(8,128)(2,1)}, u32[]{:S(2)}, u32[]{:S(2)}) collective-permute-start(bf16[4,288,384]{2,1,0:T(8,128)(2,1)S(1)} %pad_maximum_fusion.refs_0_), channel_id=1, source_target_pairs={{0,64},{32,96},{64,0},{96,32},{1,65},{33,97},{65,1},{97,33},{2,66}... | collective-permute-start | bytes 2654216 | tf_op jit(solution)/shard_map/ppermute | solution.py:21
  67.8 5.6 %turn.1.left_ref = bf16[768,2304]{1,0:T(8,128)(2,1)} custom-call(s32[8]{0:T(128)} %pad_add_fusion.3.slot_ref, bf16[2,288,384]{2,1,0:T(8,128)(2,1)} %bitcast.49, bf16[2,288,384]{2,1,0:T(8,128)(2,1)} %copy-done.6, bf16[2,288,384]{2,1,0:T(8,128)(2,1)} %copy-done.7, bf16[2,288,384]{2,1,0:T(8,128)(2,1)} %collective-permute-done.3.refs_3_, ...), custom_call_target="tpu_custom_call" | custom-call | bytes 7000000 | tf_op jit(solution)/shard_map/turn/pallas_call | solution.py:166
  73.4 8.2 %collective-permute-done.12.refs_2_ = bf16[4,288,384]{2,1,0:T(8,128)(2,1)} collective-permute-done((bf16[4,288,384]{2,1,0:T(8,128)(2,1)S(1)}, bf16[4,288,384]{2,1,0:T(8,128)(2,1)}, u32[]{:S(2)}, u32[]{:S(2)}) %collective-permute-start.12) | collective-permute-done | bytes 884768 | tf_op jit(solution)/shard_map/ppermute | solution.py:21
  81.6 13.9 %collective-permute-done.13.refs_3_ = bf16[4,288,384]{2,1,0:T(8,128)(2,1)} collective-permute-done((bf16[4,288,384]{2,1,0:T(8,128)(2,1)S(1)}, bf16[4,288,384]{2,1,0:T(8,128)(2,1)}, u32[]{:S(2)}, u32[]{:S(2)}) %collective-permute-start.13) | collective-permute-done | bytes 884768 | tf_op jit(solution)/shard_map/ppermute | solution.py:21
  95.5 4.7 %collective-permute-done.18.refs_6_ = bf16[4,288,384]{2,1,0:T(8,128)(2,1)} collective-permute-done((bf16[4,288,384]{2,1,0:T(8,128)(2,1)S(1)}, bf16[4,288,384]{2,1,0:T(8,128)(2,1)}, u32[]{:S(2)}, u32[]{:S(2)}) %collective-permute-start.18) | collective-permute-done | bytes 884768 | tf_op jit(solution)/shard_map/ppermute | solution.py:21
  100.9 17.1 %amplitudes.1 = (bf16[2,768,768]{2,1,0:T(8,128)(2,1)}, f32[384,384]{1,0:T(8,128)}, bf16[2,2304,768]{2,1,0:T(8,128)(2,1)}) custom-call(s32[8]{0:T(128)} %pad_add_fusion.2.place_ref, f32[16]{0:T(128)} %concatenate.27.scal_ref, bf16[768,2304]{1,0:T(8,128)(2,1)} %turn.1.left_ref, f32[1,384]{1,0:T(1,128)} %reshape.68.row_ref, f32[384,1]{1,0:T(8,128)} %reshape.89.col_ref, ...), custom_call_target="tpu_custom_call" | custom-call | flops 6200000000 | bytes 20000000 | tf_op jit(solution)/shard_map/amplitudes/pallas_call | solution.py:177
  119.8 7.1 %shard_map.95 = (f32[2,288,768]{2,1,0:T(8,128)}, f32[2,288,768]{2,1,0:T(8,128)}) custom-call(s32[2,2]{1,0:T(2,128)} %pad_add_fusion.slot_ref, f32[16]{0:T(128)} %concatenate.27.scal_ref, bf16[2,2304,768]{2,1,0:T(8,128)(2,1)} %get-tuple-element.13.mine_ref.other_ref, bf16[2,2304,768]{2,1,0:T(8,128)(2,1)} %get-tuple-element.13.mine_ref.other_ref, ...), custom_call_target="tpu_custom_call" | custom-call | flops 2720000000 | bytes 10000000 | tf_op jit(solution)/shard_map/pallas_call | solution.py:203
  130.2 7.0 %shard_map.96 = (f32[2,288,768]{2,1,0:T(8,128)}, f32[2,288,768]{2,1,0:T(8,128)}) custom-call(s32[2,2]{1,0:T(2,128)} %pad_add_fusion.1.slot_ref, f32[16]{0:T(128)} %concatenate.27.scal_ref, bf16[2,2304,768]{2,1,0:T(8,128)(2,1)} %get-tuple-element.13.mine_ref.other_ref, bf16[2,2304,768]{2,1,0:T(8,128)(2,1)} %get-tuple-element.13.mine_ref.other_ref, ...), custom_call_target="tpu_custom_call" | custom-call | flops 2720000000 | bytes 10000000 | tf_op jit(solution)/shard_map/pallas_call | solution.py:203
  137.4 4.6 %collective-permute-done.27 = f32[48,384]{1,0:T(8,128)S(1)} collective-permute-done((f32[48,384]{1,0:T(8,128)S(1)}, f32[48,384]{1,0:T(8,128)S(1)}, u32[]{:S(2)}, u32[]{:S(2)}) %collective-permute-start.27) | collective-permute-done | bytes 73760 | tf_op jit(solution)/shard_map/ppermute | solution.py:116
  142.4 4.1 %collective-permute-done.28 = f32[48,384]{1,0:T(8,128)S(1)} collective-permute-done((f32[48,384]{1,0:T(8,128)S(1)}, f32[48,384]{1,0:T(8,128)S(1)}, u32[]{:S(2)}, u32[]{:S(2)}) %collective-permute-start.28) | collective-permute-done | bytes 73760 | tf_op jit(solution)/shard_map/ppermute | solution.py:116
  146.5 2.9 %collective-permute-start.29 = (f32[48,384]{1,0:T(8,128)S(1)}, f32[48,384]{1,0:T(8,128)S(1)}, u32[]{:S(2)}, u32[]{:S(2)}) collective-permute-start(f32[48,384]{1,0:T(8,128)S(1)} %add.209), channel_id=1, source_target_pairs={{0,24},{8,16},{16,8},{24,0},{1,25},{9,17},{17,9},{25,1},{2,26},{10... | collective-permute-start | bytes 221192 | tf_op jit(solution)/shard_map/ppermute | solution.py:116
  149.4 2.9 %collective-permute-done.29 = f32[48,384]{1,0:T(8,128)S(1)} collective-permute-done((f32[48,384]{1,0:T(8,128)S(1)}, f32[48,384]{1,0:T(8,128)S(1)}, u32[]{:S(2)}, u32[]{:S(2)}) %collective-permute-start.29) | collective-permute-done | bytes 73760 | tf_op jit(solution)/shard_map/ppermute | solution.py:116
  153.9 3.0 %collective-permute-done.30 = f32[48,384]{1,0:T(8,128)S(1)} collective-permute-done((f32[48,384]{1,0:T(8,128)S(1)}, f32[48,384]{1,0:T(8,128)S(1)}, u32[]{:S(2)}, u32[]{:S(2)}) %collective-permute-start.30) | collective-permute-done | bytes 73760 | tf_op jit(solution)/shard_map/ppermute | solution.py:116
  157.6 4.8 %collective-permute-done.31 = f32[48,384]{1,0:T(8,128)S(1)} collective-permute-done((f32[48,384]{1,0:T(8,128)S(1)}, f32[48,384]{1,0:T(8,128)S(1)}, u32[]{:S(2)}, u32[]{:S(2)}) %collective-permute-start.31) | collective-permute-done | bytes 73760 | tf_op jit(solution)/shard_map/ppermute | solution.py:116
  162.8 4.9 %collective-permute-done.32 = f32[48,384]{1,0:T(8,128)S(1)} collective-permute-done((f32[48,384]{1,0:T(8,128)S(1)}, f32[48,384]{1,0:T(8,128)S(1)}, u32[]{:S(2)}, u32[]{:S(2)}) %collective-permute-start.32) | collective-permute-done | bytes 73760 | tf_op jit(solution)/shard_map/ppermute | solution.py:116
  169.1 3.3 %collective-permute-start.23 = (bf16[288,768]{1,0:T(8,128)(2,1)S(1)}, bf16[288,768]{1,0:T(8,128)(2,1)S(1)}, u32[]{:S(2)}, u32[]{:S(2)}) collective-permute-start(bf16[288,768]{1,0:T(8,128)(2,1)S(1)} %fusion.8), channel_id=1, source_target_pairs={{0,6},{2,0},{4,2},{6,4},{1,7},{3,1},{5,3},{7,5},{8,14},{10,8},{12,... | collective-permute-start | bytes 1327112 | tf_op jit(solution)/shard_map/ppermute | solution.py:21
  174.2 5.9 %collective-permute-done.33 = f32[96,384]{1,0:T(8,128)S(1)} collective-permute-done((f32[96,384]{1,0:T(8,128)S(1)}, f32[96,384]{1,0:T(8,128)S(1)}, u32[]{:S(2)}, u32[]{:S(2)}) %collective-permute-start.33) | collective-permute-done | bytes 147488 | tf_op jit(solution)/shard_map/ppermute | solution.py:116
  182.7 3.2 %collective-permute-done.23 = bf16[288,768]{1,0:T(8,128)(2,1)S(1)} collective-permute-done((bf16[288,768]{1,0:T(8,128)(2,1)S(1)}, bf16[288,768]{1,0:T(8,128)(2,1)S(1)}, u32[]{:S(2)}, u32[]{:S(2)}) %collective-permute-start.23) | collective-permute-done | bytes 442400 | tf_op jit(solution)/shard_map/ppermute | solution.py:21
  185.8 3.8 %collective-permute-done.22 = bf16[288,768]{1,0:T(8,128)(2,1)S(1)} collective-permute-done((bf16[288,768]{1,0:T(8,128)(2,1)S(1)}, bf16[288,768]{1,0:T(8,128)(2,1)S(1)}, u32[]{:S(2)}, u32[]{:S(2)}) %collective-permute-start.22) | collective-permute-done | bytes 442400 | tf_op jit(solution)/shard_map/ppermute | solution.py:21
  (135 shorter events, 49.7 us)
Async XLA Ops:
  1.7 7.7 %collective-permute-start = (bf16[2,288,384]{2,1,0:T(8,128)(2,1)S(1)}, bf16[2,288,384]{2,1,0:T(8,128)(2,1)S(1)}, u32[]{:S(2)}, u32[]{:S(2)}) collective-permute-start(bf16[2,288,384]{2,1,0:T(8,128)(2,1)S(1)} %bitcast.44), channel_id=1, source_target_pairs={{0,0},{1,32},{2,8},{3,40},{4,16},{5,48},{6,24},{7,56},{8,10},{9,42... | collective-permute-start | bytes 1327112 | tf_op jit(solution)/shard_map/ppermute | solution.py:137
  9.5 19.9 %collective-permute-start.9 = (bf16[288,384]{1,0:T(8,128)(2,1)S(1)}, bf16[288,384]{1,0:T(8,128)(2,1)S(1)}, u32[]{:S(2)}, u32[]{:S(2)}) collective-permute-start(bf16[288,384]{1,0:T(8,128)(2,1)S(1)} %get-tuple-element.29), channel_id=1, source_target_pairs={{0,16},{8,24},{16,0},{24,8},{1,17},{9,25},{17,1},{25,9},{2,18},{10... | collective-permute-start | bytes 663560 | tf_op jit(solution)/shard_map/ppermute | solution.py:21
  23.2 10.9 %collective-permute-start.10 = (bf16[288,384]{1,0:T(8,128)(2,1)S(1)}, bf16[288,384]{1,0:T(8,128)(2,1)S(1)}, u32[]{:S(2)}, u32[]{:S(2)}) collective-permute-start(bf16[288,384]{1,0:T(8,128)(2,1)S(1)} %get-tuple-element.29), channel_id=1, source_target_pairs={{0,24},{8,0},{16,8},{24,16},{1,25},{9,1},{17,9},{25,17},{2,26},{10... | collective-permute-start | bytes 663560 | tf_op jit(solution)/shard_map/ppermute | solution.py:21
  23.2 11.8 %collective-permute-start.8 = (bf16[288,384]{1,0:T(8,128)(2,1)S(1)}, bf16[288,384]{1,0:T(8,128)(2,1)S(1)}, u32[]{:S(2)}, u32[]{:S(2)}) collective-permute-start(bf16[288,384]{1,0:T(8,128)(2,1)S(1)} %get-tuple-element.29), channel_id=1, source_target_pairs={{0,8},{8,16},{16,24},{24,0},{1,9},{9,17},{17,25},{25,1},{2,10},{10... | collective-permute-start | bytes 663560 | tf_op jit(solution)/shard_map/ppermute | solution.py:21
  25.3 13.5 %collective-permute-start.14 = (bf16[288,384]{1,0:T(8,128)(2,1)S(1)}, bf16[288,384]{1,0:T(8,128)(2,1)S(1)}, u32[]{:S(2)}, u32[]{:S(2)}) collective-permute-start(bf16[288,384]{1,0:T(8,128)(2,1)S(1)} %get-tuple-element.30), channel_id=1, source_target_pairs={{0,32},{32,64},{64,96},{96,0},{1,33},{33,65},{65,97},{97,1},{2,34}... | collective-permute-start | bytes 663560 | tf_op jit(solution)/shard_map/ppermute | solution.py:21
  27.5 23.3 %collective-permute-start.1 = (bf16[2,288,384]{2,1,0:T(8,128)(2,1)S(1)}, bf16[2,288,384]{2,1,0:T(8,128)(2,1)S(1)}, u32[]{:S(2)}, u32[]{:S(2)}) collective-permute-start(bf16[2,288,384]{2,1,0:T(8,128)(2,1)S(1)} %bitcast.45), channel_id=1, source_target_pairs={{0,2},{2,4},{4,6},{6,0},{1,3},{3,5},{5,7},{7,1},{8,10},{10,12},{12... | collective-permute-start | bytes 1327112 | tf_op jit(solution)/shard_map/ppermute | solution.py:21
  29.5 21.9 %collective-permute-start.2 = (bf16[2,288,384]{2,1,0:T(8,128)(2,1)S(1)}, bf16[2,288,384]{2,1,0:T(8,128)(2,1)S(1)}, u32[]{:S(2)}, u32[]{:S(2)}) collective-permute-start(bf16[2,288,384]{2,1,0:T(8,128)(2,1)S(1)} %bitcast.46), channel_id=1, source_target_pairs={{0,4},{2,6},{4,0},{6,2},{1,5},{3,7},{5,1},{7,3},{8,12},{10,14},{12... | collective-permute-start | bytes 1327112 | tf_op jit(solution)/shard_map/ppermute | solution.py:21
  34.1 19.0 %collective-permute-start.3 = (bf16[2,288,384]{2,1,0:T(8,128)(2,1)S(1)}, bf16[2,288,384]{2,1,0:T(8,128)(2,1)}, u32[]{:S(2)}, u32[]{:S(2)}) collective-permute-start(bf16[2,288,384]{2,1,0:T(8,128)(2,1)S(1)} %bitcast.47), channel_id=1, source_target_pairs={{0,6},{2,0},{4,2},{6,4},{1,7},{3,1},{5,3},{7,5},{8,14},{10,8},{12,... | collective-permute-start | bytes 1327112 | tf_op jit(solution)/shard_map/ppermute | solution.py:21
  35.1 9.9 %collective-permute-start.15 = (bf16[288,384]{1,0:T(8,128)(2,1)S(1)}, bf16[288,384]{1,0:T(8,128)(2,1)S(1)}, u32[]{:S(2)}, u32[]{:S(2)}) collective-permute-start(bf16[288,384]{1,0:T(8,128)(2,1)S(1)} %get-tuple-element.30), channel_id=1, source_target_pairs={{0,64},{32,96},{64,0},{96,32},{1,65},{33,97},{65,1},{97,33},{2,66}... | collective-permute-start | bytes 663560 | tf_op jit(solution)/shard_map/ppermute | solution.py:21
  38.8 25.2 %collective-permute-start.11 = (bf16[4,288,384]{2,1,0:T(8,128)(2,1)S(1)}, bf16[4,288,384]{2,1,0:T(8,128)(2,1)}, u32[]{:S(2)}, u32[]{:S(2)}) collective-permute-start(bf16[4,288,384]{2,1,0:T(8,128)(2,1)S(1)} %pad_maximum_fusion.refs_0_), channel_id=1, source_target_pairs={{0,32},{32,64},{64,96},{96,0},{1,33},{33,65},{65,97},{97,1},{2,34}... | collective-permute-start | bytes 2654216 | tf_op jit(solution)/shard_map/ppermute | solution.py:21
  50.9 7.2 %collective-permute-start.5 = (bf16[2,288,384]{2,1,0:T(8,128)(2,1)S(1)}, bf16[2,288,384]{2,1,0:T(8,128)(2,1)S(1)}, u32[]{:S(2)}, u32[]{:S(2)}) collective-permute-start(bf16[2,288,384]{2,1,0:T(8,128)(2,1)S(1)} %collective-permute-done.1.refs_1_), channel_id=1, source_target_pairs={{0,1},{1,0},{2,3},{3,2},{4,5},{5,4},{6,7},{7,6},{8,9},{9,8},{10,11... | collective-permute-start | bytes 1327112 | tf_op jit(solution)/shard_map/ppermute | solution.py:25
  55.0 26.6 %collective-permute-start.12 = (bf16[4,288,384]{2,1,0:T(8,128)(2,1)S(1)}, bf16[4,288,384]{2,1,0:T(8,128)(2,1)}, u32[]{:S(2)}, u32[]{:S(2)}) collective-permute-start(bf16[4,288,384]{2,1,0:T(8,128)(2,1)S(1)} %pad_maximum_fusion.refs_0_), channel_id=1, source_target_pairs={{0,64},{32,96},{64,0},{96,32},{1,65},{33,97},{65,1},{97,33},{2,66}... | collective-permute-start | bytes 2654216 | tf_op jit(solution)/shard_map/ppermute | solution.py:21
  58.1 37.4 %collective-permute-start.13 = (bf16[4,288,384]{2,1,0:T(8,128)(2,1)S(1)}, bf16[4,288,384]{2,1,0:T(8,128)(2,1)}, u32[]{:S(2)}, u32[]{:S(2)}) collective-permute-start(bf16[4,288,384]{2,1,0:T(8,128)(2,1)S(1)} %pad_maximum_fusion.refs_0_), channel_id=1, source_target_pairs={{0,96},{32,0},{64,32},{96,64},{1,97},{33,1},{65,33},{97,65},{2,98}... | collective-permute-start | bytes 2654216 | tf_op jit(solution)/shard_map/ppermute | solution.py:21
  58.1 37.4 %collective-permute-start.17 = (bf16[4,288,384]{2,1,0:T(8,128)(2,1)S(1)}, bf16[4,288,384]{2,1,0:T(8,128)(2,1)}, u32[]{:S(2)}, u32[]{:S(2)}) collective-permute-start(bf16[4,288,384]{2,1,0:T(8,128)(2,1)S(1)} %pad_maximum_fusion.1.refs_4_), channel_id=1, source_target_pairs={{0,8},{8,16},{16,24},{24,0},{1,9},{9,17},{17,25},{25,1},{2,10},{10... | collective-permute-start | bytes 2654216 | tf_op jit(solution)/shard_map/ppermute | solution.py:21
  60.2 40.0 %collective-permute-start.18 = (bf16[4,288,384]{2,1,0:T(8,128)(2,1)S(1)}, bf16[4,288,384]{2,1,0:T(8,128)(2,1)}, u32[]{:S(2)}, u32[]{:S(2)}) collective-permute-start(bf16[4,288,384]{2,1,0:T(8,128)(2,1)S(1)} %pad_maximum_fusion.1.refs_4_), channel_id=1, source_target_pairs={{0,16},{8,24},{16,0},{24,8},{1,17},{9,25},{17,1},{25,9},{2,18},{10... | collective-permute-start | bytes 2654216 | tf_op jit(solution)/shard_map/ppermute | solution.py:21
  64.0 36.9 %collective-permute-start.19 = (bf16[4,288,384]{2,1,0:T(8,128)(2,1)S(1)}, bf16[4,288,384]{2,1,0:T(8,128)(2,1)}, u32[]{:S(2)}, u32[]{:S(2)}) collective-permute-start(bf16[4,288,384]{2,1,0:T(8,128)(2,1)S(1)} %pad_maximum_fusion.1.refs_4_), channel_id=1, source_target_pairs={{0,24},{8,0},{16,8},{24,16},{1,25},{9,1},{17,9},{25,17},{2,26},{10... | collective-permute-start | bytes 2654216 | tf_op jit(solution)/shard_map/ppermute | solution.py:21
  119.1 8.3 %collective-permute-start.25 = (f32[192,384]{1,0:T(8,128)S(1)}, f32[192,384]{1,0:T(8,128)S(1)}, u32[]{:S(2)}, u32[]{:S(2)}) collective-permute-start(f32[192,384]{1,0:T(8,128)S(1)} %slice_select_fusion), channel_id=1, source_target_pairs={{0,1},{1,0},{2,3},{3,2},{4,5},{5,4},{6,7},{7,6},{8,9},{9,8},{10,11... | collective-permute-start | bytes 884744 | tf_op jit(solution)/shard_map/ppermute | solution.py:25
  126.9 40.9 %collective-permute-start.20 = (f32[2,288,768]{2,1,0:T(8,128)}, f32[2,288,768]{2,1,0:T(8,128)}, u32[]{:S(2)}, u32[]{:S(2)}) collective-permute-start(f32[2,288,768]{2,1,0:T(8,128)} %get-tuple-element.16), channel_id=1, source_target_pairs={{0,1},{1,0},{2,3},{3,2},{4,5},{5,4},{6,7},{7,6},{8,9},{9,8},{10,11... | collective-permute-start | bytes 5308424 | tf_op jit(solution)/shard_map/ppermute | solution.py:25
  127.5 9.8 %collective-permute-start.26 = (f32[96,384]{1,0:T(8,128)S(1)}, f32[96,384]{1,0:T(8,128)S(1)}, u32[]{:S(2)}, u32[]{:S(2)}) collective-permute-start(f32[96,384]{1,0:T(8,128)S(1)} %slice_select_fusion.1), channel_id=1, source_target_pairs={{0,6},{2,4},{4,2},{6,0},{1,7},{3,5},{5,3},{7,1},{8,14},{10,12},{12... | collective-permute-start | bytes 442376 | tf_op jit(solution)/shard_map/ppermute | solution.py:116
  137.2 35.2 %collective-permute-start.21 = (f32[2,288,768]{2,1,0:T(8,128)}, f32[2,288,768]{2,1,0:T(8,128)S(1)}, u32[]{:S(2)}, u32[]{:S(2)}) collective-permute-start(f32[2,288,768]{2,1,0:T(8,128)} %get-tuple-element.18), channel_id=1, source_target_pairs={{0,1},{1,0},{2,3},{3,2},{4,5},{5,4},{6,7},{7,6},{8,9},{9,8},{10,11... | collective-permute-start | bytes 5308424 | tf_op jit(solution)/shard_map/ppermute | solution.py:25
  167.7 12.4 %collective-permute-start.33 = (f32[96,384]{1,0:T(8,128)S(1)}, f32[96,384]{1,0:T(8,128)S(1)}, u32[]{:S(2)}, u32[]{:S(2)}) collective-permute-start(f32[96,384]{1,0:T(8,128)S(1)} %maximum_select_fusion.2), channel_id=1, source_target_pairs={{0,6},{2,4},{4,2},{6,0},{1,7},{3,5},{5,3},{7,1},{8,14},{10,12},{12... | collective-permute-start | bytes 442376 | tf_op jit(solution)/shard_map/ppermute | solution.py:116
  169.1 16.7 %collective-permute-start.23 = (bf16[288,768]{1,0:T(8,128)(2,1)S(1)}, bf16[288,768]{1,0:T(8,128)(2,1)S(1)}, u32[]{:S(2)}, u32[]{:S(2)}) collective-permute-start(bf16[288,768]{1,0:T(8,128)(2,1)S(1)} %fusion.8), channel_id=1, source_target_pairs={{0,6},{2,0},{4,2},{6,4},{1,7},{3,1},{5,3},{7,5},{8,14},{10,8},{12,... | collective-permute-start | bytes 1327112 | tf_op jit(solution)/shard_map/ppermute | solution.py:21
  172.7 16.9 %collective-permute-start.22 = (bf16[288,768]{1,0:T(8,128)(2,1)S(1)}, bf16[288,768]{1,0:T(8,128)(2,1)S(1)}, u32[]{:S(2)}, u32[]{:S(2)}) collective-permute-start(bf16[288,768]{1,0:T(8,128)(2,1)S(1)} %get-tuple-element.26), channel_id=1, source_target_pairs={{0,2},{2,4},{4,6},{6,0},{1,3},{3,5},{5,7},{7,1},{8,10},{10,12},{12... | collective-permute-start | bytes 1327112 | tf_op jit(solution)/shard_map/ppermute | solution.py:21
  172.8 16.9 %collective-permute-start.24 = (bf16[288,768]{1,0:T(8,128)(2,1)S(1)}, bf16[288,768]{1,0:T(8,128)(2,1)S(1)}, u32[]{:S(2)}, u32[]{:S(2)}) collective-permute-start(bf16[288,768]{1,0:T(8,128)(2,1)S(1)} %get-tuple-element.27), channel_id=1, source_target_pairs={{0,4},{2,6},{4,0},{6,2},{1,5},{3,7},{5,1},{7,3},{8,12},{10,14},{12... | collective-permute-start | bytes 1327112 | tf_op jit(solution)/shard_map/ppermute | solution.py:21
  (29 other events, 440.0 us)
where the time goes:
time: 193 us; the launch traced here: 192 us
  waiting for transfers between devices  86 us (45%)
  starting transfers between devices  49.4 us (26%)
  Pallas kernels  36.9 us (19%)
  other arithmetic  11.1 us (6%)
  local copies, waits for them, and re-layouts  8.03 us (4%)
    ppermute x18, waiting for transfers between devices, move(): return lax.ppermute(x, axis, [(i, (i + s) % n) for i in range(n)])  54.2 us
    ppermute x18, starting transfers between devices, move(): return lax.ppermute(x, axis, [(i, (i + s) % n) for i in range(n)])  38.5 us
    ppermute x8, waiting for transfers between devices, swap_bits(): lax.ppermute(x, axis, [(i, i ^ bits) for i in range(lax.axis_size(axis))])  30.2 us
    pallas_call x1, Pallas kernels, local(): pl.pallas_call(amp_kernel, in_specs=[SMEM, SMEM, vmem, vmem, vmem] + [ANY...  17.1 us
    pallas_call x2, Pallas kernels, gamma_parts(): pl.pallas_call(gamma_kernel, grid_spec=pltpu.PrefetchScalarGridSpec(num_s...  14.2 us
    ppermute x8, starting transfers between devices, swap_bits(): lax.ppermute(x, axis, [(i, i ^ bits) for i in range(lax.axis_size(axis))])  8.77 us
    pallas_call x1, Pallas kernels, local(): pl.pallas_call(turn_kernel, in_specs=[SMEM] + [ANY] * 8, out_specs=pl.Blo...  5.59 us
  transfers between devices with their start and end apart: 35, of which 20 were waited for; matrix products, arithmetic and copies ran while one was open for 7% of the time, Pallas kernels for 10%

commit v1 on v0

--- a/solution.py
+++ b/solution.py
@@ -57,8 +57,8 @@
 
 def amp_kernel(place_ref, scal_ref, left_ref, row_ref, col_ref, *refs):
     sets_a, sets_b = refs[0:4], refs[4:8]
-    ampt_ref, dens_ref, right_ref = refs[8:11]
-    held, k_ref, amp_ref, sem, out_sem = refs[11:]
+    right_ref, ampt_ref, keep_ref, give_ref = refs[8:12]
+    held, k_ref, amp_ref, dens_ref, sem, out_sem = refs[12:]
     rows, v = sets_a[0].shape[1:]
 
     def piece(source, slot, h, half):
@@ -77,8 +77,7 @@
     for h in range(2):
         for _ in range(16):
             piece(sets_a[0].at[0], 0, h, 0).wait()
-        copy_out = pltpu.make_async_copy(held.at[h], right_ref.at[h], out_sem.at[h])
-        copy_out.start()
+        pltpu.make_async_copy(held.at[h], right_ref.at[h], out_sem.at[h]).start()
         k_ref[...] = jnp.dot(left_ref[...], held[h], preferred_element_type=F32)
         for i in range(2):
             for j in range(2):
@@ -100,31 +99,34 @@
             dens_ref[...] = part
         else:
             dens_ref[...] += part
+    chunk = v // 8
+    for n in range(8):
+        start = pl.multiple_of(place_ref[8 + n] * chunk, 8)
+        out_ref = keep_ref if n < 4 else give_ref
+        out_ref[(n % 4) * chunk : (n % 4 + 1) * chunk, :] = dens_ref[pl.ds(start, chunk), :]
     for h in range(2):
         pltpu.make_async_copy(held.at[h], right_ref.at[h], out_sem.at[h]).wait()
 
 
-def gamma_kernel(slot_ref, scal_ref, mine_ref, other_ref, ampt_ref, keep_ref, give_ref):
-    for right_ref, out_ref in ((other_ref, give_ref), (mine_ref, keep_ref)):
-        total = scal_ref[8] * jnp.dot(right_ref[0], ampt_ref[0], preferred_element_type=F32)
-        out_ref[0] = total + scal_ref[9] * jnp.dot(
-            right_ref[1], ampt_ref[1], preferred_element_type=F32
-        )
+def gamma_kernel(slot_ref, scal_ref, right_ref, ampt_ref, keep_ref, give_ref, both_ref):
+    rows = keep_ref.shape[1]
+    both_ref[...] = scal_ref[8] * jnp.dot(
+        right_ref[0], ampt_ref[0], preferred_element_type=F32
+    ) + scal_ref[9] * jnp.dot(right_ref[1], ampt_ref[1], preferred_element_type=F32)
+    for out_ref, side in ((keep_ref, slot_ref[2]), (give_ref, 1 - slot_ref[2])):
+        out_ref[0] = both_ref[pl.ds(pl.multiple_of(side * rows, rows), rows), :]
+
+
+def place_kernel(place_ref, mine_ref, other_ref, out_ref):
+    chunk = out_ref.shape[0] // 8
+    for n in range(8):
+        ref = mine_ref if n < 4 else other_ref
+        start = pl.multiple_of(place_ref[8 + n] * chunk, 8)
+        out_ref[pl.ds(start, chunk), :] = ref[(n % 4) * chunk : (n % 4 + 1) * chunk, :]
 
 
 def swap_bits(x, axis, bits):
     return lax.ppermute(x, axis, [(i, i ^ bits) for i in range(lax.axis_size(axis))])
-
-
-def halves_of(x, second):
-    low, high = jnp.split(x, 2)
-    return jnp.where(second, high, low), jnp.where(second, low, high)
-
-
-def joined(mine, other, second):
-    return jnp.where(
-        second, jnp.concatenate([other, mine]), jnp.concatenate([mine, other])
-    )
 
 
 def local(integrals, occ_count, occ_energy, vir_energy, task_iblock, task_jblock):
@@ -136,16 +138,23 @@
 
     planed = lax.ppermute(shard, AXES, to_plane())
     shard, planed = lax.optimization_barrier((shard, planed))
-    around = [shard] + [move(shard, "y", s) for s in (1, 2, 3)]
+    around = [shard]
+    for s in (1, 2, 3):
+        around.append(move(shard, "y", s))
     across = [swap(p) for p in around]
     first_a = jnp.stack([planed[0]] + [move(planed[0], "x", s) for s in (1, 2, 3)])
     first_b = jnp.stack([planed[1]] + [move(planed[1], "z", s) for s in (1, 2, 3)])
     sets_a = [first_a] + [move(first_a, "z", s) for s in (1, 2, 3)]
-    sets_b = [first_b] + [move(first_b, "x", s) for s in (1, 2, 3)]
+    sets_b = [first_b]
+    for s in (1, 2, 3):
+        sets_b.append(move(first_b, "x", s))
 
     ys = (y - steps) % 4
     slots = jnp.concatenate([2 * ys + c, 2 * ys + 1 - c]).astype(jnp.int32)
-    place = jnp.concatenate([(z - steps) % 4, (x - steps - y) % 4]).astype(jnp.int32)
+    chunks = y ^ jnp.array([0, 1, 3, 2])
+    place = jnp.concatenate(
+        [(z - steps) % 4, (x - steps - y) % 4, 4 * c + chunks, 4 - 4 * c + chunks]
+    ).astype(jnp.int32)
     blocks = 4 * (2 * jnp.arange(2) + c) + y
     first, second = task_iblock[:, 0], task_jblock
     ours = ((first == my_row)[:, None] & (second[:, None] == blocks[None])).sum(0)
@@ -163,69 +172,73 @@
         ]
     )
 
+    vmem = pl.BlockSpec(memory_space=pltpu.VMEM)
     left = pl.pallas_call(
         turn_kernel,
         in_specs=[SMEM] + [ANY] * 8,
-        out_specs=pl.BlockSpec(memory_space=pltpu.VMEM),
-        out_shape=jax.ShapeDtypeStruct((2 * v, 8 * rows), BF16),
+        out_specs=vmem,
+        out_shape=pltpu.VMEM((2 * v, 8 * rows), BF16),
         scratch_shapes=[pltpu.VMEM((2, 8 * rows, v), BF16), pltpu.SemaphoreType.DMA((8,))],
+        compiler_params=pltpu.CompilerParams(vmem_limit_bytes=24 * 2**20),
         cost_estimate=pl.CostEstimate(flops=0, bytes_accessed=7_000_000, transcendentals=0),
         name="turn",
     )(slots, *around, *across)
 
-    vmem = pl.BlockSpec(memory_space=pltpu.VMEM)
-    ampt, dens, right = pl.pallas_call(
+    right, ampt, dens_keep, dens_give = pl.pallas_call(
         amp_kernel,
         in_specs=[SMEM, SMEM, vmem, vmem, vmem] + [ANY] * 8,
-        out_specs=[vmem, vmem, ANY],
+        out_specs=[ANY] + [vmem] * 3,
         out_shape=[
+            jax.ShapeDtypeStruct((2, 8 * rows, 2 * v), BF16),
             jax.ShapeDtypeStruct((2, 2 * v, 2 * v), BF16),
-            jax.ShapeDtypeStruct((v, v), F32),
-            jax.ShapeDtypeStruct((2, 8 * rows, 2 * v), BF16),
+            jax.ShapeDtypeStruct((v // 2, v), F32),
+            jax.ShapeDtypeStruct((v // 2, v), F32),
         ],
         scratch_shapes=[
             pltpu.VMEM((2, 8 * rows, 2 * v), BF16),
             pltpu.VMEM((2 * v, 2 * v), F32),
             pltpu.VMEM((2 * v, 2 * v), BF16),
+            pltpu.VMEM((v, v), F32),
             pltpu.SemaphoreType.DMA((2,)),
             pltpu.SemaphoreType.DMA((2,)),
         ],
+        compiler_params=pltpu.CompilerParams(vmem_limit_bytes=62_900_000),
         cost_estimate=pl.CostEstimate(
-            flops=6_200_000_000, bytes_accessed=20_000_000, transcendentals=0
+            flops=6_200_000_000, bytes_accessed=12_000_000, transcendentals=0
         ),
         name="amplitudes",
     )(place, scal, left, vir_energy.reshape(1, -1), vir_energy.reshape(-1, 1), *sets_a, *sets_b)
 
     def gamma_parts(ends):
-        at = 2 * ((y + jnp.array(ends)) % 4)
-        slot = jnp.stack([at + c, at + 1 - c]).astype(jnp.int32)
+        slot = jnp.stack([(y + s) % 4 for s in ends] + [c]).astype(jnp.int32)
         width = 2 * v
         return pl.pallas_call(
             gamma_kernel,
             grid_spec=pltpu.PrefetchScalarGridSpec(
                 num_scalar_prefetch=1,
-                grid=(len(ends),),
+                grid=(2,),
                 in_specs=[
                     SMEM,
-                    pl.BlockSpec((2, rows, width), lambda n, slot: (0, slot[0, n], 0)),
-                    pl.BlockSpec((2, rows, width), lambda n, slot: (0, slot[1, n], 0)),
+                    pl.BlockSpec((2, 2 * rows, width), lambda n, slot: (0, slot[n], 0)),
                     pl.BlockSpec((2, width, width), lambda n, slot: (0, 0, 0)),
                 ],
                 out_specs=[pl.BlockSpec((1, rows, width), lambda n, slot: (n, 0, 0))] * 2,
+                scratch_shapes=[pltpu.VMEM((2 * rows, width), F32)],
             ),
-            out_shape=[jax.ShapeDtypeStruct((len(ends), rows, width), F32)] * 2,
+            out_shape=[jax.ShapeDtypeStruct((2, rows, width), F32)] * 2,
+            compiler_params=pltpu.CompilerParams(vmem_limit_bytes=62_000_000),
             cost_estimate=pl.CostEstimate(
-                flops=1_360_000_000 * len(ends), bytes_accessed=10_000_000, transcendentals=0
+                flops=2_720_000_000, bytes_accessed=4_000_000, transcendentals=0
             ),
-        )(slot, scal, right, right, ampt)
-
-    low, high = halves_of(dens, c == 1)
-    dens_got = swap(high)
+        )(slot, scal, right, ampt)
+
+    got = swap(dens_give)
+    own = dens_keep + got
     keep, give = gamma_parts((2, 1))
-    got = swap(give)
+    got_far = swap(give)
     keep_near, give_near = gamma_parts((3, 0))
     got_near = swap(give_near)
-    to_far, to_next = (keep[0] + got[0]).astype(BF16), (keep[1] + got[1]).astype(BF16)
+    to_far, to_next = (keep[0] + got_far[0]).astype(BF16), (keep[1] + got_far[1]).astype(BF16)
     far = move(to_far, "y", 2)
     next_one = move(to_next, "y", 1)
     to_last = (keep_near[0] + got_near[0]).astype(BF16)
@@ -234,22 +247,27 @@
     gamma = gamma + next_one.astype(F32) + last_one.astype(F32) + far.astype(F32)
     gamma_out = gamma.reshape(rows, orbitals, v)
 
-    own = low + dens_got
-    upper, odd = y // 2 == 1, y % 2 == 1
-    for bits, second in ((3, upper), (1, odd)):
-        own, sent = halves_of(own, second)
+    for bits in (3, 1):
+        mine, sent = jnp.split(own, 2)
         got = swap_bits(sent, "y", bits)
-        own = own + got
+        own = mine + got
     for axis in ("x", "z"):
         for bits in (1, 3):
             got = swap_bits(own, axis, bits)
             own = own + got
     own = own / task_iblock.shape[0]
-    for bits, second in ((1, odd), (3, upper)):
+    for bits in (1, 3):
         got = swap_bits(own, "y", bits)
-        own = joined(own, got, second)
+        own = jnp.concatenate([own, got])
     got = swap(own)
-    density = joined(own, got, c == 1)
+    density = pl.pallas_call(
+        place_kernel,
+        in_specs=[SMEM, vmem, vmem],
+        out_specs=vmem,
+        out_shape=jax.ShapeDtypeStruct((v, v), F32),
+        compiler_params=pltpu.CompilerParams(vmem_limit_bytes=4 * 2**20),
+        name="place",
+    )(place, own, got)
     return gamma_out, density
 
 

time: 193 us -> 199 us (1.031)
  the two profiles are of different devices: /device:TPU:0 before, /device:TPU:6 now
where the time goes in v1:
time: 199 us; the launch traced here: 198 us
  waiting for transfers between devices  104 us (52%)
  starting transfers between devices  36.5 us (18%)
  Pallas kernels  36.5 us (18%)
  local copies, waits for them, and re-layouts  12.5 us (6%)
  other arithmetic  8.02 us (4%)
    ppermute x18, waiting for transfers between devices, move(): return lax.ppermute(x, axis, [(i, (i + s) % n) for i in range(n)])  55 us
    ppermute x8, waiting for transfers between devices, swap_bits(): lax.ppermute(x, axis, [(i, i ^ bits) for i in range(lax.axis_size(axis))])  39 us
    ppermute x18, starting transfers between devices, move(): return lax.ppermute(x, axis, [(i, (i + s) % n) for i in range(n)])  27.1 us
    pallas_call x1, Pallas kernels, local(): pl.pallas_call(amp_kernel, in_specs=[SMEM, SMEM, vmem, vmem, vmem] + [ANY...  17.2 us
    pallas_call x2, Pallas kernels, gamma_parts(): pl.pallas_call(gamma_kernel, grid_spec=pltpu.PrefetchScalarGridSpec(num_s...  15.2 us
    ppermute x1, waiting for transfers between devices, local(): planed = lax.ppermute(shard, AXES, to_plane())  8.38 us
    ppermute x1, starting transfers between devices, local(): planed = lax.ppermute(shard, AXES, to_plane())  4.92 us
  transfers between devices with their start and end apart: 35, of which 21 were waited for; matrix products, arithmetic and copies ran while one was open for 7% of the time, Pallas kernels for 6%

profile of v1, /device:TPU:6, one launch (start us, length us, event | category | flops | bytes accessed | tf_op | source)
XLA Modules:
  0.0 198.3 jit_solution(2111307297705717437)
XLA Ops:
  1.7 4.9 %collective-permute-start = (bf16[2,288,384]{2,1,0:T(8,128)(2,1)S(1)}, bf16[2,288,384]{2,1,0:T(8,128)(2,1)S(1)}, u32[]{:S(2)}, u32[]{:S(2)}) collective-permute-start(bf16[2,288,384]{2,1,0:T(8,128)(2,1)S(1)} %bitcast.41), channel_id=1, source_target_pairs={{0,0},{1,32},{2,8},{3,40},{4,16},{5,48},{6,24},{7,56},{8,10},{9,42... | collective-permute-start | bytes 1327112 | tf_op jit(solution)/shard_map/ppermute | solution.py:139
  10.8 8.4 %collective-permute-done = bf16[2,288,384]{2,1,0:T(8,128)(2,1)S(1)} collective-permute-done((bf16[2,288,384]{2,1,0:T(8,128)(2,1)S(1)}, bf16[2,288,384]{2,1,0:T(8,128)(2,1)S(1)}, u32[]{:S(2)}, u32[]{:S(2)}) %collective-permute-start) | collective-permute-done | bytes 442400 | tf_op jit(solution)/shard_map/ppermute | solution.py:139
  20.0 4.7 %collective-permute-start.16 = (bf16[288,384]{1,0:T(8,128)(2,1)S(1)}, bf16[288,384]{1,0:T(8,128)(2,1)S(1)}, u32[]{:S(2)}, u32[]{:S(2)}) collective-permute-start(bf16[288,384]{1,0:T(8,128)(2,1)S(1)} %get-tuple-element.28), channel_id=1, source_target_pairs={{0,96},{32,0},{64,32},{96,64},{1,97},{33,1},{65,33},{97,65},{2,98}... | collective-permute-start | bytes 663560 | tf_op jit(solution)/shard_map/ppermute | solution.py:21
  29.4 3.5 %collective-permute-done.16 = bf16[288,384]{1,0:T(8,128)(2,1)S(1)} collective-permute-done((bf16[288,384]{1,0:T(8,128)(2,1)S(1)}, bf16[288,384]{1,0:T(8,128)(2,1)S(1)}, u32[]{:S(2)}, u32[]{:S(2)}) %collective-permute-start.16) | collective-permute-done | bytes 221216 | tf_op jit(solution)/shard_map/ppermute | solution.py:21
  41.9 4.4 %collective-permute-done.8 = bf16[288,384]{1,0:T(8,128)(2,1)S(1)} collective-permute-done((bf16[288,384]{1,0:T(8,128)(2,1)S(1)}, bf16[288,384]{1,0:T(8,128)(2,1)S(1)}, u32[]{:S(2)}, u32[]{:S(2)}) %collective-permute-start.8) | collective-permute-done | bytes 221216 | tf_op jit(solution)/shard_map/ppermute | solution.py:21
  46.3 4.9 %collective-permute-done.3.refs_3_ = bf16[2,288,384]{2,1,0:T(8,128)(2,1)S(1)} collective-permute-done((bf16[2,288,384]{2,1,0:T(8,128)(2,1)S(1)}, bf16[2,288,384]{2,1,0:T(8,128)(2,1)S(1)}, u32[]{:S(2)}, u32[]{:S(2)}) %collective-permute-start.3) | collective-permute-done | bytes 442400 | tf_op jit(solution)/shard_map/ppermute | solution.py:21
  60.8 4.3 %collective-permute-start.13 = (bf16[4,288,384]{2,1,0:T(8,128)(2,1)}, bf16[4,288,384]{2,1,0:T(8,128)(2,1)}, u32[]{:S(2)}, u32[]{:S(2)}) collective-permute-start(bf16[4,288,384]{2,1,0:T(8,128)(2,1)} %pad_maximum_fusion.refs_0_), channel_id=1, source_target_pairs={{0,96},{32,0},{64,32},{96,64},{1,97},{33,1},{65,33},{97,65},{2,98}... | collective-permute-start | bytes 2654216 | tf_op jit(solution)/shard_map/ppermute | solution.py:21
  75.9 5.5 %collective-permute-done.18.refs_6_ = bf16[4,288,384]{2,1,0:T(8,128)(2,1)} collective-permute-done((bf16[4,288,384]{2,1,0:T(8,128)(2,1)}, bf16[4,288,384]{2,1,0:T(8,128)(2,1)}, u32[]{:S(2)}, u32[]{:S(2)}) %collective-permute-start.18) | collective-permute-done | bytes 884768 | tf_op jit(solution)/shard_map/ppermute | solution.py:21
  81.4 17.2 %collective-permute-done.17.refs_5_ = bf16[4,288,384]{2,1,0:T(8,128)(2,1)} collective-permute-done((bf16[4,288,384]{2,1,0:T(8,128)(2,1)}, bf16[4,288,384]{2,1,0:T(8,128)(2,1)}, u32[]{:S(2)}, u32[]{:S(2)}) %collective-permute-start.17) | collective-permute-done | bytes 884768 | tf_op jit(solution)/shard_map/ppermute | solution.py:21
  98.6 4.8 %collective-permute-done.13.refs_3_ = bf16[4,288,384]{2,1,0:T(8,128)(2,1)} collective-permute-done((bf16[4,288,384]{2,1,0:T(8,128)(2,1)}, bf16[4,288,384]{2,1,0:T(8,128)(2,1)}, u32[]{:S(2)}, u32[]{:S(2)}) %collective-permute-start.13) | collective-permute-done | bytes 884768 | tf_op jit(solution)/shard_map/ppermute | solution.py:21
  103.4 3.7 %collective-permute-done.11.refs_1_ = bf16[4,288,384]{2,1,0:T(8,128)(2,1)} collective-permute-done((bf16[4,288,384]{2,1,0:T(8,128)(2,1)}, bf16[4,288,384]{2,1,0:T(8,128)(2,1)}, u32[]{:S(2)}, u32[]{:S(2)}) %collective-permute-start.11) | collective-permute-done | bytes 884768 | tf_op jit(solution)/shard_map/ppermute | solution.py:21
  107.1 17.2 %amplitudes.1 = (bf16[2,2304,768]{2,1,0:T(8,128)(2,1)}, bf16[2,768,768]{2,1,0:T(8,128)(2,1)}, f32[192,384]{1,0:T(8,128)}, f32[192,384]{1,0:T(8,128)}) custom-call(s32[16]{0:T(128)} %pad_add_fusion.place_ref, f32[16]{0:T(128)} %concatenate.16.scal_ref, bf16[768,2304]{1,0:T(8,128)(2,1)} %copy-done, f32[1,384]{1,0:T(1,128)} %reshape.68.row_ref, ...), custom_call_target="tpu_custom_call" | custom-call | flops 6200000000 | bytes 12000000 | tf_op jit(solution)/shard_map/amplitudes/pallas_call | solution.py:187
  124.3 7.6 %shard_map.87 = (f32[2,288,768]{2,1,0:T(8,128)}, f32[2,288,768]{2,1,0:T(8,128)}) custom-call(s32[3]{0:T(128)} %get-tuple-element.39.slot_ref, f32[16]{0:T(128)} %concatenate.16.scal_ref, bf16[2,2304,768]{2,1,0:T(8,128)(2,1)} %get-tuple-element.14.right_ref, bf16[2,768,768]{2,1,0:T(8,128)(2,1)} %get-tuple-element.15.ampt_ref), custom_call_target="tpu_custom_call" | custom-call | flops 2720000000 | bytes 4000000 | tf_op jit(solution)/shard_map/pallas_call | solution.py:215
  132.4 7.5 %shard_map.86 = (f32[2,288,768]{2,1,0:T(8,128)}, f32[2,288,768]{2,1,0:T(8,128)}) custom-call(s32[3]{0:T(128)} %get-tuple-element.38.slot_ref, f32[16]{0:T(128)} %concatenate.16.scal_ref, bf16[2,2304,768]{2,1,0:T(8,128)(2,1)} %get-tuple-element.14.right_ref, bf16[2,768,768]{2,1,0:T(8,128)(2,1)} %get-tuple-element.15.ampt_ref), custom_call_target="tpu_custom_call" | custom-call | flops 2720000000 | bytes 4000000 | tf_op jit(solution)/shard_map/pallas_call | solution.py:215
  140.8 6.8 %collective-permute-done.26 = f32[96,384]{1,0:T(8,128)S(1)} collective-permute-done((f32[96,384]{1,0:T(8,128)S(1)}, f32[96,384]{1,0:T(8,128)S(1)}, u32[]{:S(2)}, u32[]{:S(2)}) %collective-permute-start.26) | collective-permute-done | bytes 147488 | tf_op jit(solution)/shard_map/ppermute | solution.py:129
  147.7 4.3 %collective-permute-done.27 = f32[48,384]{1,0:T(8,128)S(1)} collective-permute-done((f32[48,384]{1,0:T(8,128)S(1)}, f32[48,384]{1,0:T(8,128)S(1)}, u32[]{:S(2)}, u32[]{:S(2)}) %collective-permute-start.27) | collective-permute-done | bytes 73760 | tf_op jit(solution)/shard_map/ppermute | solution.py:129
  152.4 4.3 %collective-permute-done.28 = f32[48,384]{1,0:T(8,128)S(1)} collective-permute-done((f32[48,384]{1,0:T(8,128)S(1)}, f32[48,384]{1,0:T(8,128)S(1)}, u32[]{:S(2)}, u32[]{:S(2)}) %collective-permute-start.28) | collective-permute-done | bytes 73760 | tf_op jit(solution)/shard_map/ppermute | solution.py:129
  157.2 5.2 %collective-permute-done.29 = f32[48,384]{1,0:T(8,128)S(1)} collective-permute-done((f32[48,384]{1,0:T(8,128)S(1)}, f32[48,384]{1,0:T(8,128)S(1)}, u32[]{:S(2)}, u32[]{:S(2)}) %collective-permute-start.29) | collective-permute-done | bytes 73760 | tf_op jit(solution)/shard_map/ppermute | solution.py:129
  162.7 4.1 %collective-permute-done.30 = f32[48,384]{1,0:T(8,128)S(1)} collective-permute-done((f32[48,384]{1,0:T(8,128)S(1)}, f32[48,384]{1,0:T(8,128)S(1)}, u32[]{:S(2)}, u32[]{:S(2)}) %collective-permute-start.30) | collective-permute-done | bytes 73760 | tf_op jit(solution)/shard_map/ppermute | solution.py:129
  167.5 5.0 %collective-permute-done.31 = f32[48,384]{1,0:T(8,128)S(1)} collective-permute-done((f32[48,384]{1,0:T(8,128)S(1)}, f32[48,384]{1,0:T(8,128)S(1)}, u32[]{:S(2)}, u32[]{:S(2)}) %collective-permute-start.31) | collective-permute-done | bytes 73760 | tf_op jit(solution)/shard_map/ppermute | solution.py:129
  172.6 5.1 %collective-permute-done.32 = f32[48,384]{1,0:T(8,128)S(1)} collective-permute-done((f32[48,384]{1,0:T(8,128)S(1)}, f32[48,384]{1,0:T(8,128)S(1)}, u32[]{:S(2)}, u32[]{:S(2)}) %collective-permute-start.32) | collective-permute-done | bytes 73760 | tf_op jit(solution)/shard_map/ppermute | solution.py:129
  178.8 4.1 %collective-permute-start.24 = (bf16[288,768]{1,0:T(8,128)(2,1)S(1)}, bf16[288,768]{1,0:T(8,128)(2,1)S(1)}, u32[]{:S(2)}, u32[]{:S(2)}) collective-permute-start(bf16[288,768]{1,0:T(8,128)(2,1)S(1)} %get-tuple-element.25), channel_id=1, source_target_pairs={{0,4},{2,6},{4,0},{6,2},{1,5},{3,7},{5,1},{7,3},{8,12},{10,14},{12... | collective-permute-start | bytes 1327112 | tf_op jit(solution)/shard_map/ppermute | solution.py:21
  183.1 4.1 %collective-permute-done.33 = f32[96,384]{1,0:T(8,128)S(1)} collective-permute-done((f32[96,384]{1,0:T(8,128)S(1)}, f32[96,384]{1,0:T(8,128)S(1)}, u32[]{:S(2)}, u32[]{:S(2)}) %collective-permute-start.33) | collective-permute-done | bytes 147488 | tf_op jit(solution)/shard_map/ppermute | solution.py:129
  190.3 6.4 %collective-permute-done.22 = bf16[288,768]{1,0:T(8,128)(2,1)S(1)} collective-permute-done((bf16[288,768]{1,0:T(8,128)(2,1)S(1)}, bf16[288,768]{1,0:T(8,128)(2,1)S(1)}, u32[]{:S(2)}, u32[]{:S(2)}) %collective-permute-start.22) | collective-permute-done | bytes 442400 | tf_op jit(solution)/shard_map/ppermute | solution.py:21
  (119 shorter events, 49.4 us)
Async XLA Ops:
  1.7 17.5 %collective-permute-start = (bf16[2,288,384]{2,1,0:T(8,128)(2,1)S(1)}, bf16[2,288,384]{2,1,0:T(8,128)(2,1)S(1)}, u32[]{:S(2)}, u32[]{:S(2)}) collective-permute-start(bf16[2,288,384]{2,1,0:T(8,128)(2,1)S(1)} %bitcast.41), channel_id=1, source_target_pairs={{0,0},{1,32},{2,8},{3,40},{4,16},{5,48},{6,24},{7,56},{8,10},{9,42... | collective-permute-start | bytes 1327112 | tf_op jit(solution)/shard_map/ppermute | solution.py:139
  20.0 13.0 %collective-permute-start.16 = (bf16[288,384]{1,0:T(8,128)(2,1)S(1)}, bf16[288,384]{1,0:T(8,128)(2,1)S(1)}, u32[]{:S(2)}, u32[]{:S(2)}) collective-permute-start(bf16[288,384]{1,0:T(8,128)(2,1)S(1)} %get-tuple-element.28), channel_id=1, source_target_pairs={{0,96},{32,0},{64,32},{96,64},{1,97},{33,1},{65,33},{97,65},{2,98}... | collective-permute-start | bytes 663560 | tf_op jit(solution)/shard_map/ppermute | solution.py:21
  24.6 9.7 %collective-permute-start.15 = (bf16[288,384]{1,0:T(8,128)(2,1)S(1)}, bf16[288,384]{1,0:T(8,128)(2,1)S(1)}, u32[]{:S(2)}, u32[]{:S(2)}) collective-permute-start(bf16[288,384]{1,0:T(8,128)(2,1)S(1)} %get-tuple-element.28), channel_id=1, source_target_pairs={{0,64},{32,96},{64,0},{96,32},{1,65},{33,97},{65,1},{97,33},{2,66}... | collective-permute-start | bytes 663560 | tf_op jit(solution)/shard_map/ppermute | solution.py:21
  24.6 12.0 %collective-permute-start.14 = (bf16[288,384]{1,0:T(8,128)(2,1)S(1)}, bf16[288,384]{1,0:T(8,128)(2,1)S(1)}, u32[]{:S(2)}, u32[]{:S(2)}) collective-permute-start(bf16[288,384]{1,0:T(8,128)(2,1)S(1)} %get-tuple-element.28), channel_id=1, source_target_pairs={{0,32},{32,64},{64,96},{96,0},{1,33},{33,65},{65,97},{97,1},{2,34}... | collective-permute-start | bytes 663560 | tf_op jit(solution)/shard_map/ppermute | solution.py:21
  25.6 12.8 %collective-permute-start.10 = (bf16[288,384]{1,0:T(8,128)(2,1)S(1)}, bf16[288,384]{1,0:T(8,128)(2,1)S(1)}, u32[]{:S(2)}, u32[]{:S(2)}) collective-permute-start(bf16[288,384]{1,0:T(8,128)(2,1)S(1)} %get-tuple-element.27), channel_id=1, source_target_pairs={{0,24},{8,0},{16,8},{24,16},{1,25},{9,1},{17,9},{25,17},{2,26},{10... | collective-permute-start | bytes 663560 | tf_op jit(solution)/shard_map/ppermute | solution.py:21
  29.4 9.7 %collective-permute-start.9 = (bf16[288,384]{1,0:T(8,128)(2,1)S(1)}, bf16[288,384]{1,0:T(8,128)(2,1)S(1)}, u32[]{:S(2)}, u32[]{:S(2)}) collective-permute-start(bf16[288,384]{1,0:T(8,128)(2,1)S(1)} %get-tuple-element.27), channel_id=1, source_target_pairs={{0,16},{8,24},{16,0},{24,8},{1,17},{9,25},{17,1},{25,9},{2,18},{10... | collective-permute-start | bytes 663560 | tf_op jit(solution)/shard_map/ppermute | solution.py:21
  33.0 18.2 %collective-permute-start.3 = (bf16[2,288,384]{2,1,0:T(8,128)(2,1)S(1)}, bf16[2,288,384]{2,1,0:T(8,128)(2,1)S(1)}, u32[]{:S(2)}, u32[]{:S(2)}) collective-permute-start(bf16[2,288,384]{2,1,0:T(8,128)(2,1)S(1)} %bitcast.42), channel_id=1, source_target_pairs={{0,6},{2,0},{4,2},{6,4},{1,7},{3,1},{5,3},{7,5},{8,14},{10,8},{12,... | collective-permute-start | bytes 1327112 | tf_op jit(solution)/shard_map/ppermute | solution.py:21
  34.3 16.9 %collective-permute-start.2 = (bf16[2,288,384]{2,1,0:T(8,128)(2,1)S(1)}, bf16[2,288,384]{2,1,0:T(8,128)(2,1)S(1)}, u32[]{:S(2)}, u32[]{:S(2)}) collective-permute-start(bf16[2,288,384]{2,1,0:T(8,128)(2,1)S(1)} %bitcast.43), channel_id=1, source_target_pairs={{0,4},{2,6},{4,0},{6,2},{1,5},{3,7},{5,1},{7,3},{8,12},{10,14},{12... | collective-permute-start | bytes 1327112 | tf_op jit(solution)/shard_map/ppermute | solution.py:21
  36.7 18.2 %collective-permute-start.1 = (bf16[2,288,384]{2,1,0:T(8,128)(2,1)S(1)}, bf16[2,288,384]{2,1,0:T(8,128)(2,1)S(1)}, u32[]{:S(2)}, u32[]{:S(2)}) collective-permute-start(bf16[2,288,384]{2,1,0:T(8,128)(2,1)S(1)} %bitcast.44), channel_id=1, source_target_pairs={{0,2},{2,4},{4,6},{6,0},{1,3},{3,5},{5,7},{7,1},{8,10},{10,12},{12... | collective-permute-start | bytes 1327112 | tf_op jit(solution)/shard_map/ppermute | solution.py:21
  38.4 28.7 %collective-permute-start.19 = (bf16[4,288,384]{2,1,0:T(8,128)(2,1)}, bf16[4,288,384]{2,1,0:T(8,128)(2,1)S(1)}, u32[]{:S(2)}, u32[]{:S(2)}) collective-permute-start(bf16[4,288,384]{2,1,0:T(8,128)(2,1)} %pad_maximum_fusion.1.refs_4_), channel_id=1, source_target_pairs={{0,24},{8,0},{16,8},{24,16},{1,25},{9,1},{17,9},{25,17},{2,26},{10... | collective-permute-start | bytes 2654216 | tf_op jit(solution)/shard_map/ppermute | solution.py:21
  46.3 11.2 %collective-permute-start.4 = (bf16[2,288,384]{2,1,0:T(8,128)(2,1)S(1)}, bf16[2,288,384]{2,1,0:T(8,128)(2,1)S(1)}, u32[]{:S(2)}, u32[]{:S(2)}) collective-permute-start(bf16[2,288,384]{2,1,0:T(8,128)(2,1)S(1)} %bitcast.45), channel_id=1, source_target_pairs={{0,1},{1,0},{2,3},{3,2},{4,5},{5,4},{6,7},{7,6},{8,9},{9,8},{10,11... | collective-permute-start | bytes 1327112 | tf_op jit(solution)/shard_map/ppermute | solution.py:25
  51.2 9.6 %collective-permute-start.6 = (bf16[2,288,384]{2,1,0:T(8,128)(2,1)S(1)}, bf16[2,288,384]{2,1,0:T(8,128)(2,1)S(1)}, u32[]{:S(2)}, u32[]{:S(2)}) collective-permute-start(bf16[2,288,384]{2,1,0:T(8,128)(2,1)S(1)} %collective-permute-done.2.refs_2_), channel_id=1, source_target_pairs={{0,1},{1,0},{2,3},{3,2},{4,5},{5,4},{6,7},{7,6},{8,9},{9,8},{10,11... | collective-permute-start | bytes 1327112 | tf_op jit(solution)/shard_map/ppermute | solution.py:25
  54.9 10.2 %collective-permute-start.5 = (bf16[2,288,384]{2,1,0:T(8,128)(2,1)S(1)}, bf16[2,288,384]{2,1,0:T(8,128)(2,1)S(1)}, u32[]{:S(2)}, u32[]{:S(2)}) collective-permute-start(bf16[2,288,384]{2,1,0:T(8,128)(2,1)S(1)} %collective-permute-done.1.refs_1_), channel_id=1, source_target_pairs={{0,1},{1,0},{2,3},{3,2},{4,5},{5,4},{6,7},{7,6},{8,9},{9,8},{10,11... | collective-permute-start | bytes 1327112 | tf_op jit(solution)/shard_map/ppermute | solution.py:25
  57.5 23.9 %collective-permute-start.18 = (bf16[4,288,384]{2,1,0:T(8,128)(2,1)}, bf16[4,288,384]{2,1,0:T(8,128)(2,1)}, u32[]{:S(2)}, u32[]{:S(2)}) collective-permute-start(bf16[4,288,384]{2,1,0:T(8,128)(2,1)} %pad_maximum_fusion.1.refs_4_), channel_id=1, source_target_pairs={{0,16},{8,24},{16,0},{24,8},{1,17},{9,25},{17,1},{25,9},{2,18},{10... | collective-permute-start | bytes 2654216 | tf_op jit(solution)/shard_map/ppermute | solution.py:21
  57.8 40.7 %collective-permute-start.17 = (bf16[4,288,384]{2,1,0:T(8,128)(2,1)}, bf16[4,288,384]{2,1,0:T(8,128)(2,1)}, u32[]{:S(2)}, u32[]{:S(2)}) collective-permute-start(bf16[4,288,384]{2,1,0:T(8,128)(2,1)} %pad_maximum_fusion.1.refs_4_), channel_id=1, source_target_pairs={{0,8},{8,16},{16,24},{24,0},{1,9},{9,17},{17,25},{25,1},{2,10},{10... | collective-permute-start | bytes 2654216 | tf_op jit(solution)/shard_map/ppermute | solution.py:21
  60.8 42.6 %collective-permute-start.13 = (bf16[4,288,384]{2,1,0:T(8,128)(2,1)}, bf16[4,288,384]{2,1,0:T(8,128)(2,1)}, u32[]{:S(2)}, u32[]{:S(2)}) collective-permute-start(bf16[4,288,384]{2,1,0:T(8,128)(2,1)} %pad_maximum_fusion.refs_0_), channel_id=1, source_target_pairs={{0,96},{32,0},{64,32},{96,64},{1,97},{33,1},{65,33},{97,65},{2,98}... | collective-permute-start | bytes 2654216 | tf_op jit(solution)/shard_map/ppermute | solution.py:21
  65.1 38.3 %collective-permute-start.12 = (bf16[4,288,384]{2,1,0:T(8,128)(2,1)}, bf16[4,288,384]{2,1,0:T(8,128)(2,1)}, u32[]{:S(2)}, u32[]{:S(2)}) collective-permute-start(bf16[4,288,384]{2,1,0:T(8,128)(2,1)} %pad_maximum_fusion.refs_0_), channel_id=1, source_target_pairs={{0,64},{32,96},{64,0},{96,32},{1,65},{33,97},{65,1},{97,33},{2,66}... | collective-permute-start | bytes 2654216 | tf_op jit(solution)/shard_map/ppermute | solution.py:21
  67.1 40.0 %collective-permute-start.11 = (bf16[4,288,384]{2,1,0:T(8,128)(2,1)}, bf16[4,288,384]{2,1,0:T(8,128)(2,1)}, u32[]{:S(2)}, u32[]{:S(2)}) collective-permute-start(bf16[4,288,384]{2,1,0:T(8,128)(2,1)} %pad_maximum_fusion.refs_0_), channel_id=1, source_target_pairs={{0,32},{32,64},{64,96},{96,0},{1,33},{33,65},{65,97},{97,1},{2,34}... | collective-permute-start | bytes 2654216 | tf_op jit(solution)/shard_map/ppermute | solution.py:21
  131.9 46.5 %collective-permute-start.21 = (f32[2,288,768]{2,1,0:T(8,128)}, f32[2,288,768]{2,1,0:T(8,128)S(1)}, u32[]{:S(2)}, u32[]{:S(2)}) collective-permute-start(f32[2,288,768]{2,1,0:T(8,128)} %get-tuple-element.19), channel_id=1, source_target_pairs={{0,1},{1,0},{2,3},{3,2},{4,5},{5,4},{6,7},{7,6},{8,9},{9,8},{10,11... | collective-permute-start | bytes 5308424 | tf_op jit(solution)/shard_map/ppermute | solution.py:25
  140.0 42.9 %collective-permute-start.20 = (f32[2,288,768]{2,1,0:T(8,128)}, f32[2,288,768]{2,1,0:T(8,128)S(1)}, u32[]{:S(2)}, u32[]{:S(2)}) collective-permute-start(f32[2,288,768]{2,1,0:T(8,128)} %get-tuple-element.17), channel_id=1, source_target_pairs={{0,1},{1,0},{2,3},{3,2},{4,5},{5,4},{6,7},{7,6},{8,9},{9,8},{10,11... | collective-permute-start | bytes 5308424 | tf_op jit(solution)/shard_map/ppermute | solution.py:25
  177.8 9.4 %collective-permute-start.33 = (f32[96,384]{1,0:T(8,128)S(1)}, f32[96,384]{1,0:T(8,128)S(1)}, u32[]{:S(2)}, u32[]{:S(2)}) collective-permute-start(f32[96,384]{1,0:T(8,128)S(1)} %pad_maximum_fusion.3), channel_id=1, source_target_pairs={{0,6},{2,4},{4,2},{6,0},{1,7},{3,5},{5,3},{7,1},{8,14},{10,12},{12... | collective-permute-start | bytes 442376 | tf_op jit(solution)/shard_map/ppermute | solution.py:129
  178.7 18.0 %collective-permute-start.22 = (bf16[288,768]{1,0:T(8,128)(2,1)S(1)}, bf16[288,768]{1,0:T(8,128)(2,1)S(1)}, u32[]{:S(2)}, u32[]{:S(2)}) collective-permute-start(bf16[288,768]{1,0:T(8,128)(2,1)S(1)} %get-tuple-element.24), channel_id=1, source_target_pairs={{0,2},{2,4},{4,6},{6,0},{1,3},{3,5},{5,7},{7,1},{8,10},{10,12},{12... | collective-permute-start | bytes 1327112 | tf_op jit(solution)/shard_map/ppermute | solution.py:21
  178.8 17.9 %collective-permute-start.24 = (bf16[288,768]{1,0:T(8,128)(2,1)S(1)}, bf16[288,768]{1,0:T(8,128)(2,1)S(1)}, u32[]{:S(2)}, u32[]{:S(2)}) collective-permute-start(bf16[288,768]{1,0:T(8,128)(2,1)S(1)} %get-tuple-element.25), channel_id=1, source_target_pairs={{0,4},{2,6},{4,0},{6,2},{1,5},{3,7},{5,1},{7,3},{8,12},{10,14},{12... | collective-permute-start | bytes 1327112 | tf_op jit(solution)/shard_map/ppermute | solution.py:21
  183.0 13.7 %collective-permute-start.23 = (bf16[288,768]{1,0:T(8,128)(2,1)S(1)}, bf16[288,768]{1,0:T(8,128)(2,1)S(1)}, u32[]{:S(2)}, u32[]{:S(2)}) collective-permute-start(bf16[288,768]{1,0:T(8,128)(2,1)S(1)} %fusion.8), channel_id=1, source_target_pairs={{0,6},{2,0},{4,2},{6,4},{1,7},{3,1},{5,3},{7,5},{8,14},{10,8},{12,... | collective-permute-start | bytes 1327112 | tf_op jit(solution)/shard_map/ppermute | solution.py:21
  (23 other events, 266.9 us)

commit v2 on v1

v2 whole, which is shorter than its diff:
```python
import jax
import jax.numpy as jnp
from jax import lax
from jax.experimental import pallas as pl
from jax.experimental.pallas import tpu as pltpu
from jax.sharding import Mesh
from jax.sharding import PartitionSpec as P


AXES = ("z", "x", "y", "c")
OROW = ("z", "x")
OCOL = ("y", "c")
BF16 = jnp.bfloat16
F32 = jnp.float32
ANY = pl.BlockSpec(memory_space=pl.ANY)
SMEM = pl.BlockSpec(memory_space=pltpu.SMEM)


def move(x, axis, s):
    n = lax.axis_size(axis)
    return lax.ppermute(x, axis, [(i, (i + s) % n) for i in range(n)])


def swap(x):
    return lax.ppermute(x, "c", [(0, 1), (1, 0)])


def to_plane(turn):
    pairs = []
    for z in range(4):
        for x in range(4):
            for y in range(4):
                for c in range(2):
                    source = ((z * 4 + x) * 4 + y) * 2 + c
                    target = (((2 * (z // 2) + c) * 4 + (x + turn * y) % 4) * 4 + x) * 2 + z % 2
                    pairs.append((source, target))
    return pairs


def turn_kernel(slot_ref, *refs):
    pieces, out_ref, held, sem = refs[:8], refs[8], refs[9], refs[10]
    rows = pieces[0].shape[1]
    copies = [
        pltpu.make_async_copy(
            piece, held.at[:, pl.ds(pl.multiple_of(slot_ref[n] * rows, rows), rows), :], sem.at[n]
        )
        for n, piece in enumerate(pieces)
    ]
    for copy in copies:
        copy.start()
    for copy in copies:
        copy.wait()
    v = held.shape[2]
    for i in range(2):
        out_ref[i * v : (i + 1) * v, :] = held[i].T


def pair_kernel(place_ref, scal_ref, left_ref, row_ref, col_ref, *refs):
    sets_a, sets_b = refs[0:4], refs[4:8]
    parts = (refs[8:10], refs[10:12])
    dens_keep, dens_give = refs[12:14]
    held, own_ref, k_ref, amp_ref, ampt_ref, dens_ref, both_ref, sem, out_sem = refs[14:]
    rows, v = sets_a[0].shape[1:]

    def piece(source, slot, h, half):
        at = pl.ds(pl.multiple_of(slot * rows, rows), rows)
        return pltpu.make_async_copy(
            source, held.at[h, at, half * v : (half + 1) * v], sem.at[h]
        )

    fetch = pltpu.make_async_copy(left_ref, own_ref, sem.at[2])
    fetch.start()
    for s in range(4):
        for t in range(4):
            for source, zs, ys, half in (
                (sets_a[s], s, 4 + t, 0),
                (sets_b[s], t, 8 + s, 1),
            ):
                zz = place_ref[zs]
                piece(source.at[t], 2 * place_ref[ys] + lax.rem(zz, 2), zz // 2, half).start()
    fetch.wait()
    for h in range(2):
        for _ in range(16):
            piece(sets_a[0].at[0], 0, h, 0).wait()
        k_ref[...] = jnp.dot(own_ref[...], held[h], preferred_element_type=F32)
        for i in range(2):
            for j in range(2):
                a, b = slice(i * v, (i + 1) * v), slice(j * v, (j + 1) * v)
                k = k_ref[a, b]
                kt = k.T
                pair = scal_ref[i] + scal_ref[2 + 2 * h + j]
                both = scal_ref[10 + i] * scal_ref[12 + 2 * h + j]
                delta = (pair - col_ref[...]) - row_ref[...]
                amp_ref[a, b] = (both * ((2.0 * k - kt) / delta)).astype(BF16)
                ampt_ref[h, b, a] = (both * ((2.0 * kt - k) / delta)).astype(BF16)
        part = None
        for i in range(2):
            a = slice(i * v, (i + 1) * v)
            prod = jnp.dot(amp_ref[a, :], ampt_ref[h, :, a], preferred_element_type=F32)
            part = prod if part is None else part + prod
        part = scal_ref[6 + h] * part
        if h == 0:
            dens_ref[...] = part
        else:
            dens_ref[...] += part

    def leave(n, side):
        core = place_ref[24] if side == 0 else 1 - place_ref[24]
        return pltpu.make_async_copy(
            both_ref.at[n % 2, pl.ds(pl.multiple_of(core * rows, rows), rows), :],
            parts[n // 2][side].at[n % 2],
            out_sem.at[n % 2, side],
        )

    for n in range(4):
        if n >= 2:
            leave(n - 2, 0).wait()
            leave(n - 2, 1).wait()
        at = pl.ds(pl.multiple_of(place_ref[20 + n] * rows, rows), 2 * rows)
        both_ref[n % 2] = scal_ref[8] * jnp.dot(
            held[0, at, :], ampt_ref[0], preferred_element_type=F32
        ) + scal_ref[9] * jnp.dot(held[1, at, :], ampt_ref[1], preferred_element_type=F32)
        leave(n, 1).start()
        leave(n, 0).start()
    chunk = v // 8
    for n in range(8):
        start = pl.multiple_of(place_ref[12 + n] * chunk, 8)
        out_ref = dens_keep if n < 4 else dens_give
        out_ref[(n % 4) * chunk : (n % 4 + 1) * chunk, :] = dens_ref[pl.ds(start, chunk), :]
    for n in (2, 3):
        leave(n, 1).wait()
        leave(n, 0).wait()


def place_kernel(place_ref, mine_ref, other_ref, out_ref):
    chunk = out_ref.shape[0] // 8
    for n in range(8):
        ref = mine_ref if n < 4 else other_ref
        start = pl.multiple_of(place_ref[12 + n] * chunk, 8)
        out_ref[pl.ds(start, chunk), :] = ref[(n % 4) * chunk : (n % 4 + 1) * chunk, :]


def swap_bits(x, axis, bits):
    return lax.ppermute(x, axis, [(i, i ^ bits) for i in range(lax.axis_size(axis))])


def local(integrals, occ_count, occ_energy, vir_energy, task_iblock, task_jblock):
    rows, orbitals, v = integrals.shape
    z, x, y, c = (lax.axis_index(a) for a in AXES)
    my_row = z * 4 + x
    steps = jnp.arange(4)
    shard = jnp.swapaxes(integrals, 0, 1)

    plane_a = lax.ppermute(shard[0], AXES, to_plane(1))
    plane_b = lax.ppermute(shard[1], AXES, to_plane(-1))
    around = [shard]
    for s in (1, 2, 3):
        around.append(move(shard, "y", s))
    across = [swap(p) for p in around]
    sets = []
    for half, near, far in ((plane_a, "x", "z"), (plane_b, "z", "x")):
        first = [half]
        for s in (1, 2, 3):
            first.append(move(half, near, s))
        first = jnp.stack(first)
        sets.append([first])
        for s in (1, 2, 3):
            sets[-1].append(move(first, far, s))
    sets_a, sets_b = sets

    ys = (y - steps) % 4
    slots = jnp.concatenate([2 * ys + c, 2 * ys + 1 - c]).astype(jnp.int32)
    chunks = y ^ jnp.array([0, 1, 3, 2])
    place = jnp.concatenate(
        [
            (z - steps) % 4,
            (x - steps - y) % 4,
            (y - x + steps) % 4,
            4 * c + chunks,
            4 - 4 * c + chunks,
            2 * ((y + jnp.array([2, 1, 3, 0])) % 4),
            c[None],
        ]
    ).astype(jnp.int32)
    blocks = 4 * (2 * jnp.arange(2) + c) + y
    first, second = task_iblock[:, 0], task_jblock
    ours = ((first == my_row)[:, None] & (second[:, None] == blocks[None])).sum(0)
    theirs = ((second == my_row)[:, None] & (first[:, None] == blocks[None])).sum(0)
    energy = occ_energy.reshape(-1, orbitals)
    used = jnp.arange(orbitals)[None, :] < occ_count[:, None]
    scal = jnp.concatenate(
        [
            energy[my_row],
            energy[blocks].reshape(-1),
            ours.astype(F32),
            (ours + theirs).astype(F32),
            used[my_row].astype(F32),
            used[blocks].reshape(-1).astype(F32),
        ]
    )

    vmem = pl.BlockSpec(memory_space=pltpu.VMEM)
    left = pl.pallas_call(
        turn_kernel,
        in_specs=[SMEM] + [ANY] * 8,
        out_specs=vmem,
        out_shape=jax.ShapeDtypeStruct((2 * v, 8 * rows), BF16),
        scratch_shapes=[pltpu.VMEM((2, 8 * rows, v), BF16), pltpu.SemaphoreType.DMA((8,))],
        compiler_params=pltpu.CompilerParams(vmem_limit_bytes=24 * 2**20),
        cost_estimate=pl.CostEstimate(flops=0, bytes_accessed=7_000_000, transcendentals=0),
        name="turn",
    )(slots, *around, *across)

    part = jax.ShapeDtypeStruct((2, rows, 2 * v), F32)
    half = jax.ShapeDtypeStruct((v // 2, v), F32)
    keep, give, keep_near, give_near, dens_keep, dens_give = pl.pallas_call(
        pair_kernel,
        in_specs=[SMEM, SMEM, ANY, vmem, vmem] + [ANY] * 8,
        out_specs=[ANY] * 4 + [vmem] * 2,
        out_shape=[part] * 4 + [half] * 2,
        scratch_shapes=[
            pltpu.VMEM((2, 8 * rows, 2 * v), BF16),
            pltpu.VMEM((2 * v, 8 * rows), BF16),
            pltpu.VMEM((2 * v, 2 * v), F32),
            pltpu.VMEM((2 * v, 2 * v), BF16),
            pltpu.VMEM((2, 2 * v, 2 * v), BF16),
            pltpu.VMEM((v, v), F32),
            pltpu.VMEM((2, 2 * rows, 2 * v), F32),
            pltpu.SemaphoreType.DMA((3,)),
            pltpu.SemaphoreType.DMA((2, 2)),
        ],
        compiler_params=pltpu.CompilerParams(vmem_limit_bytes=62_000_000),
        cost_estimate=pl.CostEstimate(
            flops=11_800_000_000, bytes_accessed=18_000_000, transcendentals=0
        ),
        name="pairs",
    )(place, scal, left, vir_energy.reshape(1, -1), vir_energy.reshape(-1, 1), *sets_a, *sets_b)

    got = swap(dens_give)
    own = dens_keep + got
    got_far = swap(give)
    got_near = swap(give_near)
    to_far, to_next = (keep[0] + got_far[0]).astype(BF16), (keep[1] + got_far[1]).astype(BF16)
    far = move(to_far, "y", 2)
    next_one = move(to_next, "y", 1)
    to_last = (keep_near[0] + got_near[0]).astype(BF16)
    last_one = move(to_last, "y", 3)
    gamma = keep_near[1] + got_near[1]
    gamma = gamma + next_one.astype(F32) + last_one.astype(F32) + far.astype(F32)
    gamma_out = gamma.reshape(rows, orbitals, v)

    for bits in (3, 1):
        mine, sent = jnp.split(own, 2)
        got = swap_bits(sent, "y", bits)
        own = mine + got
    for axis in ("x", "z"):
        for bits in (1, 3):
            got = swap_bits(own, axis, bits)
            own = own + got
    own = own / task_iblock.shape[0]
    for bits in (1, 3):
        got = swap_bits(own, "y", bits)
        own = jnp.concatenate([own, got])
    got = swap(own)
    density = pl.pallas_call(
        place_kernel,
        in_specs=[SMEM, vmem, vmem],
        out_specs=vmem,
        out_shape=jax.ShapeDtypeStruct((v, v), F32),
        compiler_params=pltpu.CompilerParams(vmem_limit_bytes=4 * 2**20),
        name="place",
    )(place, own, got)
    return gamma_out, density


def solution(mesh):
    finer = Mesh(mesh.devices.reshape(4, 4, 4, 2), AXES)
    placed = (P(OCOL, OROW, None), P(), P(), P(), P(), P())
    return jax.shard_map(
        local, mesh=finer, in_specs=placed, out_specs=(P(OCOL, OROW, None), P()), check_vma=False
    )
```

time: 199 us -> 199 us (level)
  the two profiles are of different devices: /device:TPU:6 before, /device:TPU:0 now
where the time goes in v2:
time: 199 us; the launch traced here: 198 us
  waiting for transfers between devices  93.6 us (47%)
  starting transfers between devices  57.1 us (29%)
  Pallas kernels  27.6 us (14%)
  local copies, waits for them, and re-layouts  11.3 us (6%)
  other arithmetic  7.62 us (4%)
    ppermute x18, waiting for transfers between devices, move(): return lax.ppermute(x, axis, [(i, (i + s) % n) for i in range(n)])  50.4 us
    ppermute x18, starting transfers between devices, move(): return lax.ppermute(x, axis, [(i, (i + s) % n) for i in range(n)])  49.2 us
    ppermute x8, waiting for transfers between devices, swap_bits(): lax.ppermute(x, axis, [(i, i ^ bits) for i in range(lax.axis_size(axis))])  38 us
    pallas_call x1, Pallas kernels, local(): pl.pallas_call(pair_kernel, in_specs=[SMEM, SMEM, ANY, vmem, vmem] + [ANY...  23.3 us
    ppermute x8, waiting for transfers between devices, swap(): return lax.ppermute(x, 'c', [(0, 1), (1, 0)])  5.3 us
    ppermute x8, starting transfers between devices, swap_bits(): lax.ppermute(x, axis, [(i, i ^ bits) for i in range(lax.axis_size(axis))])  4.59 us
  transfers between devices with their start and end apart: 36, of which 20 were waited for; matrix products, arithmetic and copies ran while one was open for 7% of the time, Pallas kernels for 2%

profile of v2, /device:TPU:0, one launch (start us, length us, event | category | flops | bytes accessed | tf_op | source)
XLA Modules:
  0.0 198.3 jit_solution(2120234475054242354)
XLA Ops:
  1.8 3.2 %collective-permute-start.2 = (bf16[2,288,384]{2,1,0:T(8,128)(2,1)S(1)}, bf16[2,288,384]{2,1,0:T(8,128)(2,1)S(1)}, u32[]{:S(2)}, u32[]{:S(2)}) collective-permute-start(bf16[2,288,384]{2,1,0:T(8,128)(2,1)S(1)} %bitcast.39), channel_id=1, source_target_pairs={{0,6},{2,0},{4,2},{6,4},{1,7},{3,1},{5,3},{7,5},{8,14},{10,8},{12,... | collective-permute-start | bytes 1327112 | tf_op jit(solution)/shard_map/ppermute | solution.py:21
  7.9 18.8 %collective-permute-start.10 = (bf16[288,384]{1,0:T(8,128)(2,1)S(1)}, bf16[288,384]{1,0:T(8,128)(2,1)S(1)}, u32[]{:S(2)}, u32[]{:S(2)}) collective-permute-start(bf16[288,384]{1,0:T(8,128)(2,1)S(1)} %collective-permute-done.7), channel_id=1, source_target_pairs={{0,24},{8,0},{16,8},{24,16},{1,25},{9,1},{17,9},{25,17},{2,26},{10... | collective-permute-start | bytes 663560 | tf_op jit(solution)/shard_map/ppermute | solution.py:21
  27.6 4.7 %collective-permute-start.17 = (bf16[288,384]{1,0:T(8,128)(2,1)S(1)}, bf16[288,384]{1,0:T(8,128)(2,1)S(1)}, u32[]{:S(2)}, u32[]{:S(2)}) collective-permute-start(bf16[288,384]{1,0:T(8,128)(2,1)S(1)} %collective-permute-done.14), channel_id=1, source_target_pairs={{0,96},{32,0},{64,32},{96,64},{1,97},{33,1},{65,33},{97,65},{2,98}... | collective-permute-start | bytes 663560 | tf_op jit(solution)/shard_map/ppermute | solution.py:21
  36.5 5.1 %collective-permute-start = (bf16[2,288,384]{2,1,0:T(8,128)(2,1)S(1)}, bf16[2,288,384]{2,1,0:T(8,128)(2,1)S(1)}, u32[]{:S(2)}, u32[]{:S(2)}) collective-permute-start(bf16[2,288,384]{2,1,0:T(8,128)(2,1)S(1)} %bitcast.42), channel_id=1, source_target_pairs={{0,2},{2,4},{4,6},{6,0},{1,3},{3,5},{5,7},{7,1},{8,10},{10,12},{12... | collective-permute-start | bytes 1327112 | tf_op jit(solution)/shard_map/ppermute | solution.py:21
  41.6 4.0 %collective-permute-start.16 = (bf16[288,384]{1,0:T(8,128)(2,1)S(1)}, bf16[288,384]{1,0:T(8,128)(2,1)S(1)}, u32[]{:S(2)}, u32[]{:S(2)}) collective-permute-start(bf16[288,384]{1,0:T(8,128)(2,1)S(1)} %collective-permute-done.14), channel_id=1, source_target_pairs={{0,64},{32,96},{64,0},{96,32},{1,65},{33,97},{65,1},{97,33},{2,66}... | collective-permute-start | bytes 663560 | tf_op jit(solution)/shard_map/ppermute | solution.py:21
  46.6 4.0 %collective-permute-done.16 = bf16[288,384]{1,0:T(8,128)(2,1)S(1)} collective-permute-done((bf16[288,384]{1,0:T(8,128)(2,1)S(1)}, bf16[288,384]{1,0:T(8,128)(2,1)S(1)}, u32[]{:S(2)}, u32[]{:S(2)}) %collective-permute-start.16) | collective-permute-done | bytes 221216 | tf_op jit(solution)/shard_map/ppermute | solution.py:21
  50.8 7.2 %collective-permute-done.15 = bf16[288,384]{1,0:T(8,128)(2,1)S(1)} collective-permute-done((bf16[288,384]{1,0:T(8,128)(2,1)S(1)}, bf16[288,384]{1,0:T(8,128)(2,1)S(1)}, u32[]{:S(2)}, u32[]{:S(2)}) %collective-permute-start.15) | collective-permute-done | bytes 221216 | tf_op jit(solution)/shard_map/ppermute | solution.py:21
  65.5 3.7 %collective-permute-start.20 = (bf16[4,288,384]{2,1,0:T(8,128)(2,1)}, bf16[4,288,384]{2,1,0:T(8,128)(2,1)}, u32[]{:S(2)}, u32[]{:S(2)}) collective-permute-start(bf16[4,288,384]{2,1,0:T(8,128)(2,1)} %pad_maximum_fusion.1.refs_4_), channel_id=1, source_target_pairs={{0,24},{8,0},{16,8},{24,16},{1,25},{9,1},{17,9},{25,17},{2,26},{10... | collective-permute-start | bytes 2654216 | tf_op jit(solution)/shard_map/ppermute | solution.py:21
  75.2 2.9 %turn.1.left_ref = bf16[768,2304]{1,0:T(8,128)(2,1)S(1)} custom-call(s32[8]{0:T(128)S(1)} %pad_add_fusion.slot_ref, bf16[2,288,384]{2,1,0:T(8,128)(2,1)S(1)} %bitcast.44, bf16[2,288,384]{2,1,0:T(8,128)(2,1)S(1)} %collective-permute-done.refs_1_, bf16[2,288,384]{2,1,0:T(8,128)(2,1)S(1)} %collective-permute-done.1.refs_2_, ...), custom_call_target="tpu_custom_call" | custom-call | bytes 7000000 | tf_op jit(solution)/shard_map/turn/pallas_call | solution.py:203
  79.9 6.2 %collective-permute-done.12.refs_2_ = bf16[4,288,384]{2,1,0:T(8,128)(2,1)} collective-permute-done((bf16[4,288,384]{2,1,0:T(8,128)(2,1)}, bf16[4,288,384]{2,1,0:T(8,128)(2,1)}, u32[]{:S(2)}, u32[]{:S(2)}) %collective-permute-start.12) | collective-permute-done | bytes 884768 | tf_op jit(solution)/shard_map/ppermute | solution.py:21
  86.0 18.0 %collective-permute-done.11.refs_1_ = bf16[4,288,384]{2,1,0:T(8,128)(2,1)} collective-permute-done((bf16[4,288,384]{2,1,0:T(8,128)(2,1)}, bf16[4,288,384]{2,1,0:T(8,128)(2,1)}, u32[]{:S(2)}, u32[]{:S(2)}) %collective-permute-start.11) | collective-permute-done | bytes 884768 | tf_op jit(solution)/shard_map/ppermute | solution.py:21
  104.1 3.4 %collective-permute-done.20.refs_7_ = bf16[4,288,384]{2,1,0:T(8,128)(2,1)} collective-permute-done((bf16[4,288,384]{2,1,0:T(8,128)(2,1)}, bf16[4,288,384]{2,1,0:T(8,128)(2,1)}, u32[]{:S(2)}, u32[]{:S(2)}) %collective-permute-start.20) | collective-permute-done | bytes 884768 | tf_op jit(solution)/shard_map/ppermute | solution.py:21
  107.5 3.5 %collective-permute-done.18.refs_5_ = bf16[4,288,384]{2,1,0:T(8,128)(2,1)} collective-permute-done((bf16[4,288,384]{2,1,0:T(8,128)(2,1)}, bf16[4,288,384]{2,1,0:T(8,128)(2,1)}, u32[]{:S(2)}, u32[]{:S(2)}) %collective-permute-start.18) | collective-permute-done | bytes 884768 | tf_op jit(solution)/shard_map/ppermute | solution.py:21
  111.0 23.3 %pairs.1 = (f32[2,288,768]{2,1,0:T(8,128)}, f32[2,288,768]{2,1,0:T(8,128)}, f32[2,288,768]{2,1,0:T(8,128)}, f32[2,288,768]{2,1,0:T(8,128)}, f32[192,384]{1,0:T(8,128)}, /*index=5*/f32[192,384]{1,0:T(8,128)}) custom-call(s32[25]{0:T(128)} %concatenate.16.place_ref, f32[16]{0:T(128)} %concatenate.17.scal_ref, bf16[768,2304]{1,0:T(8,128)(2,1)} %copy-done, ...), custom_call_target="tpu_custom_call" | custom-call | flops 11800000512 | bytes 18000000 | tf_op jit(solution)/shard_map/pairs/pallas_call | solution.py:216
  135.2 3.7 %collective-permute-done.26 = f32[192,384]{1,0:T(8,128)S(1)} collective-permute-done((f32[192,384]{1,0:T(8,128)}, f32[192,384]{1,0:T(8,128)S(1)}, u32[]{:S(2)}, u32[]{:S(2)}) %collective-permute-start.26) | collective-permute-done | bytes 294944 | tf_op jit(solution)/shard_map/ppermute | solution.py:25
  140.9 6.3 %collective-permute-done.27 = f32[96,384]{1,0:T(8,128)S(1)} collective-permute-done((f32[96,384]{1,0:T(8,128)S(1)}, f32[96,384]{1,0:T(8,128)S(1)}, u32[]{:S(2)}, u32[]{:S(2)}) %collective-permute-start.27) | collective-permute-done | bytes 147488 | tf_op jit(solution)/shard_map/ppermute | solution.py:144
  147.3 4.3 %collective-permute-done.28 = f32[48,384]{1,0:T(8,128)S(1)} collective-permute-done((f32[48,384]{1,0:T(8,128)S(1)}, f32[48,384]{1,0:T(8,128)S(1)}, u32[]{:S(2)}, u32[]{:S(2)}) %collective-permute-start.28) | collective-permute-done | bytes 73760 | tf_op jit(solution)/shard_map/ppermute | solution.py:144
  151.7 4.3 %collective-permute-done.29 = f32[48,384]{1,0:T(8,128)S(1)} collective-permute-done((f32[48,384]{1,0:T(8,128)S(1)}, f32[48,384]{1,0:T(8,128)S(1)}, u32[]{:S(2)}, u32[]{:S(2)}) %collective-permute-start.29) | collective-permute-done | bytes 73760 | tf_op jit(solution)/shard_map/ppermute | solution.py:144
  157.0 4.7 %collective-permute-done.30 = f32[48,384]{1,0:T(8,128)S(1)} collective-permute-done((f32[48,384]{1,0:T(8,128)S(1)}, f32[48,384]{1,0:T(8,128)S(1)}, u32[]{:S(2)}, u32[]{:S(2)}) %collective-permute-start.30) | collective-permute-done | bytes 73760 | tf_op jit(solution)/shard_map/ppermute | solution.py:144
  161.9 4.3 %collective-permute-done.31 = f32[48,384]{1,0:T(8,128)S(1)} collective-permute-done((f32[48,384]{1,0:T(8,128)S(1)}, f32[48,384]{1,0:T(8,128)S(1)}, u32[]{:S(2)}, u32[]{:S(2)}) %collective-permute-start.31) | collective-permute-done | bytes 73760 | tf_op jit(solution)/shard_map/ppermute | solution.py:144
  167.7 4.2 %collective-permute-done.32 = f32[48,384]{1,0:T(8,128)S(1)} collective-permute-done((f32[48,384]{1,0:T(8,128)S(1)}, f32[48,384]{1,0:T(8,128)S(1)}, u32[]{:S(2)}, u32[]{:S(2)}) %collective-permute-start.32) | collective-permute-done | bytes 73760 | tf_op jit(solution)/shard_map/ppermute | solution.py:144
  172.0 5.1 %collective-permute-done.33 = f32[48,384]{1,0:T(8,128)S(1)} collective-permute-done((f32[48,384]{1,0:T(8,128)S(1)}, f32[48,384]{1,0:T(8,128)S(1)}, u32[]{:S(2)}, u32[]{:S(2)}) %collective-permute-start.33) | collective-permute-done | bytes 73760 | tf_op jit(solution)/shard_map/ppermute | solution.py:144
  182.4 4.7 %collective-permute-done.34 = f32[96,384]{1,0:T(8,128)S(1)} collective-permute-done((f32[96,384]{1,0:T(8,128)S(1)}, f32[96,384]{1,0:T(8,128)S(1)}, u32[]{:S(2)}, u32[]{:S(2)}) %collective-permute-start.34) | collective-permute-done | bytes 147488 | tf_op jit(solution)/shard_map/ppermute | solution.py:144
  192.9 3.7 %collective-permute-done.23 = bf16[288,768]{1,0:T(8,128)(2,1)S(1)} collective-permute-done((bf16[288,768]{1,0:T(8,128)(2,1)S(1)}, bf16[288,768]{1,0:T(8,128)(2,1)S(1)}, u32[]{:S(2)}, u32[]{:S(2)}) %collective-permute-start.23) | collective-permute-done | bytes 442400 | tf_op jit(solution)/shard_map/ppermute | solution.py:21
  (119 shorter events, 43.9 us)
Async XLA Ops:
  1.8 56.3 %collective-permute-start.2 = (bf16[2,288,384]{2,1,0:T(8,128)(2,1)S(1)}, bf16[2,288,384]{2,1,0:T(8,128)(2,1)S(1)}, u32[]{:S(2)}, u32[]{:S(2)}) collective-permute-start(bf16[2,288,384]{2,1,0:T(8,128)(2,1)S(1)} %bitcast.39), channel_id=1, source_target_pairs={{0,6},{2,0},{4,2},{6,4},{1,7},{3,1},{5,3},{7,5},{8,14},{10,8},{12,... | collective-permute-start | bytes 1327112 | tf_op jit(solution)/shard_map/ppermute | solution.py:21
  5.0 22.5 %collective-permute-start.14 = (bf16[288,384]{1,0:T(8,128)(2,1)S(1)}, bf16[288,384]{1,0:T(8,128)(2,1)S(1)}, u32[]{:S(2)}, u32[]{:S(2)}) collective-permute-start(bf16[288,384]{1,0:T(8,128)(2,1)S(1)} %get-tuple-element.18), channel_id=1, source_target_pairs={{0,0},{1,32},{2,24},{3,56},{4,16},{5,48},{6,8},{7,40},{8,10},{9,42... | collective-permute-start | bytes 663560 | tf_op jit(solution)/shard_map/ppermute | solution.py:155
  7.9 27.3 %collective-permute-start.10 = (bf16[288,384]{1,0:T(8,128)(2,1)S(1)}, bf16[288,384]{1,0:T(8,128)(2,1)S(1)}, u32[]{:S(2)}, u32[]{:S(2)}) collective-permute-start(bf16[288,384]{1,0:T(8,128)(2,1)S(1)} %collective-permute-done.7), channel_id=1, source_target_pairs={{0,24},{8,0},{16,8},{24,16},{1,25},{9,1},{17,9},{25,17},{2,26},{10... | collective-permute-start | bytes 663560 | tf_op jit(solution)/shard_map/ppermute | solution.py:21
  26.6 9.8 %collective-permute-start.9 = (bf16[288,384]{1,0:T(8,128)(2,1)S(1)}, bf16[288,384]{1,0:T(8,128)(2,1)S(1)}, u32[]{:S(2)}, u32[]{:S(2)}) collective-permute-start(bf16[288,384]{1,0:T(8,128)(2,1)S(1)} %collective-permute-done.7), channel_id=1, source_target_pairs={{0,16},{8,24},{16,0},{24,8},{1,17},{9,25},{17,1},{25,9},{2,18},{10... | collective-permute-start | bytes 663560 | tf_op jit(solution)/shard_map/ppermute | solution.py:21
  26.6 14.9 %collective-permute-start.8 = (bf16[288,384]{1,0:T(8,128)(2,1)S(1)}, bf16[288,384]{1,0:T(8,128)(2,1)S(1)}, u32[]{:S(2)}, u32[]{:S(2)}) collective-permute-start(bf16[288,384]{1,0:T(8,128)(2,1)S(1)} %collective-permute-done.7), channel_id=1, source_target_pairs={{0,8},{8,16},{16,24},{24,0},{1,9},{9,17},{17,25},{25,1},{2,10},{10... | collective-permute-start | bytes 663560 | tf_op jit(solution)/shard_map/ppermute | solution.py:21
  27.6 19.0 %collective-permute-start.17 = (bf16[288,384]{1,0:T(8,128)(2,1)S(1)}, bf16[288,384]{1,0:T(8,128)(2,1)S(1)}, u32[]{:S(2)}, u32[]{:S(2)}) collective-permute-start(bf16[288,384]{1,0:T(8,128)(2,1)S(1)} %collective-permute-done.14), channel_id=1, source_target_pairs={{0,96},{32,0},{64,32},{96,64},{1,97},{33,1},{65,33},{97,65},{2,98}... | collective-permute-start | bytes 663560 | tf_op jit(solution)/shard_map/ppermute | solution.py:21
  35.2 23.3 %collective-permute-start.1 = (bf16[2,288,384]{2,1,0:T(8,128)(2,1)S(1)}, bf16[2,288,384]{2,1,0:T(8,128)(2,1)S(1)}, u32[]{:S(2)}, u32[]{:S(2)}) collective-permute-start(bf16[2,288,384]{2,1,0:T(8,128)(2,1)S(1)} %bitcast.41), channel_id=1, source_target_pairs={{0,4},{2,6},{4,0},{6,2},{1,5},{3,7},{5,1},{7,3},{8,12},{10,14},{12... | collective-permute-start | bytes 1327112 | tf_op jit(solution)/shard_map/ppermute | solution.py:21
  36.5 22.2 %collective-permute-start = (bf16[2,288,384]{2,1,0:T(8,128)(2,1)S(1)}, bf16[2,288,384]{2,1,0:T(8,128)(2,1)S(1)}, u32[]{:S(2)}, u32[]{:S(2)}) collective-permute-start(bf16[2,288,384]{2,1,0:T(8,128)(2,1)S(1)} %bitcast.42), channel_id=1, source_target_pairs={{0,2},{2,4},{4,6},{6,0},{1,3},{3,5},{5,7},{7,1},{8,10},{10,12},{12... | collective-permute-start | bytes 1327112 | tf_op jit(solution)/shard_map/ppermute | solution.py:21
  41.6 9.0 %collective-permute-start.16 = (bf16[288,384]{1,0:T(8,128)(2,1)S(1)}, bf16[288,384]{1,0:T(8,128)(2,1)S(1)}, u32[]{:S(2)}, u32[]{:S(2)}) collective-permute-start(bf16[288,384]{1,0:T(8,128)(2,1)S(1)} %collective-permute-done.14), channel_id=1, source_target_pairs={{0,64},{32,96},{64,0},{96,32},{1,65},{33,97},{65,1},{97,33},{2,66}... | collective-permute-start | bytes 663560 | tf_op jit(solution)/shard_map/ppermute | solution.py:21
  46.6 22.6 %collective-permute-start.13 = (bf16[4,288,384]{2,1,0:T(8,128)(2,1)}, bf16[4,288,384]{2,1,0:T(8,128)(2,1)S(1)}, u32[]{:S(2)}, u32[]{:S(2)}) collective-permute-start(bf16[4,288,384]{2,1,0:T(8,128)(2,1)} %pad_maximum_fusion.refs_0_), channel_id=1, source_target_pairs={{0,96},{32,0},{64,32},{96,64},{1,97},{33,1},{65,33},{97,65},{2,98}... | collective-permute-start | bytes 2654216 | tf_op jit(solution)/shard_map/ppermute | solution.py:21
  50.6 7.4 %collective-permute-start.15 = (bf16[288,384]{1,0:T(8,128)(2,1)S(1)}, bf16[288,384]{1,0:T(8,128)(2,1)S(1)}, u32[]{:S(2)}, u32[]{:S(2)}) collective-permute-start(bf16[288,384]{1,0:T(8,128)(2,1)S(1)} %collective-permute-done.14), channel_id=1, source_target_pairs={{0,32},{32,64},{64,96},{96,0},{1,33},{33,65},{65,97},{97,1},{2,34}... | collective-permute-start | bytes 663560 | tf_op jit(solution)/shard_map/ppermute | solution.py:21
  58.6 10.6 %collective-permute-start.4 = (bf16[2,288,384]{2,1,0:T(8,128)(2,1)S(1)}, bf16[2,288,384]{2,1,0:T(8,128)(2,1)S(1)}, u32[]{:S(2)}, u32[]{:S(2)}) collective-permute-start(bf16[2,288,384]{2,1,0:T(8,128)(2,1)S(1)} %collective-permute-done.refs_1_), channel_id=1, source_target_pairs={{0,1},{1,0},{2,3},{3,2},{4,5},{5,4},{6,7},{7,6},{8,9},{9,8},{10,11... | collective-permute-start | bytes 1327112 | tf_op jit(solution)/shard_map/ppermute | solution.py:25
  61.7 24.4 %collective-permute-start.12 = (bf16[4,288,384]{2,1,0:T(8,128)(2,1)}, bf16[4,288,384]{2,1,0:T(8,128)(2,1)}, u32[]{:S(2)}, u32[]{:S(2)}) collective-permute-start(bf16[4,288,384]{2,1,0:T(8,128)(2,1)} %pad_maximum_fusion.refs_0_), channel_id=1, source_target_pairs={{0,64},{32,96},{64,0},{96,32},{1,65},{33,97},{65,1},{97,33},{2,66}... | collective-permute-start | bytes 2654216 | tf_op jit(solution)/shard_map/ppermute | solution.py:21
  63.5 40.6 %collective-permute-start.11 = (bf16[4,288,384]{2,1,0:T(8,128)(2,1)}, bf16[4,288,384]{2,1,0:T(8,128)(2,1)}, u32[]{:S(2)}, u32[]{:S(2)}) collective-permute-start(bf16[4,288,384]{2,1,0:T(8,128)(2,1)} %pad_maximum_fusion.refs_0_), channel_id=1, source_target_pairs={{0,32},{32,64},{64,96},{96,0},{1,33},{33,65},{65,97},{97,1},{2,34}... | collective-permute-start | bytes 2654216 | tf_op jit(solution)/shard_map/ppermute | solution.py:21
  65.5 42.0 %collective-permute-start.20 = (bf16[4,288,384]{2,1,0:T(8,128)(2,1)}, bf16[4,288,384]{2,1,0:T(8,128)(2,1)}, u32[]{:S(2)}, u32[]{:S(2)}) collective-permute-start(bf16[4,288,384]{2,1,0:T(8,128)(2,1)} %pad_maximum_fusion.1.refs_4_), channel_id=1, source_target_pairs={{0,24},{8,0},{16,8},{24,16},{1,25},{9,1},{17,9},{25,17},{2,26},{10... | collective-permute-start | bytes 2654216 | tf_op jit(solution)/shard_map/ppermute | solution.py:21
  69.2 38.3 %collective-permute-start.19 = (bf16[4,288,384]{2,1,0:T(8,128)(2,1)}, bf16[4,288,384]{2,1,0:T(8,128)(2,1)}, u32[]{:S(2)}, u32[]{:S(2)}) collective-permute-start(bf16[4,288,384]{2,1,0:T(8,128)(2,1)} %pad_maximum_fusion.1.refs_4_), channel_id=1, source_target_pairs={{0,16},{8,24},{16,0},{24,8},{1,17},{9,25},{17,1},{25,9},{2,18},{10... | collective-permute-start | bytes 2654216 | tf_op jit(solution)/shard_map/ppermute | solution.py:21
  69.2 41.8 %collective-permute-start.18 = (bf16[4,288,384]{2,1,0:T(8,128)(2,1)}, bf16[4,288,384]{2,1,0:T(8,128)(2,1)}, u32[]{:S(2)}, u32[]{:S(2)}) collective-permute-start(bf16[4,288,384]{2,1,0:T(8,128)(2,1)} %pad_maximum_fusion.1.refs_4_), channel_id=1, source_target_pairs={{0,8},{8,16},{16,24},{24,0},{1,9},{9,17},{17,25},{25,1},{2,10},{10... | collective-permute-start | bytes 2654216 | tf_op jit(solution)/shard_map/ppermute | solution.py:21
  134.3 43.6 %collective-permute-start.21 = (f32[2,288,768]{2,1,0:T(8,128)}, f32[2,288,768]{2,1,0:T(8,128)S(1)}, u32[]{:S(2)}, u32[]{:S(2)}) collective-permute-start(f32[2,288,768]{2,1,0:T(8,128)} %get-tuple-element.9), channel_id=1, source_target_pairs={{0,1},{1,0},{2,3},{3,2},{4,5},{5,4},{6,7},{7,6},{8,9},{9,8},{10,11... | collective-permute-start | bytes 5308424 | tf_op jit(solution)/shard_map/ppermute | solution.py:25
  135.2 45.4 %collective-permute-start.22 = (f32[2,288,768]{2,1,0:T(8,128)}, f32[2,288,768]{2,1,0:T(8,128)S(1)}, u32[]{:S(2)}, u32[]{:S(2)}) collective-permute-start(f32[2,288,768]{2,1,0:T(8,128)} %get-tuple-element.11), channel_id=1, source_target_pairs={{0,1},{1,0},{2,3},{3,2},{4,5},{5,4},{6,7},{7,6},{8,9},{9,8},{10,11... | collective-permute-start | bytes 5308424 | tf_op jit(solution)/shard_map/ppermute | solution.py:25
  140.0 7.2 %collective-permute-start.27 = (f32[96,384]{1,0:T(8,128)S(1)}, f32[96,384]{1,0:T(8,128)S(1)}, u32[]{:S(2)}, u32[]{:S(2)}) collective-permute-start(f32[96,384]{1,0:T(8,128)S(1)} %split.17), channel_id=1, source_target_pairs={{0,6},{2,4},{4,2},{6,0},{1,7},{3,5},{5,3},{7,1},{8,14},{10,12},{12... | collective-permute-start | bytes 442376 | tf_op jit(solution)/shard_map/ppermute | solution.py:144
  177.1 10.0 %collective-permute-start.34 = (f32[96,384]{1,0:T(8,128)S(1)}, f32[96,384]{1,0:T(8,128)S(1)}, u32[]{:S(2)}, u32[]{:S(2)}) collective-permute-start(f32[96,384]{1,0:T(8,128)S(1)} %pad_maximum_fusion.3), channel_id=1, source_target_pairs={{0,6},{2,4},{4,2},{6,0},{1,7},{3,5},{5,3},{7,1},{8,14},{10,12},{12... | collective-permute-start | bytes 442376 | tf_op jit(solution)/shard_map/ppermute | solution.py:144
  178.1 14.8 %collective-permute-start.24 = (bf16[288,768]{1,0:T(8,128)(2,1)S(1)}, bf16[288,768]{1,0:T(8,128)(2,1)S(1)}, u32[]{:S(2)}, u32[]{:S(2)}) collective-permute-start(bf16[288,768]{1,0:T(8,128)(2,1)S(1)} %fusion.8), channel_id=1, source_target_pairs={{0,6},{2,0},{4,2},{6,4},{1,7},{3,1},{5,3},{7,5},{8,14},{10,8},{12,... | collective-permute-start | bytes 1327112 | tf_op jit(solution)/shard_map/ppermute | solution.py:21
  180.8 15.7 %collective-permute-start.23 = (bf16[288,768]{1,0:T(8,128)(2,1)S(1)}, bf16[288,768]{1,0:T(8,128)(2,1)S(1)}, u32[]{:S(2)}, u32[]{:S(2)}) collective-permute-start(bf16[288,768]{1,0:T(8,128)(2,1)S(1)} %get-tuple-element.16), channel_id=1, source_target_pairs={{0,2},{2,4},{4,6},{6,0},{1,3},{3,5},{5,7},{7,1},{8,10},{10,12},{12... | collective-permute-start | bytes 1327112 | tf_op jit(solution)/shard_map/ppermute | solution.py:21
  180.9 15.7 %collective-permute-start.25 = (bf16[288,768]{1,0:T(8,128)(2,1)S(1)}, bf16[288,768]{1,0:T(8,128)(2,1)S(1)}, u32[]{:S(2)}, u32[]{:S(2)}) collective-permute-start(bf16[288,768]{1,0:T(8,128)(2,1)S(1)} %get-tuple-element.17), channel_id=1, source_target_pairs={{0,4},{2,6},{4,0},{6,2},{1,5},{3,7},{5,1},{7,3},{8,12},{10,14},{12... | collective-permute-start | bytes 1327112 | tf_op jit(solution)/shard_map/ppermute | solution.py:21
  (24 other events, 266.2 us)

commit v3 on v2

--- a/solution.py
+++ b/solution.py
@@ -156,7 +156,9 @@
     around = [shard]
     for s in (1, 2, 3):
         around.append(move(shard, "y", s))
-    across = [swap(p) for p in around]
+    across = []
+    for part in around:
+        across.append(swap(part))
     sets = []
     for half, near, far in ((plane_a, "x", "z"), (plane_b, "z", "x")):
         first = [half]
@@ -229,7 +231,7 @@
             pltpu.SemaphoreType.DMA((3,)),
             pltpu.SemaphoreType.DMA((2, 2)),
         ],
-        compiler_params=pltpu.CompilerParams(vmem_limit_bytes=62_000_000),
+        compiler_params=pltpu.CompilerParams(vmem_limit_bytes=36 * 2**20),
         cost_estimate=pl.CostEstimate(
             flops=11_800_000_000, bytes_accessed=18_000_000, transcendentals=0
         ),

time: 199 us -> 199 us (level)
  local copies, waits for them, and re-layouts: 11.3 us -> 15.9 us
  waiting for transfers between devices: 93.6 us -> 91 us
    unnamed x25 -> x41, local copies, waits for them, and re-layouts: 2.89 us -> 9.2 us
    ppermute x18, waiting for transfers between devices: 50.4 us -> 47.3 us  [move(): return lax.ppermute(x, axis, [(i, (i + s) % n) for i in range(n)])]
where the time goes in v3:
time: 199 us; the launch traced here: 198 us
  waiting for transfers between devices  91 us (46%)
  starting transfers between devices  56.4 us (28%)
  Pallas kernels  26.1 us (13%)
  local copies, waits for them, and re-layouts  15.9 us (8%)
  other arithmetic  8.09 us (4%)
    ppermute x18, starting transfers between devices, move(): return lax.ppermute(x, axis, [(i, (i + s) % n) for i in range(n)])  49.4 us
    ppermute x18, waiting for transfers between devices, move(): return lax.ppermute(x, axis, [(i, (i + s) % n) for i in range(n)])  47.3 us
    ppermute x8, waiting for transfers between devices, swap_bits(): lax.ppermute(x, axis, [(i, i ^ bits) for i in range(lax.axis_size(axis))])  38.5 us
    pallas_call x1, Pallas kernels, local(): pl.pallas_call(pair_kernel, in_specs=[SMEM, SMEM, ANY, vmem, vmem] + [ANY...  22 us
    unnamed x41, local copies, waits for them, and re-layouts  9.2 us
    ppermute x8, waiting for transfers between devices, swap(): return lax.ppermute(x, 'c', [(0, 1), (1, 0)])  5.09 us
  transfers between devices with their start and end apart: 36, of which 20 were waited for; matrix products, arithmetic and copies ran while one was open for 7% of the time, Pallas kernels for 2%

profile of v3, /device:TPU:0, one launch (start us, length us, event | category | flops | bytes accessed | tf_op | source)
XLA Modules:
  0.0 198.4 jit_solution(479524136556009008)
XLA Ops:
  1.8 3.2 %collective-permute-start.2 = (bf16[2,288,384]{2,1,0:T(8,128)(2,1)S(1)}, bf16[2,288,384]{2,1,0:T(8,128)(2,1)S(1)}, u32[]{:S(2)}, u32[]{:S(2)}) collective-permute-start(bf16[2,288,384]{2,1,0:T(8,128)(2,1)S(1)} %bitcast.39), channel_id=1, source_target_pairs={{0,6},{2,0},{4,2},{6,4},{1,7},{3,1},{5,3},{7,5},{8,14},{10,8},{12,... | collective-permute-start | bytes 1327112 | tf_op jit(solution)/shard_map/ppermute | solution.py:21
  7.8 18.8 %collective-permute-start.10 = (bf16[288,384]{1,0:T(8,128)(2,1)S(1)}, bf16[288,384]{1,0:T(8,128)(2,1)S(1)}, u32[]{:S(2)}, u32[]{:S(2)}) collective-permute-start(bf16[288,384]{1,0:T(8,128)(2,1)S(1)} %collective-permute-done.7), channel_id=1, source_target_pairs={{0,24},{8,0},{16,8},{24,16},{1,25},{9,1},{17,9},{25,17},{2,26},{10... | collective-permute-start | bytes 663560 | tf_op jit(solution)/shard_map/ppermute | solution.py:21
  27.5 4.7 %collective-permute-start.17 = (bf16[288,384]{1,0:T(8,128)(2,1)S(1)}, bf16[288,384]{1,0:T(8,128)(2,1)}, u32[]{:S(2)}, u32[]{:S(2)}) collective-permute-start(bf16[288,384]{1,0:T(8,128)(2,1)S(1)} %collective-permute-done.14), channel_id=1, source_target_pairs={{0,96},{32,0},{64,32},{96,64},{1,97},{33,1},{65,33},{97,65},{2,98}... | collective-permute-start | bytes 663560 | tf_op jit(solution)/shard_map/ppermute | solution.py:21
  36.5 5.1 %collective-permute-start = (bf16[2,288,384]{2,1,0:T(8,128)(2,1)S(1)}, bf16[2,288,384]{2,1,0:T(8,128)(2,1)S(1)}, u32[]{:S(2)}, u32[]{:S(2)}) collective-permute-start(bf16[2,288,384]{2,1,0:T(8,128)(2,1)S(1)} %bitcast.42), channel_id=1, source_target_pairs={{0,2},{2,4},{4,6},{6,0},{1,3},{3,5},{5,7},{7,1},{8,10},{10,12},{12... | collective-permute-start | bytes 1327112 | tf_op jit(solution)/shard_map/ppermute | solution.py:21
  41.5 4.0 %collective-permute-start.16 = (bf16[288,384]{1,0:T(8,128)(2,1)S(1)}, bf16[288,384]{1,0:T(8,128)(2,1)S(1)}, u32[]{:S(2)}, u32[]{:S(2)}) collective-permute-start(bf16[288,384]{1,0:T(8,128)(2,1)S(1)} %collective-permute-done.14), channel_id=1, source_target_pairs={{0,64},{32,96},{64,0},{96,32},{1,65},{33,97},{65,1},{97,33},{2,66}... | collective-permute-start | bytes 663560 | tf_op jit(solution)/shard_map/ppermute | solution.py:21
  46.7 3.9 %collective-permute-done.16 = bf16[288,384]{1,0:T(8,128)(2,1)S(1)} collective-permute-done((bf16[288,384]{1,0:T(8,128)(2,1)S(1)}, bf16[288,384]{1,0:T(8,128)(2,1)S(1)}, u32[]{:S(2)}, u32[]{:S(2)}) %collective-permute-start.16) | collective-permute-done | bytes 221216 | tf_op jit(solution)/shard_map/ppermute | solution.py:21
  50.8 7.2 %collective-permute-done.15 = bf16[288,384]{1,0:T(8,128)(2,1)S(1)} collective-permute-done((bf16[288,384]{1,0:T(8,128)(2,1)S(1)}, bf16[288,384]{1,0:T(8,128)(2,1)S(1)}, u32[]{:S(2)}, u32[]{:S(2)}) %collective-permute-start.15) | collective-permute-done | bytes 221216 | tf_op jit(solution)/shard_map/ppermute | solution.py:21
  67.5 3.7 %collective-permute-start.20 = (bf16[4,288,384]{2,1,0:T(8,128)(2,1)S(1)}, bf16[4,288,384]{2,1,0:T(8,128)(2,1)}, u32[]{:S(2)}, u32[]{:S(2)}) collective-permute-start(bf16[4,288,384]{2,1,0:T(8,128)(2,1)S(1)} %pad_maximum_fusion.1.refs_4_), channel_id=1, source_target_pairs={{0,24},{8,0},{16,8},{24,16},{1,25},{9,1},{17,9},{25,17},{2,26},{10... | collective-permute-start | bytes 2654216 | tf_op jit(solution)/shard_map/ppermute | solution.py:21
  83.0 2.7 %turn.1.left_ref = bf16[768,2304]{1,0:T(8,128)(2,1)S(1)} custom-call(s32[8]{0:T(128)S(1)} %pad_add_fusion.slot_ref, bf16[2,288,384]{2,1,0:T(8,128)(2,1)S(1)} %bitcast.44, bf16[2,288,384]{2,1,0:T(8,128)(2,1)S(1)} %collective-permute-done.refs_1_, bf16[2,288,384]{2,1,0:T(8,128)(2,1)S(1)} %collective-permute-done.1.refs_2_, ...), custom_call_target="tpu_custom_call" | custom-call | bytes 7000000 | tf_op jit(solution)/shard_map/turn/pallas_call | solution.py:205
  86.3 18.0 %collective-permute-done.11.refs_1_ = bf16[4,288,384]{2,1,0:T(8,128)(2,1)} collective-permute-done((bf16[4,288,384]{2,1,0:T(8,128)(2,1)S(1)}, bf16[4,288,384]{2,1,0:T(8,128)(2,1)}, u32[]{:S(2)}, u32[]{:S(2)}) %collective-permute-start.11) | collective-permute-done | bytes 884768 | tf_op jit(solution)/shard_map/ppermute | solution.py:21
  104.3 4.9 %collective-permute-done.20.refs_7_ = bf16[4,288,384]{2,1,0:T(8,128)(2,1)} collective-permute-done((bf16[4,288,384]{2,1,0:T(8,128)(2,1)S(1)}, bf16[4,288,384]{2,1,0:T(8,128)(2,1)}, u32[]{:S(2)}, u32[]{:S(2)}) %collective-permute-start.20) | collective-permute-done | bytes 884768 | tf_op jit(solution)/shard_map/ppermute | solution.py:21
  109.2 4.6 %collective-permute-done.18.refs_5_ = bf16[4,288,384]{2,1,0:T(8,128)(2,1)} collective-permute-done((bf16[4,288,384]{2,1,0:T(8,128)(2,1)S(1)}, bf16[4,288,384]{2,1,0:T(8,128)(2,1)}, u32[]{:S(2)}, u32[]{:S(2)}) %collective-permute-start.18) | collective-permute-done | bytes 884768 | tf_op jit(solution)/shard_map/ppermute | solution.py:21
  113.8 22.0 %pairs.1 = (f32[2,288,768]{2,1,0:T(8,128)S(1)}, f32[2,288,768]{2,1,0:T(8,128)S(1)}, f32[2,288,768]{2,1,0:T(8,128)S(1)}, f32[2,288,768]{2,1,0:T(8,128)S(1)}, f32[...) custom-call(s32[25]{0:T(128)S(1)} %concatenate.16.place_ref, f32[16]{0:T(128)S(1)} %concatenate.17.scal_ref, ...), custom_call_target="tpu_custom_call" | custom-call | flops 11800000512 | bytes 18000000 | tf_op jit(solution)/shard_map/pairs/pallas_call | solution.py:218
  136.5 3.5 %collective-permute-done.26 = f32[192,384]{1,0:T(8,128)S(1)} collective-permute-done((f32[192,384]{1,0:T(8,128)S(1)}, f32[192,384]{1,0:T(8,128)S(1)}, u32[]{:S(2)}, u32[]{:S(2)}) %collective-permute-start.26) | collective-permute-done | bytes 294944 | tf_op jit(solution)/shard_map/ppermute | solution.py:25
  140.8 6.5 %collective-permute-done.27 = f32[96,384]{1,0:T(8,128)S(1)} collective-permute-done((f32[96,384]{1,0:T(8,128)S(1)}, f32[96,384]{1,0:T(8,128)S(1)}, u32[]{:S(2)}, u32[]{:S(2)}) %collective-permute-start.27) | collective-permute-done | bytes 147488 | tf_op jit(solution)/shard_map/ppermute | solution.py:144
  147.4 4.3 %collective-permute-done.28 = f32[48,384]{1,0:T(8,128)S(1)} collective-permute-done((f32[48,384]{1,0:T(8,128)S(1)}, f32[48,384]{1,0:T(8,128)S(1)}, u32[]{:S(2)}, u32[]{:S(2)}) %collective-permute-start.28) | collective-permute-done | bytes 73760 | tf_op jit(solution)/shard_map/ppermute | solution.py:144
  151.8 4.3 %collective-permute-done.29 = f32[48,384]{1,0:T(8,128)S(1)} collective-permute-done((f32[48,384]{1,0:T(8,128)S(1)}, f32[48,384]{1,0:T(8,128)S(1)}, u32[]{:S(2)}, u32[]{:S(2)}) %collective-permute-start.29) | collective-permute-done | bytes 73760 | tf_op jit(solution)/shard_map/ppermute | solution.py:144
  156.9 5.0 %collective-permute-done.30 = f32[48,384]{1,0:T(8,128)S(1)} collective-permute-done((f32[48,384]{1,0:T(8,128)S(1)}, f32[48,384]{1,0:T(8,128)S(1)}, u32[]{:S(2)}, u32[]{:S(2)}) %collective-permute-start.30) | collective-permute-done | bytes 73760 | tf_op jit(solution)/shard_map/ppermute | solution.py:144
  162.1 4.2 %collective-permute-done.31 = f32[48,384]{1,0:T(8,128)S(1)} collective-permute-done((f32[48,384]{1,0:T(8,128)S(1)}, f32[48,384]{1,0:T(8,128)S(1)}, u32[]{:S(2)}, u32[]{:S(2)}) %collective-permute-start.31) | collective-permute-done | bytes 73760 | tf_op jit(solution)/shard_map/ppermute | solution.py:144
  167.6 4.4 %collective-permute-done.32 = f32[48,384]{1,0:T(8,128)S(1)} collective-permute-done((f32[48,384]{1,0:T(8,128)S(1)}, f32[48,384]{1,0:T(8,128)S(1)}, u32[]{:S(2)}, u32[]{:S(2)}) %collective-permute-start.32) | collective-permute-done | bytes 73760 | tf_op jit(solution)/shard_map/ppermute | solution.py:144
  172.0 5.1 %collective-permute-done.33 = f32[48,384]{1,0:T(8,128)S(1)} collective-permute-done((f32[48,384]{1,0:T(8,128)S(1)}, f32[48,384]{1,0:T(8,128)S(1)}, u32[]{:S(2)}, u32[]{:S(2)}) %collective-permute-start.33) | collective-permute-done | bytes 73760 | tf_op jit(solution)/shard_map/ppermute | solution.py:144
  178.0 2.7 %collective-permute-start.24 = (bf16[288,768]{1,0:T(8,128)(2,1)S(1)}, bf16[288,768]{1,0:T(8,128)(2,1)S(1)}, u32[]{:S(2)}, u32[]{:S(2)}) collective-permute-start(bf16[288,768]{1,0:T(8,128)(2,1)S(1)} %fusion.8), channel_id=1, source_target_pairs={{0,6},{2,0},{4,2},{6,4},{1,7},{3,1},{5,3},{7,5},{8,14},{10,8},{12,... | collective-permute-start | bytes 1327112 | tf_op jit(solution)/shard_map/ppermute | solution.py:21
  182.5 4.7 %collective-permute-done.34 = f32[96,384]{1,0:T(8,128)S(1)} collective-permute-done((f32[96,384]{1,0:T(8,128)S(1)}, f32[96,384]{1,0:T(8,128)S(1)}, u32[]{:S(2)}, u32[]{:S(2)}) %collective-permute-start.34) | collective-permute-done | bytes 147488 | tf_op jit(solution)/shard_map/ppermute | solution.py:144
  193.0 3.8 %collective-permute-done.23 = bf16[288,768]{1,0:T(8,128)(2,1)S(1)} collective-permute-done((bf16[288,768]{1,0:T(8,128)(2,1)S(1)}, bf16[288,768]{1,0:T(8,128)(2,1)S(1)}, u32[]{:S(2)}, u32[]{:S(2)}) %collective-permute-start.23) | collective-permute-done | bytes 442400 | tf_op jit(solution)/shard_map/ppermute | solution.py:21
  (135 shorter events, 46.2 us)
Async XLA Ops:
  1.8 56.3 %collective-permute-start.2 = (bf16[2,288,384]{2,1,0:T(8,128)(2,1)S(1)}, bf16[2,288,384]{2,1,0:T(8,128)(2,1)S(1)}, u32[]{:S(2)}, u32[]{:S(2)}) collective-permute-start(bf16[2,288,384]{2,1,0:T(8,128)(2,1)S(1)} %bitcast.39), channel_id=1, source_target_pairs={{0,6},{2,0},{4,2},{6,4},{1,7},{3,1},{5,3},{7,5},{8,14},{10,8},{12,... | collective-permute-start | bytes 1327112 | tf_op jit(solution)/shard_map/ppermute | solution.py:21
  5.0 22.5 %collective-permute-start.14 = (bf16[288,384]{1,0:T(8,128)(2,1)S(1)}, bf16[288,384]{1,0:T(8,128)(2,1)S(1)}, u32[]{:S(2)}, u32[]{:S(2)}) collective-permute-start(bf16[288,384]{1,0:T(8,128)(2,1)S(1)} %get-tuple-element.18), channel_id=1, source_target_pairs={{0,0},{1,32},{2,24},{3,56},{4,16},{5,48},{6,8},{7,40},{8,10},{9,42... | collective-permute-start | bytes 663560 | tf_op jit(solution)/shard_map/ppermute | solution.py:155
  7.8 27.4 %collective-permute-start.10 = (bf16[288,384]{1,0:T(8,128)(2,1)S(1)}, bf16[288,384]{1,0:T(8,128)(2,1)S(1)}, u32[]{:S(2)}, u32[]{:S(2)}) collective-permute-start(bf16[288,384]{1,0:T(8,128)(2,1)S(1)} %collective-permute-done.7), channel_id=1, source_target_pairs={{0,24},{8,0},{16,8},{24,16},{1,25},{9,1},{17,9},{25,17},{2,26},{10... | collective-permute-start | bytes 663560 | tf_op jit(solution)/shard_map/ppermute | solution.py:21
  26.6 9.8 %collective-permute-start.9 = (bf16[288,384]{1,0:T(8,128)(2,1)S(1)}, bf16[288,384]{1,0:T(8,128)(2,1)S(1)}, u32[]{:S(2)}, u32[]{:S(2)}) collective-permute-start(bf16[288,384]{1,0:T(8,128)(2,1)S(1)} %collective-permute-done.7), channel_id=1, source_target_pairs={{0,16},{8,24},{16,0},{24,8},{1,17},{9,25},{17,1},{25,9},{2,18},{10... | collective-permute-start | bytes 663560 | tf_op jit(solution)/shard_map/ppermute | solution.py:21
  26.6 14.9 %collective-permute-start.8 = (bf16[288,384]{1,0:T(8,128)(2,1)S(1)}, bf16[288,384]{1,0:T(8,128)(2,1)}, u32[]{:S(2)}, u32[]{:S(2)}) collective-permute-start(bf16[288,384]{1,0:T(8,128)(2,1)S(1)} %collective-permute-done.7), channel_id=1, source_target_pairs={{0,8},{8,16},{16,24},{24,0},{1,9},{9,17},{17,25},{25,1},{2,10},{10... | collective-permute-start | bytes 663560 | tf_op jit(solution)/shard_map/ppermute | solution.py:21
  27.5 19.1 %collective-permute-start.17 = (bf16[288,384]{1,0:T(8,128)(2,1)S(1)}, bf16[288,384]{1,0:T(8,128)(2,1)}, u32[]{:S(2)}, u32[]{:S(2)}) collective-permute-start(bf16[288,384]{1,0:T(8,128)(2,1)S(1)} %collective-permute-done.14), channel_id=1, source_target_pairs={{0,96},{32,0},{64,32},{96,64},{1,97},{33,1},{65,33},{97,65},{2,98}... | collective-permute-start | bytes 663560 | tf_op jit(solution)/shard_map/ppermute | solution.py:21
  35.2 23.3 %collective-permute-start.1 = (bf16[2,288,384]{2,1,0:T(8,128)(2,1)S(1)}, bf16[2,288,384]{2,1,0:T(8,128)(2,1)S(1)}, u32[]{:S(2)}, u32[]{:S(2)}) collective-permute-start(bf16[2,288,384]{2,1,0:T(8,128)(2,1)S(1)} %bitcast.41), channel_id=1, source_target_pairs={{0,4},{2,6},{4,0},{6,2},{1,5},{3,7},{5,1},{7,3},{8,12},{10,14},{12... | collective-permute-start | bytes 1327112 | tf_op jit(solution)/shard_map/ppermute | solution.py:21
  36.5 22.2 %collective-permute-start = (bf16[2,288,384]{2,1,0:T(8,128)(2,1)S(1)}, bf16[2,288,384]{2,1,0:T(8,128)(2,1)S(1)}, u32[]{:S(2)}, u32[]{:S(2)}) collective-permute-start(bf16[2,288,384]{2,1,0:T(8,128)(2,1)S(1)} %bitcast.42), channel_id=1, source_target_pairs={{0,2},{2,4},{4,6},{6,0},{1,3},{3,5},{5,7},{7,1},{8,10},{10,12},{12... | collective-permute-start | bytes 1327112 | tf_op jit(solution)/shard_map/ppermute | solution.py:21
  41.5 9.0 %collective-permute-start.16 = (bf16[288,384]{1,0:T(8,128)(2,1)S(1)}, bf16[288,384]{1,0:T(8,128)(2,1)S(1)}, u32[]{:S(2)}, u32[]{:S(2)}) collective-permute-start(bf16[288,384]{1,0:T(8,128)(2,1)S(1)} %collective-permute-done.14), channel_id=1, source_target_pairs={{0,64},{32,96},{64,0},{96,32},{1,65},{33,97},{65,1},{97,33},{2,66}... | collective-permute-start | bytes 663560 | tf_op jit(solution)/shard_map/ppermute | solution.py:21
  46.6 25.4 %collective-permute-start.13 = (bf16[4,288,384]{2,1,0:T(8,128)(2,1)S(1)}, bf16[4,288,384]{2,1,0:T(8,128)(2,1)S(1)}, u32[]{:S(2)}, u32[]{:S(2)}) collective-permute-start(bf16[4,288,384]{2,1,0:T(8,128)(2,1)S(1)} %pad_maximum_fusion.refs_0_), channel_id=1, source_target_pairs={{0,96},{32,0},{64,32},{96,64},{1,97},{33,1},{65,33},{97,65},{2,98}... | collective-permute-start | bytes 2654216 | tf_op jit(solution)/shard_map/ppermute | solution.py:21
  50.6 7.4 %collective-permute-start.15 = (bf16[288,384]{1,0:T(8,128)(2,1)S(1)}, bf16[288,384]{1,0:T(8,128)(2,1)S(1)}, u32[]{:S(2)}, u32[]{:S(2)}) collective-permute-start(bf16[288,384]{1,0:T(8,128)(2,1)S(1)} %collective-permute-done.14), channel_id=1, source_target_pairs={{0,32},{32,64},{64,96},{96,0},{1,33},{33,65},{65,97},{97,1},{2,34}... | collective-permute-start | bytes 663560 | tf_op jit(solution)/shard_map/ppermute | solution.py:21
  58.5 8.2 %collective-permute-start.5 = (bf16[2,288,384]{2,1,0:T(8,128)(2,1)S(1)}, bf16[2,288,384]{2,1,0:T(8,128)(2,1)S(1)}, u32[]{:S(2)}, u32[]{:S(2)}) collective-permute-start(bf16[2,288,384]{2,1,0:T(8,128)(2,1)S(1)} %collective-permute-done.1.refs_2_), channel_id=1, source_target_pairs={{0,1},{1,0},{2,3},{3,2},{4,5},{5,4},{6,7},{7,6},{8,9},{9,8},{10,11... | collective-permute-start | bytes 1327112 | tf_op jit(solution)/shard_map/ppermute | solution.py:25
  58.6 12.6 %collective-permute-start.4 = (bf16[2,288,384]{2,1,0:T(8,128)(2,1)S(1)}, bf16[2,288,384]{2,1,0:T(8,128)(2,1)S(1)}, u32[]{:S(2)}, u32[]{:S(2)}) collective-permute-start(bf16[2,288,384]{2,1,0:T(8,128)(2,1)S(1)} %collective-permute-done.refs_1_), channel_id=1, source_target_pairs={{0,1},{1,0},{2,3},{3,2},{4,5},{5,4},{6,7},{7,6},{8,9},{9,8},{10,11... | collective-permute-start | bytes 1327112 | tf_op jit(solution)/shard_map/ppermute | solution.py:25
  62.1 24.2 %collective-permute-start.12 = (bf16[4,288,384]{2,1,0:T(8,128)(2,1)S(1)}, bf16[4,288,384]{2,1,0:T(8,128)(2,1)}, u32[]{:S(2)}, u32[]{:S(2)}) collective-permute-start(bf16[4,288,384]{2,1,0:T(8,128)(2,1)S(1)} %pad_maximum_fusion.refs_0_), channel_id=1, source_target_pairs={{0,64},{32,96},{64,0},{96,32},{1,65},{33,97},{65,1},{97,33},{2,66}... | collective-permute-start | bytes 2654216 | tf_op jit(solution)/shard_map/ppermute | solution.py:21
  64.8 39.6 %collective-permute-start.11 = (bf16[4,288,384]{2,1,0:T(8,128)(2,1)S(1)}, bf16[4,288,384]{2,1,0:T(8,128)(2,1)}, u32[]{:S(2)}, u32[]{:S(2)}) collective-permute-start(bf16[4,288,384]{2,1,0:T(8,128)(2,1)S(1)} %pad_maximum_fusion.refs_0_), channel_id=1, source_target_pairs={{0,32},{32,64},{64,96},{96,0},{1,33},{33,65},{65,97},{97,1},{2,34}... | collective-permute-start | bytes 2654216 | tf_op jit(solution)/shard_map/ppermute | solution.py:21
  67.5 41.7 %collective-permute-start.20 = (bf16[4,288,384]{2,1,0:T(8,128)(2,1)S(1)}, bf16[4,288,384]{2,1,0:T(8,128)(2,1)}, u32[]{:S(2)}, u32[]{:S(2)}) collective-permute-start(bf16[4,288,384]{2,1,0:T(8,128)(2,1)S(1)} %pad_maximum_fusion.1.refs_4_), channel_id=1, source_target_pairs={{0,24},{8,0},{16,8},{24,16},{1,25},{9,1},{17,9},{25,17},{2,26},{10... | collective-permute-start | bytes 2654216 | tf_op jit(solution)/shard_map/ppermute | solution.py:21
  72.0 37.2 %collective-permute-start.19 = (bf16[4,288,384]{2,1,0:T(8,128)(2,1)S(1)}, bf16[4,288,384]{2,1,0:T(8,128)(2,1)}, u32[]{:S(2)}, u32[]{:S(2)}) collective-permute-start(bf16[4,288,384]{2,1,0:T(8,128)(2,1)S(1)} %pad_maximum_fusion.1.refs_4_), channel_id=1, source_target_pairs={{0,16},{8,24},{16,0},{24,8},{1,17},{9,25},{17,1},{25,9},{2,18},{10... | collective-permute-start | bytes 2654216 | tf_op jit(solution)/shard_map/ppermute | solution.py:21
  72.9 40.9 %collective-permute-start.18 = (bf16[4,288,384]{2,1,0:T(8,128)(2,1)S(1)}, bf16[4,288,384]{2,1,0:T(8,128)(2,1)}, u32[]{:S(2)}, u32[]{:S(2)}) collective-permute-start(bf16[4,288,384]{2,1,0:T(8,128)(2,1)S(1)} %pad_maximum_fusion.1.refs_4_), channel_id=1, source_target_pairs={{0,8},{8,16},{16,24},{24,0},{1,9},{9,17},{17,25},{25,1},{2,10},{10... | collective-permute-start | bytes 2654216 | tf_op jit(solution)/shard_map/ppermute | solution.py:21
  135.8 42.0 %collective-permute-start.21 = (f32[2,288,768]{2,1,0:T(8,128)S(1)}, f32[2,288,768]{2,1,0:T(8,128)S(1)}, u32[]{:S(2)}, u32[]{:S(2)}) collective-permute-start(f32[2,288,768]{2,1,0:T(8,128)S(1)} %get-tuple-element.9), channel_id=1, source_target_pairs={{0,1},{1,0},{2,3},{3,2},{4,5},{5,4},{6,7},{7,6},{8,9},{9,8},{10,11... | collective-permute-start | bytes 5308424 | tf_op jit(solution)/shard_map/ppermute | solution.py:25
  136.4 44.3 %collective-permute-start.22 = (f32[2,288,768]{2,1,0:T(8,128)S(1)}, f32[2,288,768]{2,1,0:T(8,128)S(1)}, u32[]{:S(2)}, u32[]{:S(2)}) collective-permute-start(f32[2,288,768]{2,1,0:T(8,128)S(1)} %get-tuple-element.11), channel_id=1, source_target_pairs={{0,1},{1,0},{2,3},{3,2},{4,5},{5,4},{6,7},{7,6},{8,9},{9,8},{10,11... | collective-permute-start | bytes 5308424 | tf_op jit(solution)/shard_map/ppermute | solution.py:25
  177.2 10.1 %collective-permute-start.34 = (f32[96,384]{1,0:T(8,128)S(1)}, f32[96,384]{1,0:T(8,128)S(1)}, u32[]{:S(2)}, u32[]{:S(2)}) collective-permute-start(f32[96,384]{1,0:T(8,128)S(1)} %pad_maximum_fusion.3), channel_id=1, source_target_pairs={{0,6},{2,4},{4,2},{6,0},{1,7},{3,5},{5,3},{7,1},{8,14},{10,12},{12... | collective-permute-start | bytes 442376 | tf_op jit(solution)/shard_map/ppermute | solution.py:144
  178.0 15.0 %collective-permute-start.24 = (bf16[288,768]{1,0:T(8,128)(2,1)S(1)}, bf16[288,768]{1,0:T(8,128)(2,1)S(1)}, u32[]{:S(2)}, u32[]{:S(2)}) collective-permute-start(bf16[288,768]{1,0:T(8,128)(2,1)S(1)} %fusion.8), channel_id=1, source_target_pairs={{0,6},{2,0},{4,2},{6,4},{1,7},{3,1},{5,3},{7,5},{8,14},{10,8},{12,... | collective-permute-start | bytes 1327112 | tf_op jit(solution)/shard_map/ppermute | solution.py:21
  181.0 15.7 %collective-permute-start.23 = (bf16[288,768]{1,0:T(8,128)(2,1)S(1)}, bf16[288,768]{1,0:T(8,128)(2,1)S(1)}, u32[]{:S(2)}, u32[]{:S(2)}) collective-permute-start(bf16[288,768]{1,0:T(8,128)(2,1)S(1)} %get-tuple-element.16), channel_id=1, source_target_pairs={{0,2},{2,4},{4,6},{6,0},{1,3},{3,5},{5,7},{7,1},{8,10},{10,12},{12... | collective-permute-start | bytes 1327112 | tf_op jit(solution)/shard_map/ppermute | solution.py:21
  181.1 15.7 %collective-permute-start.25 = (bf16[288,768]{1,0:T(8,128)(2,1)S(1)}, bf16[288,768]{1,0:T(8,128)(2,1)S(1)}, u32[]{:S(2)}, u32[]{:S(2)}) collective-permute-start(bf16[288,768]{1,0:T(8,128)(2,1)S(1)} %get-tuple-element.17), channel_id=1, source_target_pairs={{0,4},{2,6},{4,0},{6,2},{1,5},{3,7},{5,1},{7,3},{8,12},{10,14},{12... | collective-permute-start | bytes 1327112 | tf_op jit(solution)/shard_map/ppermute | solution.py:21
  (32 other events, 265.1 us)

commit v4 on v3

--- a/solution.py
+++ b/solution.py
@@ -56,11 +56,14 @@
 
 
 def pair_kernel(place_ref, scal_ref, left_ref, row_ref, col_ref, *refs):
-    sets_a, sets_b = refs[0:4], refs[4:8]
-    parts = (refs[8:10], refs[10:12])
-    dens_keep, dens_give = refs[12:14]
-    held, own_ref, k_ref, amp_ref, ampt_ref, dens_ref, both_ref, sem, out_sem = refs[14:]
+    sets_a, sets_b = refs[0:5], refs[5:10]
+    parts = (refs[10:12], refs[12:14])
+    dens_keep, dens_give = refs[14:16]
+    held, k_ref, amp_ref, ampt_ref, dens_ref, both_ref, sem, out_sem = refs[16:]
     rows, v = sets_a[0].shape[1:]
+
+    def at(sets, s, t):
+        return sets[s].at[t] if s != 2 else sets[2 if t < 2 else 4].at[t % 2]
 
     def piece(source, slot, h, half):
         at = pl.ds(pl.multiple_of(slot * rows, rows), rows)
@@ -68,31 +71,32 @@
             source, held.at[h, at, half * v : (half + 1) * v], sem.at[h]
         )
 
-    fetch = pltpu.make_async_copy(left_ref, own_ref, sem.at[2])
-    fetch.start()
     for s in range(4):
         for t in range(4):
             for source, zs, ys, half in (
-                (sets_a[s], s, 4 + t, 0),
-                (sets_b[s], t, 8 + s, 1),
+                (at(sets_a, s, t), s, 4 + t, 0),
+                (at(sets_b, s, t), t, 8 + s, 1),
             ):
                 zz = place_ref[zs]
-                piece(source.at[t], 2 * place_ref[ys] + lax.rem(zz, 2), zz // 2, half).start()
-    fetch.wait()
-    for h in range(2):
-        for _ in range(16):
-            piece(sets_a[0].at[0], 0, h, 0).wait()
-        k_ref[...] = jnp.dot(own_ref[...], held[h], preferred_element_type=F32)
-        for i in range(2):
-            for j in range(2):
-                a, b = slice(i * v, (i + 1) * v), slice(j * v, (j + 1) * v)
-                k = k_ref[a, b]
-                kt = k.T
-                pair = scal_ref[i] + scal_ref[2 + 2 * h + j]
-                both = scal_ref[10 + i] * scal_ref[12 + 2 * h + j]
-                delta = (pair - col_ref[...]) - row_ref[...]
-                amp_ref[a, b] = (both * ((2.0 * k - kt) / delta)).astype(BF16)
-                ampt_ref[h, b, a] = (both * ((2.0 * kt - k) / delta)).astype(BF16)
+                piece(source, 2 * place_ref[ys] + lax.rem(zz, 2), zz // 2, half).start()
+    width = 2 * v
+
+    def product(h, step):
+        part = slice(step * width // 4, (step + 1) * width // 4)
+        k_ref[h, part, :] = jnp.dot(left_ref[part, :], held[h], preferred_element_type=F32)
+
+    def amplitude(h, step):
+        i, j = divmod(step, 2)
+        a, b = slice(i * v, (i + 1) * v), slice(j * v, (j + 1) * v)
+        k = k_ref[h, a, b]
+        kt = k.T
+        pair = scal_ref[i] + scal_ref[2 + 2 * h + j]
+        both = scal_ref[10 + i] * scal_ref[12 + 2 * h + j]
+        delta = (pair - col_ref[...]) - row_ref[...]
+        amp_ref[a, b] = (both * ((2.0 * k - kt) / delta)).astype(BF16)
+        ampt_ref[h, b, a] = (both * ((2.0 * kt - k) / delta)).astype(BF16)
+
+    def density(h):
         part = None
         for i in range(2):
             a = slice(i * v, (i + 1) * v)
@@ -104,22 +108,38 @@
         else:
             dens_ref[...] += part
 
+    def gamma(h, n):
+        at = pl.ds(pl.multiple_of(place_ref[20 + n] * rows, rows), 2 * rows)
+        part = scal_ref[8 + h] * jnp.dot(held[h, at, :], ampt_ref[h], preferred_element_type=F32)
+        if h == 0:
+            both_ref[n] = part
+        else:
+            both_ref[n] += part
+
     def leave(n, side):
         core = place_ref[24] if side == 0 else 1 - place_ref[24]
         return pltpu.make_async_copy(
-            both_ref.at[n % 2, pl.ds(pl.multiple_of(core * rows, rows), rows), :],
+            both_ref.at[n, pl.ds(pl.multiple_of(core * rows, rows), rows), :],
             parts[n // 2][side].at[n % 2],
-            out_sem.at[n % 2, side],
+            out_sem.at[n, side],
         )
 
+    for h in range(2):
+        for _ in range(16):
+            piece(sets_a[0].at[0], 0, h, 0).wait()
+        if h == 0:
+            for step in range(4):
+                product(0, step)
+    for step in range(4):
+        product(1, step)
+        amplitude(0, step)
+    density(0)
+    for step in range(4):
+        gamma(0, step)
+        amplitude(1, step)
+    density(1)
     for n in range(4):
-        if n >= 2:
-            leave(n - 2, 0).wait()
-            leave(n - 2, 1).wait()
-        at = pl.ds(pl.multiple_of(place_ref[20 + n] * rows, rows), 2 * rows)
-        both_ref[n % 2] = scal_ref[8] * jnp.dot(
-            held[0, at, :], ampt_ref[0], preferred_element_type=F32
-        ) + scal_ref[9] * jnp.dot(held[1, at, :], ampt_ref[1], preferred_element_type=F32)
+        gamma(1, n)
         leave(n, 1).start()
         leave(n, 0).start()
     chunk = v // 8
@@ -127,7 +147,7 @@
         start = pl.multiple_of(place_ref[12 + n] * chunk, 8)
         out_ref = dens_keep if n < 4 else dens_give
         out_ref[(n % 4) * chunk : (n % 4 + 1) * chunk, :] = dens_ref[pl.ds(start, chunk), :]
-    for n in (2, 3):
+    for n in range(4):
         leave(n, 1).wait()
         leave(n, 0).wait()
 
@@ -166,8 +186,12 @@
             first.append(move(half, near, s))
         first = jnp.stack(first)
         sets.append([first])
-        for s in (1, 2, 3):
+        for s in (1, 3):
             sets[-1].append(move(first, far, s))
+    for (_, left, right), far in zip(sets, "zx"):
+        low = move(left[:2], far, 1)
+        high = move(right[2:], far, 3)
+        sets["zx".index(far)] = [sets["zx".index(far)][0], left, low, right, high]
     sets_a, sets_b = sets
 
     ys = (y - steps) % 4
@@ -217,19 +241,18 @@
     half = jax.ShapeDtypeStruct((v // 2, v), F32)
     keep, give, keep_near, give_near, dens_keep, dens_give = pl.pallas_call(
         pair_kernel,
-        in_specs=[SMEM, SMEM, ANY, vmem, vmem] + [ANY] * 8,
+        in_specs=[SMEM, SMEM, vmem, vmem, vmem] + [ANY] * 10,
         out_specs=[ANY] * 4 + [vmem] * 2,
         out_shape=[part] * 4 + [half] * 2,
         scratch_shapes=[
             pltpu.VMEM((2, 8 * rows, 2 * v), BF16),
-            pltpu.VMEM((2 * v, 8 * rows), BF16),
-            pltpu.VMEM((2 * v, 2 * v), F32),
+            pltpu.VMEM((2, 2 * v, 2 * v), F32),
             pltpu.VMEM((2 * v, 2 * v), BF16),
             pltpu.VMEM((2, 2 * v, 2 * v), BF16),
             pltpu.VMEM((v, v), F32),
-            pltpu.VMEM((2, 2 * rows, 2 * v), F32),
-            pltpu.SemaphoreType.DMA((3,)),
-            pltpu.SemaphoreType.DMA((2, 2)),
+            pltpu.VMEM((4, 2 * rows, 2 * v), F32),
+            pltpu.SemaphoreType.DMA((2,)),
+            pltpu.SemaphoreType.DMA((4, 2)),
         ],
         compiler_params=pltpu.CompilerParams(vmem_limit_bytes=36 * 2**20),
         cost_estimate=pl.CostEstimate(

time: 199 us -> 204 us (1.025)
  starting transfers between devices: 56.4 us -> 61.7 us
    slice x0 -> x4, local copies, waits for them, and re-layouts: none -> 7.35 us  [the longest x2 3.69 us: local(): low = move(left[:2], far, 1)]
    unnamed x41 -> x35, local copies, waits for them, and re-layouts: 9.2 us -> 1.97 us
    ppermute x18 -> x20, starting transfers between devices: 49.4 us -> 53.3 us  [move(): return lax.ppermute(x, axis, [(i, (i + s) % n) for i in range(n)])]
    ppermute x18 -> x20, waiting for transfers between devices: 47.3 us -> 50.6 us  [move(): return lax.ppermute(x, axis, [(i, (i + s) % n) for i in range(n)])]
    pallas_call x1, Pallas kernels: 22 us -> 19.6 us  [local(): pl.pallas_call(pair_kernel, in_specs=[SMEM, SMEM, vmem, vmem, vmem] + [AN...]
  transfers between devices with their start and end apart: 36 -> 38, of which waited for: 20 -> 23; matrix products, arithmetic and copies ran while one was open for 7% -> 10% of each run, Pallas kernels for 2% -> 2%
where the time goes in v4:
time: 204 us; the launch traced here: 203 us
  waiting for transfers between devices  92.5 us (45%)
  starting transfers between devices  61.7 us (30%)
  Pallas kernels  24.5 us (12%)
  local copies, waits for them, and re-layouts  16.1 us (8%)
  other arithmetic  7.31 us (4%)
    ppermute x20, starting transfers between devices, move(): return lax.ppermute(x, axis, [(i, (i + s) % n) for i in range(n)])  53.3 us
    ppermute x20, waiting for transfers between devices, move(): return lax.ppermute(x, axis, [(i, (i + s) % n) for i in range(n)])  50.6 us
    ppermute x8, waiting for transfers between devices, swap_bits(): lax.ppermute(x, axis, [(i, i ^ bits) for i in range(lax.axis_size(axis))])  36.8 us
    pallas_call x1, Pallas kernels, local(): pl.pallas_call(pair_kernel, in_specs=[SMEM, SMEM, vmem, vmem, vmem] + [AN...  19.6 us
    ppermute x8, starting transfers between devices, swap_bits(): lax.ppermute(x, axis, [(i, i ^ bits) for i in range(lax.axis_size(axis))])  5.23 us
    ppermute x8, waiting for transfers between devices, swap(): return lax.ppermute(x, 'c', [(0, 1), (1, 0)])  5.09 us
  transfers between devices with their start and end apart: 38, of which 23 were waited for; matrix products, arithmetic and copies ran while one was open for 10% of the time, Pallas kernels for 2%

profile of v4, /device:TPU:0, one launch (start us, length us, event | category | flops | bytes accessed | tf_op | source)
XLA Modules:
  0.0 203.1 jit_solution(15461556718047573865)
XLA Ops:
  1.8 3.2 %collective-permute-start.2 = (bf16[2,288,384]{2,1,0:T(8,128)(2,1)S(1)}, bf16[2,288,384]{2,1,0:T(8,128)(2,1)S(1)}, u32[]{:S(2)}, u32[]{:S(2)}) collective-permute-start(bf16[2,288,384]{2,1,0:T(8,128)(2,1)S(1)} %bitcast.39), channel_id=1, source_target_pairs={{0,6},{2,0},{4,2},{6,4},{1,7},{3,1},{5,3},{7,5},{8,14},{10,8},{12,... | collective-permute-start | bytes 1327112 | tf_op jit(solution)/shard_map/ppermute | solution.py:21
  7.9 18.8 %collective-permute-start.10 = (bf16[288,384]{1,0:T(8,128)(2,1)S(1)}, bf16[288,384]{1,0:T(8,128)(2,1)S(1)}, u32[]{:S(2)}, u32[]{:S(2)}) collective-permute-start(bf16[288,384]{1,0:T(8,128)(2,1)S(1)} %collective-permute-done.7), channel_id=1, source_target_pairs={{0,24},{8,0},{16,8},{24,16},{1,25},{9,1},{17,9},{25,17},{2,26},{10... | collective-permute-start | bytes 663560 | tf_op jit(solution)/shard_map/ppermute | solution.py:21
  27.5 4.7 %collective-permute-start.18 = (bf16[288,384]{1,0:T(8,128)(2,1)S(1)}, bf16[288,384]{1,0:T(8,128)(2,1)S(1)}, u32[]{:S(2)}, u32[]{:S(2)}) collective-permute-start(bf16[288,384]{1,0:T(8,128)(2,1)S(1)} %collective-permute-done.15), channel_id=1, source_target_pairs={{0,96},{32,0},{64,32},{96,64},{1,97},{33,1},{65,33},{97,65},{2,98}... | collective-permute-start | bytes 663560 | tf_op jit(solution)/shard_map/ppermute | solution.py:21
  36.5 3.9 %collective-permute-start.17 = (bf16[288,384]{1,0:T(8,128)(2,1)S(1)}, bf16[288,384]{1,0:T(8,128)(2,1)S(1)}, u32[]{:S(2)}, u32[]{:S(2)}) collective-permute-start(bf16[288,384]{1,0:T(8,128)(2,1)S(1)} %collective-permute-done.15), channel_id=1, source_target_pairs={{0,64},{32,96},{64,0},{96,32},{1,65},{33,97},{65,1},{97,33},{2,66}... | collective-permute-start | bytes 663560 | tf_op jit(solution)/shard_map/ppermute | solution.py:21
  47.2 22.7 %collective-permute-done.16 = bf16[288,384]{1,0:T(8,128)(2,1)S(1)} collective-permute-done((bf16[288,384]{1,0:T(8,128)(2,1)S(1)}, bf16[288,384]{1,0:T(8,128)(2,1)S(1)}, u32[]{:S(2)}, u32[]{:S(2)}) %collective-permute-start.16) | collective-permute-done | bytes 221216 | tf_op jit(solution)/shard_map/ppermute | solution.py:21
  69.8 4.7 %collective-permute-start = (bf16[2,288,384]{2,1,0:T(8,128)(2,1)S(1)}, bf16[2,288,384]{2,1,0:T(8,128)(2,1)S(1)}, u32[]{:S(2)}, u32[]{:S(2)}) collective-permute-start(bf16[2,288,384]{2,1,0:T(8,128)(2,1)S(1)} %bitcast.42), channel_id=1, source_target_pairs={{0,2},{2,4},{4,6},{6,0},{1,3},{3,5},{5,7},{7,1},{8,10},{10,12},{12... | collective-permute-start | bytes 1327112 | tf_op jit(solution)/shard_map/ppermute | solution.py:21
  75.8 3.8 %collective-permute-start.21 = (bf16[4,288,384]{2,1,0:T(8,128)(2,1)S(1)}, bf16[4,288,384]{2,1,0:T(8,128)(2,1)}, u32[]{:S(2)}, u32[]{:S(2)}) collective-permute-start(bf16[4,288,384]{2,1,0:T(8,128)(2,1)S(1)} %pad_maximum_fusion.1.refs_5_), channel_id=1, source_target_pairs={{0,24},{8,0},{16,8},{24,16},{1,25},{9,1},{17,9},{25,17},{2,26},{10... | collective-permute-start | bytes 2654216 | tf_op jit(solution)/shard_map/ppermute | solution.py:21
  92.5 5.6 %collective-permute-done.21.refs_8_ = bf16[4,288,384]{2,1,0:T(8,128)(2,1)} collective-permute-done((bf16[4,288,384]{2,1,0:T(8,128)(2,1)S(1)}, bf16[4,288,384]{2,1,0:T(8,128)(2,1)}, u32[]{:S(2)}, u32[]{:S(2)}) %collective-permute-start.21) | collective-permute-done | bytes 884768 | tf_op jit(solution)/shard_map/ppermute | solution.py:21
  109.0 3.5 %turn.1.left_ref = bf16[768,2304]{1,0:T(8,128)(2,1)S(1)} custom-call(s32[8]{0:T(128)S(1)} %pad_add_fusion.slot_ref, bf16[2,288,384]{2,1,0:T(8,128)(2,1)S(1)} %bitcast.44, bf16[2,288,384]{2,1,0:T(8,128)(2,1)S(1)} %collective-permute-done.refs_1_, bf16[2,288,384]{2,1,0:T(8,128)(2,1)S(1)} %collective-permute-done.1.refs_2_, ...), custom_call_target="tpu_custom_call" | custom-call | bytes 7000000 | tf_op jit(solution)/shard_map/turn/pallas_call | solution.py:229
  112.8 3.9 %collective-permute-done.12.refs_2_ = bf16[2,288,384]{2,1,0:T(8,128)(2,1)} collective-permute-done((bf16[2,288,384]{2,1,0:T(8,128)(2,1)}, bf16[2,288,384]{2,1,0:T(8,128)(2,1)}, u32[]{:S(2)}, u32[]{:S(2)}) %collective-permute-start.12) | collective-permute-done | bytes 442400 | tf_op jit(solution)/shard_map/ppermute | solution.py:21
  117.4 3.4 %collective-permute-done.20.refs_7_ = bf16[2,288,384]{2,1,0:T(8,128)(2,1)} collective-permute-done((bf16[2,288,384]{2,1,0:T(8,128)(2,1)}, bf16[2,288,384]{2,1,0:T(8,128)(2,1)}, u32[]{:S(2)}, u32[]{:S(2)}) %collective-permute-start.20) | collective-permute-done | bytes 442400 | tf_op jit(solution)/shard_map/ppermute | solution.py:21
  120.9 19.6 %pairs.1 = (f32[2,288,768]{2,1,0:T(8,128)S(1)}, f32[2,288,768]{2,1,0:T(8,128)S(1)}, f32[2,288,768]{2,1,0:T(8,128)S(1)}, f32[2,288,768]{2,1,0:T(8,128)S(1)}, f32[...) custom-call(s32[25]{0:T(128)S(1)} %concatenate.16.place_ref, f32[16]{0:T(128)S(1)} %concatenate.17.scal_ref, ...), custom_call_target="tpu_custom_call" | custom-call | flops 11800000512 | bytes 18000000 | tf_op jit(solution)/shard_map/pairs/pallas_call | solution.py:242
  141.1 3.5 %collective-permute-done.28 = f32[192,384]{1,0:T(8,128)S(1)} collective-permute-done((f32[192,384]{1,0:T(8,128)S(1)}, f32[192,384]{1,0:T(8,128)S(1)}, u32[]{:S(2)}, u32[]{:S(2)}) %collective-permute-start.28) | collective-permute-done | bytes 294944 | tf_op jit(solution)/shard_map/ppermute | solution.py:25
  144.8 7.1 %collective-permute-done.29 = f32[96,384]{1,0:T(8,128)S(1)} collective-permute-done((f32[96,384]{1,0:T(8,128)S(1)}, f32[96,384]{1,0:T(8,128)S(1)}, u32[]{:S(2)}, u32[]{:S(2)}) %collective-permute-start.29) | collective-permute-done | bytes 147488 | tf_op jit(solution)/shard_map/ppermute | solution.py:164
  152.0 4.3 %collective-permute-done.30 = f32[48,384]{1,0:T(8,128)S(1)} collective-permute-done((f32[48,384]{1,0:T(8,128)S(1)}, f32[48,384]{1,0:T(8,128)S(1)}, u32[]{:S(2)}, u32[]{:S(2)}) %collective-permute-start.30) | collective-permute-done | bytes 73760 | tf_op jit(solution)/shard_map/ppermute | solution.py:164
  156.5 4.3 %collective-permute-done.31 = f32[48,384]{1,0:T(8,128)S(1)} collective-permute-done((f32[48,384]{1,0:T(8,128)S(1)}, f32[48,384]{1,0:T(8,128)S(1)}, u32[]{:S(2)}, u32[]{:S(2)}) %collective-permute-start.31) | collective-permute-done | bytes 73760 | tf_op jit(solution)/shard_map/ppermute | solution.py:164
  161.2 5.3 %collective-permute-done.32 = f32[48,384]{1,0:T(8,128)S(1)} collective-permute-done((f32[48,384]{1,0:T(8,128)S(1)}, f32[48,384]{1,0:T(8,128)S(1)}, u32[]{:S(2)}, u32[]{:S(2)}) %collective-permute-start.32) | collective-permute-done | bytes 73760 | tf_op jit(solution)/shard_map/ppermute | solution.py:164
  168.2 2.8 %collective-permute-done.33 = f32[48,384]{1,0:T(8,128)S(1)} collective-permute-done((f32[48,384]{1,0:T(8,128)S(1)}, f32[48,384]{1,0:T(8,128)S(1)}, u32[]{:S(2)}, u32[]{:S(2)}) %collective-permute-start.33) | collective-permute-done | bytes 73760 | tf_op jit(solution)/shard_map/ppermute | solution.py:164
  173.4 3.2 %collective-permute-done.34 = f32[48,384]{1,0:T(8,128)S(1)} collective-permute-done((f32[48,384]{1,0:T(8,128)S(1)}, f32[48,384]{1,0:T(8,128)S(1)}, u32[]{:S(2)}, u32[]{:S(2)}) %collective-permute-start.34) | collective-permute-done | bytes 73760 | tf_op jit(solution)/shard_map/ppermute | solution.py:164
  176.7 5.1 %collective-permute-done.35 = f32[48,384]{1,0:T(8,128)S(1)} collective-permute-done((f32[48,384]{1,0:T(8,128)S(1)}, f32[48,384]{1,0:T(8,128)S(1)}, u32[]{:S(2)}, u32[]{:S(2)}) %collective-permute-start.35) | collective-permute-done | bytes 73760 | tf_op jit(solution)/shard_map/ppermute | solution.py:164
  182.3 3.0 %collective-permute-start.26 = (bf16[288,768]{1,0:T(8,128)(2,1)S(1)}, bf16[288,768]{1,0:T(8,128)(2,1)S(1)}, u32[]{:S(2)}, u32[]{:S(2)}) collective-permute-start(bf16[288,768]{1,0:T(8,128)(2,1)S(1)} %fusion.8), channel_id=1, source_target_pairs={{0,6},{2,0},{4,2},{6,4},{1,7},{3,1},{5,3},{7,5},{8,14},{10,8},{12,... | collective-permute-start | bytes 1327112 | tf_op jit(solution)/shard_map/ppermute | solution.py:21
  187.2 4.7 %collective-permute-done.36 = f32[96,384]{1,0:T(8,128)S(1)} collective-permute-done((f32[96,384]{1,0:T(8,128)S(1)}, f32[96,384]{1,0:T(8,128)S(1)}, u32[]{:S(2)}, u32[]{:S(2)}) %collective-permute-start.36) | collective-permute-done | bytes 147488 | tf_op jit(solution)/shard_map/ppermute | solution.py:164
  195.0 2.6 %collective-permute-done.26 = bf16[288,768]{1,0:T(8,128)(2,1)S(1)} collective-permute-done((bf16[288,768]{1,0:T(8,128)(2,1)S(1)}, bf16[288,768]{1,0:T(8,128)(2,1)S(1)}, u32[]{:S(2)}, u32[]{:S(2)}) %collective-permute-start.26) | collective-permute-done | bytes 442400 | tf_op jit(solution)/shard_map/ppermute | solution.py:21
  197.6 3.8 %collective-permute-done.25 = bf16[288,768]{1,0:T(8,128)(2,1)S(1)} collective-permute-done((bf16[288,768]{1,0:T(8,128)(2,1)S(1)}, bf16[288,768]{1,0:T(8,128)(2,1)S(1)}, u32[]{:S(2)}, u32[]{:S(2)}) %collective-permute-start.25) | collective-permute-done | bytes 442400 | tf_op jit(solution)/shard_map/ppermute | solution.py:21
  (137 shorter events, 54.7 us)
Async XLA Ops:
  1.8 74.0 %collective-permute-start.2 = (bf16[2,288,384]{2,1,0:T(8,128)(2,1)S(1)}, bf16[2,288,384]{2,1,0:T(8,128)(2,1)S(1)}, u32[]{:S(2)}, u32[]{:S(2)}) collective-permute-start(bf16[2,288,384]{2,1,0:T(8,128)(2,1)S(1)} %bitcast.39), channel_id=1, source_target_pairs={{0,6},{2,0},{4,2},{6,4},{1,7},{3,1},{5,3},{7,5},{8,14},{10,8},{12,... | collective-permute-start | bytes 1327112 | tf_op jit(solution)/shard_map/ppermute | solution.py:21
  5.0 22.5 %collective-permute-start.15 = (bf16[288,384]{1,0:T(8,128)(2,1)S(1)}, bf16[288,384]{1,0:T(8,128)(2,1)S(1)}, u32[]{:S(2)}, u32[]{:S(2)}) collective-permute-start(bf16[288,384]{1,0:T(8,128)(2,1)S(1)} %get-tuple-element.18), channel_id=1, source_target_pairs={{0,0},{1,32},{2,24},{3,56},{4,16},{5,48},{6,8},{7,40},{8,10},{9,42... | collective-permute-start | bytes 663560 | tf_op jit(solution)/shard_map/ppermute | solution.py:175
  7.9 27.3 %collective-permute-start.10 = (bf16[288,384]{1,0:T(8,128)(2,1)S(1)}, bf16[288,384]{1,0:T(8,128)(2,1)S(1)}, u32[]{:S(2)}, u32[]{:S(2)}) collective-permute-start(bf16[288,384]{1,0:T(8,128)(2,1)S(1)} %collective-permute-done.7), channel_id=1, source_target_pairs={{0,24},{8,0},{16,8},{24,16},{1,25},{9,1},{17,9},{25,17},{2,26},{10... | collective-permute-start | bytes 663560 | tf_op jit(solution)/shard_map/ppermute | solution.py:21
  26.6 13.7 %collective-permute-start.8 = (bf16[288,384]{1,0:T(8,128)(2,1)S(1)}, bf16[288,384]{1,0:T(8,128)(2,1)S(1)}, u32[]{:S(2)}, u32[]{:S(2)}) collective-permute-start(bf16[288,384]{1,0:T(8,128)(2,1)S(1)} %collective-permute-done.7), channel_id=1, source_target_pairs={{0,8},{8,16},{16,24},{24,0},{1,9},{9,17},{17,25},{25,1},{2,10},{10... | collective-permute-start | bytes 663560 | tf_op jit(solution)/shard_map/ppermute | solution.py:21
  27.5 15.3 %collective-permute-start.18 = (bf16[288,384]{1,0:T(8,128)(2,1)S(1)}, bf16[288,384]{1,0:T(8,128)(2,1)S(1)}, u32[]{:S(2)}, u32[]{:S(2)}) collective-permute-start(bf16[288,384]{1,0:T(8,128)(2,1)S(1)} %collective-permute-done.15), channel_id=1, source_target_pairs={{0,96},{32,0},{64,32},{96,64},{1,97},{33,1},{65,33},{97,65},{2,98}... | collective-permute-start | bytes 663560 | tf_op jit(solution)/shard_map/ppermute | solution.py:21
  35.2 44.3 %collective-permute-start.1 = (bf16[2,288,384]{2,1,0:T(8,128)(2,1)S(1)}, bf16[2,288,384]{2,1,0:T(8,128)(2,1)S(1)}, u32[]{:S(2)}, u32[]{:S(2)}) collective-permute-start(bf16[2,288,384]{2,1,0:T(8,128)(2,1)S(1)} %bitcast.41), channel_id=1, source_target_pairs={{0,4},{2,6},{4,0},{6,2},{1,5},{3,7},{5,1},{7,3},{8,12},{10,14},{12... | collective-permute-start | bytes 1327112 | tf_op jit(solution)/shard_map/ppermute | solution.py:21
  40.5 43.4 %collective-permute-start.13 = (bf16[4,288,384]{2,1,0:T(8,128)(2,1)S(1)}, bf16[4,288,384]{2,1,0:T(8,128)(2,1)S(1)}, u32[]{:S(2)}, u32[]{:S(2)}) collective-permute-start(bf16[4,288,384]{2,1,0:T(8,128)(2,1)S(1)} %pad_maximum_fusion.refs_0_), channel_id=1, source_target_pairs={{0,96},{32,0},{64,32},{96,64},{1,97},{33,1},{65,33},{97,65},{2,98}... | collective-permute-start | bytes 2654216 | tf_op jit(solution)/shard_map/ppermute | solution.py:21
  42.9 41.5 %collective-permute-start.11 = (bf16[4,288,384]{2,1,0:T(8,128)(2,1)S(1)}, bf16[4,288,384]{2,1,0:T(8,128)(2,1)S(1)}, u32[]{:S(2)}, u32[]{:S(2)}) collective-permute-start(bf16[4,288,384]{2,1,0:T(8,128)(2,1)S(1)} %pad_maximum_fusion.refs_0_), channel_id=1, source_target_pairs={{0,32},{32,64},{64,96},{96,0},{1,33},{33,65},{65,97},{97,1},{2,34}... | collective-permute-start | bytes 2654216 | tf_op jit(solution)/shard_map/ppermute | solution.py:21
  44.8 25.0 %collective-permute-start.16 = (bf16[288,384]{1,0:T(8,128)(2,1)S(1)}, bf16[288,384]{1,0:T(8,128)(2,1)S(1)}, u32[]{:S(2)}, u32[]{:S(2)}) collective-permute-start(bf16[288,384]{1,0:T(8,128)(2,1)S(1)} %collective-permute-done.15), channel_id=1, source_target_pairs={{0,32},{32,64},{64,96},{96,0},{1,33},{33,65},{65,97},{97,1},{2,34}... | collective-permute-start | bytes 663560 | tf_op jit(solution)/shard_map/ppermute | solution.py:21
  69.8 14.1 %collective-permute-start = (bf16[2,288,384]{2,1,0:T(8,128)(2,1)S(1)}, bf16[2,288,384]{2,1,0:T(8,128)(2,1)S(1)}, u32[]{:S(2)}, u32[]{:S(2)}) collective-permute-start(bf16[2,288,384]{2,1,0:T(8,128)(2,1)S(1)} %bitcast.42), channel_id=1, source_target_pairs={{0,2},{2,4},{4,6},{6,0},{1,3},{3,5},{5,7},{7,1},{8,10},{10,12},{12... | collective-permute-start | bytes 1327112 | tf_op jit(solution)/shard_map/ppermute | solution.py:21
  75.8 22.3 %collective-permute-start.21 = (bf16[4,288,384]{2,1,0:T(8,128)(2,1)S(1)}, bf16[4,288,384]{2,1,0:T(8,128)(2,1)}, u32[]{:S(2)}, u32[]{:S(2)}) collective-permute-start(bf16[4,288,384]{2,1,0:T(8,128)(2,1)S(1)} %pad_maximum_fusion.1.refs_5_), channel_id=1, source_target_pairs={{0,24},{8,0},{16,8},{24,16},{1,25},{9,1},{17,9},{25,17},{2,26},{10... | collective-permute-start | bytes 2654216 | tf_op jit(solution)/shard_map/ppermute | solution.py:21
  79.5 22.1 %collective-permute-start.19 = (bf16[4,288,384]{2,1,0:T(8,128)(2,1)S(1)}, bf16[4,288,384]{2,1,0:T(8,128)(2,1)}, u32[]{:S(2)}, u32[]{:S(2)}) collective-permute-start(bf16[4,288,384]{2,1,0:T(8,128)(2,1)S(1)} %pad_maximum_fusion.1.refs_5_), channel_id=1, source_target_pairs={{0,8},{8,16},{16,24},{24,0},{1,9},{9,17},{17,25},{25,1},{2,10},{10... | collective-permute-start | bytes 2654216 | tf_op jit(solution)/shard_map/ppermute | solution.py:21
  83.9 19.6 %collective-permute-start.3 = (bf16[2,288,384]{2,1,0:T(8,128)(2,1)S(1)}, bf16[2,288,384]{2,1,0:T(8,128)(2,1)}, u32[]{:S(2)}, u32[]{:S(2)}) collective-permute-start(bf16[2,288,384]{2,1,0:T(8,128)(2,1)S(1)} %bitcast.43), channel_id=1, source_target_pairs={{0,1},{1,0},{2,3},{3,2},{4,5},{5,4},{6,7},{7,6},{8,9},{9,8},{10,11... | collective-permute-start | bytes 1327112 | tf_op jit(solution)/shard_map/ppermute | solution.py:25
  83.9 21.6 %collective-permute-start.6 = (bf16[2,288,384]{2,1,0:T(8,128)(2,1)S(1)}, bf16[2,288,384]{2,1,0:T(8,128)(2,1)}, u32[]{:S(2)}, u32[]{:S(2)}) collective-permute-start(bf16[2,288,384]{2,1,0:T(8,128)(2,1)S(1)} %collective-permute-done.2.refs_3_), channel_id=1, source_target_pairs={{0,1},{1,0},{2,3},{3,2},{4,5},{5,4},{6,7},{7,6},{8,9},{9,8},{10,11... | collective-permute-start | bytes 1327112 | tf_op jit(solution)/shard_map/ppermute | solution.py:25
  84.8 22.8 %collective-permute-start.5 = (bf16[2,288,384]{2,1,0:T(8,128)(2,1)S(1)}, bf16[2,288,384]{2,1,0:T(8,128)(2,1)}, u32[]{:S(2)}, u32[]{:S(2)}) collective-permute-start(bf16[2,288,384]{2,1,0:T(8,128)(2,1)S(1)} %collective-permute-done.1.refs_2_), channel_id=1, source_target_pairs={{0,1},{1,0},{2,3},{3,2},{4,5},{5,4},{6,7},{7,6},{8,9},{9,8},{10,11... | collective-permute-start | bytes 1327112 | tf_op jit(solution)/shard_map/ppermute | solution.py:25
  101.6 11.2 %collective-permute-start.14 = (bf16[2,288,384]{2,1,0:T(8,128)(2,1)}, bf16[2,288,384]{2,1,0:T(8,128)(2,1)}, u32[]{:S(2)}, u32[]{:S(2)}) collective-permute-start(bf16[2,288,384]{2,1,0:T(8,128)(2,1)} %slice.62), channel_id=1, source_target_pairs={{0,96},{32,0},{64,32},{96,64},{1,97},{33,1},{65,33},{97,65},{2,98}... | collective-permute-start | bytes 1327112 | tf_op jit(solution)/shard_map/ppermute | solution.py:21
  103.5 13.3 %collective-permute-start.12 = (bf16[2,288,384]{2,1,0:T(8,128)(2,1)}, bf16[2,288,384]{2,1,0:T(8,128)(2,1)}, u32[]{:S(2)}, u32[]{:S(2)}) collective-permute-start(bf16[2,288,384]{2,1,0:T(8,128)(2,1)} %slice.61), channel_id=1, source_target_pairs={{0,32},{32,64},{64,96},{96,0},{1,33},{33,65},{65,97},{97,1},{2,34}... | collective-permute-start | bytes 1327112 | tf_op jit(solution)/shard_map/ppermute | solution.py:21
  105.5 12.0 %collective-permute-start.22 = (bf16[2,288,384]{2,1,0:T(8,128)(2,1)}, bf16[2,288,384]{2,1,0:T(8,128)(2,1)}, u32[]{:S(2)}, u32[]{:S(2)}) collective-permute-start(bf16[2,288,384]{2,1,0:T(8,128)(2,1)} %slice.65), channel_id=1, source_target_pairs={{0,24},{8,0},{16,8},{24,16},{1,25},{9,1},{17,9},{25,17},{2,26},{10... | collective-permute-start | bytes 1327112 | tf_op jit(solution)/shard_map/ppermute | solution.py:21
  107.6 13.3 %collective-permute-start.20 = (bf16[2,288,384]{2,1,0:T(8,128)(2,1)}, bf16[2,288,384]{2,1,0:T(8,128)(2,1)}, u32[]{:S(2)}, u32[]{:S(2)}) collective-permute-start(bf16[2,288,384]{2,1,0:T(8,128)(2,1)} %slice.64), channel_id=1, source_target_pairs={{0,8},{8,16},{16,24},{24,0},{1,9},{9,17},{17,25},{25,1},{2,10},{10... | collective-permute-start | bytes 1327112 | tf_op jit(solution)/shard_map/ppermute | solution.py:21
  140.5 41.7 %collective-permute-start.23 = (f32[2,288,768]{2,1,0:T(8,128)S(1)}, f32[2,288,768]{2,1,0:T(8,128)S(1)}, u32[]{:S(2)}, u32[]{:S(2)}) collective-permute-start(f32[2,288,768]{2,1,0:T(8,128)S(1)} %get-tuple-element.9), channel_id=1, source_target_pairs={{0,1},{1,0},{2,3},{3,2},{4,5},{5,4},{6,7},{7,6},{8,9},{9,8},{10,11... | collective-permute-start | bytes 5308424 | tf_op jit(solution)/shard_map/ppermute | solution.py:25
  141.1 44.3 %collective-permute-start.24 = (f32[2,288,768]{2,1,0:T(8,128)S(1)}, f32[2,288,768]{2,1,0:T(8,128)S(1)}, u32[]{:S(2)}, u32[]{:S(2)}) collective-permute-start(f32[2,288,768]{2,1,0:T(8,128)S(1)} %get-tuple-element.11), channel_id=1, source_target_pairs={{0,1},{1,0},{2,3},{3,2},{4,5},{5,4},{6,7},{7,6},{8,9},{9,8},{10,11... | collective-permute-start | bytes 5308424 | tf_op jit(solution)/shard_map/ppermute | solution.py:25
  182.3 15.3 %collective-permute-start.26 = (bf16[288,768]{1,0:T(8,128)(2,1)S(1)}, bf16[288,768]{1,0:T(8,128)(2,1)S(1)}, u32[]{:S(2)}, u32[]{:S(2)}) collective-permute-start(bf16[288,768]{1,0:T(8,128)(2,1)S(1)} %fusion.8), channel_id=1, source_target_pairs={{0,6},{2,0},{4,2},{6,4},{1,7},{3,1},{5,3},{7,5},{8,14},{10,8},{12,... | collective-permute-start | bytes 1327112 | tf_op jit(solution)/shard_map/ppermute | solution.py:21
  185.7 15.7 %collective-permute-start.25 = (bf16[288,768]{1,0:T(8,128)(2,1)S(1)}, bf16[288,768]{1,0:T(8,128)(2,1)S(1)}, u32[]{:S(2)}, u32[]{:S(2)}) collective-permute-start(bf16[288,768]{1,0:T(8,128)(2,1)S(1)} %get-tuple-element.16), channel_id=1, source_target_pairs={{0,2},{2,4},{4,6},{6,0},{1,3},{3,5},{5,7},{7,1},{8,10},{10,12},{12... | collective-permute-start | bytes 1327112 | tf_op jit(solution)/shard_map/ppermute | solution.py:21
  185.8 15.7 %collective-permute-start.27 = (bf16[288,768]{1,0:T(8,128)(2,1)S(1)}, bf16[288,768]{1,0:T(8,128)(2,1)S(1)}, u32[]{:S(2)}, u32[]{:S(2)}) collective-permute-start(bf16[288,768]{1,0:T(8,128)(2,1)S(1)} %get-tuple-element.17), channel_id=1, source_target_pairs={{0,4},{2,6},{4,0},{6,2},{1,5},{3,7},{5,1},{7,3},{8,12},{10,14},{12... | collective-permute-start | bytes 1327112 | tf_op jit(solution)/shard_map/ppermute | solution.py:21
  (31 other events, 437.9 us)

commit v5 on v4

--- a/solution.py
+++ b/solution.py
@@ -56,14 +56,14 @@
 
 
 def pair_kernel(place_ref, scal_ref, left_ref, row_ref, col_ref, *refs):
-    sets_a, sets_b = refs[0:5], refs[5:10]
-    parts = (refs[10:12], refs[12:14])
-    dens_keep, dens_give = refs[14:16]
-    held, k_ref, amp_ref, ampt_ref, dens_ref, both_ref, sem, out_sem = refs[16:]
+    sets_a, sets_b = refs[0:8], refs[8:16]
+    parts = (refs[16:18], refs[18:20])
+    dens_keep, dens_give = refs[20:22]
+    held, k_ref, amp_ref, ampt_ref, dens_ref, both_ref, sem, out_sem = refs[22:]
     rows, v = sets_a[0].shape[1:]
 
     def at(sets, s, t):
-        return sets[s].at[t] if s != 2 else sets[2 if t < 2 else 4].at[t % 2]
+        return sets[2 * s + t // 2].at[t % 2]
 
     def piece(source, slot, h, half):
         at = pl.ds(pl.multiple_of(slot * rows, rows), rows)
@@ -71,14 +71,20 @@
             source, held.at[h, at, half * v : (half + 1) * v], sem.at[h]
         )
 
-    for s in range(4):
-        for t in range(4):
-            for source, zs, ys, half in (
-                (at(sets_a, s, t), s, 4 + t, 0),
-                (at(sets_b, s, t), t, 8 + s, 1),
-            ):
-                zz = place_ref[zs]
-                piece(source, 2 * place_ref[ys] + lax.rem(zz, 2), zz // 2, half).start()
+    for h in range(2):
+        for n in range(4):
+            zz = place_ref[n]
+
+            @pl.when(zz // 2 == h)
+            def _():
+                for m in range(4):
+                    for source, ys, half in (
+                        (at(sets_a, n, m), 4 + m, 0),
+                        (at(sets_b, m, n), 8 + m, 1),
+                    ):
+                        slot = 2 * place_ref[ys] + lax.rem(zz, 2)
+                        piece(source, slot, h, half).start()
+
     width = 2 * v
 
     def product(h, step):
@@ -152,12 +158,12 @@
         leave(n, 0).wait()
 
 
-def place_kernel(place_ref, mine_ref, other_ref, out_ref):
+def place_kernel(place_ref, *refs):
+    *parts, out_ref = refs
     chunk = out_ref.shape[0] // 8
     for n in range(8):
-        ref = mine_ref if n < 4 else other_ref
         start = pl.multiple_of(place_ref[12 + n] * chunk, 8)
-        out_ref[pl.ds(start, chunk), :] = ref[(n % 4) * chunk : (n % 4 + 1) * chunk, :]
+        out_ref[pl.ds(start, chunk), :] = parts[n][...]
 
 
 def swap_bits(x, axis, bits):
@@ -184,14 +190,18 @@
         first = [half]
         for s in (1, 2, 3):
             first.append(move(half, near, s))
-        first = jnp.stack(first)
-        sets.append([first])
-        for s in (1, 3):
-            sets[-1].append(move(first, far, s))
-    for (_, left, right), far in zip(sets, "zx"):
-        low = move(left[:2], far, 1)
-        high = move(right[2:], far, 3)
-        sets["zx".index(far)] = [sets["zx".index(far)][0], left, low, right, high]
+        low, high = jnp.stack(first[:2]), jnp.stack(first[2:])
+
+        def sent(half, s):
+            return move(half, far, s)
+
+        low_left = sent(low, 1)
+        high_right = sent(high, 3)
+        high_left = sent(high, 1)
+        low_right = sent(low, 3)
+        low_far = sent(low_left, 1)
+        high_far = sent(high_right, 3)
+        sets.append([low, high, low_left, high_left, low_far, high_far, low_right, high_right])
     sets_a, sets_b = sets
 
     ys = (y - steps) % 4
@@ -241,7 +251,7 @@
     half = jax.ShapeDtypeStruct((v // 2, v), F32)
     keep, give, keep_near, give_near, dens_keep, dens_give = pl.pallas_call(
         pair_kernel,
-        in_specs=[SMEM, SMEM, vmem, vmem, vmem] + [ANY] * 10,
+        in_specs=[SMEM, SMEM, vmem, vmem, vmem] + [ANY] * 16,
         out_specs=[ANY] * 4 + [vmem] * 2,
         out_shape=[part] * 4 + [half] * 2,
         scratch_shapes=[
@@ -274,27 +284,28 @@
     gamma = gamma + next_one.astype(F32) + last_one.astype(F32) + far.astype(F32)
     gamma_out = gamma.reshape(rows, orbitals, v)
 
-    for bits in (3, 1):
-        mine, sent = jnp.split(own, 2)
-        got = swap_bits(sent, "y", bits)
-        own = mine + got
+    mine, *others = jnp.split(own, 4)
+    others = dict(zip((1, 3, 2), others))
+    for bits in (2, 3, 1):
+        others[bits] = swap_bits(others[bits], "y", bits)
+    own = (mine + others[1]) + (others[2] + others[3])
     for axis in ("x", "z"):
         for bits in (1, 3):
             got = swap_bits(own, axis, bits)
             own = own + got
     own = own / task_iblock.shape[0]
-    for bits in (1, 3):
-        got = swap_bits(own, "y", bits)
-        own = jnp.concatenate([own, got])
-    got = swap(own)
+    chunks_of = [own]
+    for bits in (2, 3, 1):
+        chunks_of.insert(1, swap_bits(own, "y", bits))
+    parts = chunks_of + [swap(part) for part in chunks_of]
     density = pl.pallas_call(
         place_kernel,
-        in_specs=[SMEM, vmem, vmem],
+        in_specs=[SMEM] + [vmem] * 8,
         out_specs=vmem,
         out_shape=jax.ShapeDtypeStruct((v, v), F32),
         compiler_params=pltpu.CompilerParams(vmem_limit_bytes=4 * 2**20),
         name="place",
-    )(place, own, got)
+    )(place, *parts)
     return gamma_out, density
 
 

time: 204 us -> 184 us (0.902)
  the two profiles are of different devices: /device:TPU:0 before, /device:TPU:1 now
where the time goes in v5:
time: 184 us
  starting transfers between devices  78.4 us (43%)
  waiting for transfers between devices  64.3 us (35%)
  Pallas kernels  22.6 us (12%)
  local copies, waits for them, and re-layouts  11 us (6%)
  other arithmetic  6.54 us (4%)
    ppermute x24, starting transfers between devices, move(): return lax.ppermute(x, axis, [(i, (i + s) % n) for i in range(n)])  38.1 us
    ppermute x24, waiting for transfers between devices, move(): return lax.ppermute(x, axis, [(i, (i + s) % n) for i in range(n)])  36.8 us
    ppermute x11, starting transfers between devices, swap(): return lax.ppermute(x, 'c', [(0, 1), (1, 0)])  25.4 us
    ppermute x10, waiting for transfers between devices, swap_bits(): lax.ppermute(x, axis, [(i, i ^ bits) for i in range(lax.axis_size(axis))])  20.2 us
    pallas_call x1, Pallas kernels, local(): pl.pallas_call(pair_kernel, in_specs=[SMEM, SMEM, vmem, vmem, vmem] + [AN...  18.5 us
    ppermute x10, starting transfers between devices, swap_bits(): lax.ppermute(x, axis, [(i, i ^ bits) for i in range(lax.axis_size(axis))])  9.37 us
    ppermute x11, waiting for transfers between devices, swap(): return lax.ppermute(x, 'c', [(0, 1), (1, 0)])  7.04 us
  transfers between devices with their start and end apart: 47, of which 18 were waited for; matrix products, arithmetic and copies ran while one was open for 7% of the time, Pallas kernels for 2%

profile of v5, /device:TPU:1, one launch (start us, length us, event | category | flops | bytes accessed | tf_op | source)
XLA Modules:
  0.0 183.8 jit_solution(6920512001236750010)
XLA Ops:
  3.3 3.6 %collective-permute-start.17 = (bf16[288,384]{1,0:T(8,128)(2,1)S(1)}, bf16[288,384]{1,0:T(8,128)(2,1)S(1)}, u32[]{:S(2)}, u32[]{:S(2)}) collective-permute-start(bf16[288,384]{1,0:T(8,128)(2,1)S(1)} %get-tuple-element.18), channel_id=1, source_target_pairs={{0,0},{1,32},{2,24},{3,56},{4,16},{5,48},{6,8},{7,40},{8,10},{9,42... | collective-permute-start | bytes 663560 | tf_op jit(solution)/shard_map/ppermute | solution.py:181
  14.1 10.2 %collective-permute-start.10 = (bf16[288,384]{1,0:T(8,128)(2,1)S(1)}, bf16[288,384]{1,0:T(8,128)(2,1)S(1)}, u32[]{:S(2)}, u32[]{:S(2)}) collective-permute-start(bf16[288,384]{1,0:T(8,128)(2,1)S(1)} %collective-permute-done.7), channel_id=1, source_target_pairs={{0,24},{8,0},{16,8},{24,16},{1,25},{9,1},{17,9},{25,17},{2,26},{10... | collective-permute-start | bytes 663560 | tf_op jit(solution)/shard_map/ppermute | solution.py:21
  25.4 2.5 %collective-permute-start.2 = (bf16[2,288,384]{2,1,0:T(8,128)(2,1)S(1)}, bf16[2,288,384]{2,1,0:T(8,128)(2,1)S(1)}, u32[]{:S(2)}, u32[]{:S(2)}) collective-permute-start(bf16[2,288,384]{2,1,0:T(8,128)(2,1)S(1)} %bitcast.41), channel_id=1, source_target_pairs={{0,6},{2,0},{4,2},{6,4},{1,7},{3,1},{5,3},{7,5},{8,14},{10,8},{12,... | collective-permute-start | bytes 1327112 | tf_op jit(solution)/shard_map/ppermute | solution.py:21
  29.6 4.7 %collective-permute-done.10 = bf16[288,384]{1,0:T(8,128)(2,1)S(1)} collective-permute-done((bf16[288,384]{1,0:T(8,128)(2,1)S(1)}, bf16[288,384]{1,0:T(8,128)(2,1)S(1)}, u32[]{:S(2)}, u32[]{:S(2)}) %collective-permute-start.10) | collective-permute-done | bytes 221216 | tf_op jit(solution)/shard_map/ppermute | solution.py:21
  38.0 5.2 %collective-permute-done.8 = bf16[288,384]{1,0:T(8,128)(2,1)S(1)} collective-permute-done((bf16[288,384]{1,0:T(8,128)(2,1)S(1)}, bf16[288,384]{1,0:T(8,128)(2,1)S(1)}, u32[]{:S(2)}, u32[]{:S(2)}) %collective-permute-start.8) | collective-permute-done | bytes 221216 | tf_op jit(solution)/shard_map/ppermute | solution.py:21
  43.2 3.1 %collective-permute-start.19 = (bf16[288,384]{1,0:T(8,128)(2,1)S(1)}, bf16[288,384]{1,0:T(8,128)(2,1)S(1)}, u32[]{:S(2)}, u32[]{:S(2)}) collective-permute-start(bf16[288,384]{1,0:T(8,128)(2,1)S(1)} %collective-permute-done.17), channel_id=1, source_target_pairs={{0,64},{32,96},{64,0},{96,32},{1,65},{33,97},{65,1},{97,33},{2,66}... | collective-permute-start | bytes 663560 | tf_op jit(solution)/shard_map/ppermute | solution.py:21
  46.4 4.2 %collective-permute-done.19 = bf16[288,384]{1,0:T(8,128)(2,1)S(1)} collective-permute-done((bf16[288,384]{1,0:T(8,128)(2,1)S(1)}, bf16[288,384]{1,0:T(8,128)(2,1)S(1)}, u32[]{:S(2)}, u32[]{:S(2)}) %collective-permute-start.19) | collective-permute-done | bytes 221216 | tf_op jit(solution)/shard_map/ppermute | solution.py:21
  56.0 4.3 %collective-permute-done.16.refs_6_ = bf16[2,288,384]{2,1,0:T(8,128)(2,1)S(1)} collective-permute-done((bf16[2,288,384]{2,1,0:T(8,128)(2,1)S(1)}, bf16[2,288,384]{2,1,0:T(8,128)(2,1)S(1)}, u32[]{:S(2)}, u32[]{:S(2)}) %collective-permute-start.16) | collective-permute-done | bytes 442400 | tf_op jit(solution)/shard_map/ppermute | solution.py:21
  63.8 6.0 %collective-permute-done.14.refs_7_ = bf16[2,288,384]{2,1,0:T(8,128)(2,1)S(1)} collective-permute-done((bf16[2,288,384]{2,1,0:T(8,128)(2,1)S(1)}, bf16[2,288,384]{2,1,0:T(8,128)(2,1)S(1)}, u32[]{:S(2)}, u32[]{:S(2)}) %collective-permute-start.14) | collective-permute-done | bytes 442400 | tf_op jit(solution)/shard_map/ppermute | solution.py:21
  69.8 2.9 %collective-permute-start.6 = (bf16[2,288,384]{2,1,0:T(8,128)(2,1)S(1)}, bf16[2,288,384]{2,1,0:T(8,128)(2,1)S(1)}, u32[]{:S(2)}, u32[]{:S(2)}) collective-permute-start(bf16[2,288,384]{2,1,0:T(8,128)(2,1)S(1)} %collective-permute-done.2.refs_3_), channel_id=1, source_target_pairs={{0,1},{1,0},{2,3},{3,2},{4,5},{5,4},{6,7},{7,6},{8,9},{9,8},{10,11... | collective-permute-start | bytes 1327112 | tf_op jit(solution)/shard_map/ppermute | solution.py:25
  79.6 2.7 %collective-permute-start.15 = (bf16[2,288,384]{2,1,0:T(8,128)(2,1)}, bf16[2,288,384]{2,1,0:T(8,128)(2,1)}, u32[]{:S(2)}, u32[]{:S(2)}) collective-permute-start(bf16[2,288,384]{2,1,0:T(8,128)(2,1)} %copy-done.9), channel_id=1, source_target_pairs={{0,96},{32,0},{64,32},{96,64},{1,97},{33,1},{65,33},{97,65},{2,98}... | collective-permute-start | bytes 1327112 | tf_op jit(solution)/shard_map/ppermute | solution.py:21
  82.6 2.4 %collective-permute-start.25 = (bf16[2,288,384]{2,1,0:T(8,128)(2,1)}, bf16[2,288,384]{2,1,0:T(8,128)(2,1)}, u32[]{:S(2)}, u32[]{:S(2)}) collective-permute-start(bf16[2,288,384]{2,1,0:T(8,128)(2,1)} %collective-permute-done.24.refs_15_), channel_id=1, source_target_pairs={{0,24},{8,0},{16,8},{24,16},{1,25},{9,1},{17,9},{25,17},{2,26},{10... | collective-permute-start | bytes 1327112 | tf_op jit(solution)/shard_map/ppermute | solution.py:21
  87.1 2.7 %turn.1.left_ref = bf16[768,2304]{1,0:T(8,128)(2,1)S(1)} custom-call(s32[8]{0:T(128)S(1)} %pad_add_fusion.slot_ref, bf16[2,288,384]{2,1,0:T(8,128)(2,1)S(1)} %bitcast.44, bf16[2,288,384]{2,1,0:T(8,128)(2,1)S(1)} %collective-permute-done.refs_1_, bf16[2,288,384]{2,1,0:T(8,128)(2,1)S(1)} %collective-permute-done.1.refs_2_, ...), custom_call_target="tpu_custom_call" | custom-call | bytes 7000000 | tf_op jit(solution)/shard_map/turn/pallas_call | solution.py:239
  89.8 2.5 %collective-permute-done.22.refs_11_ = bf16[2,288,384]{2,1,0:T(8,128)(2,1)} collective-permute-done((bf16[2,288,384]{2,1,0:T(8,128)(2,1)}, bf16[2,288,384]{2,1,0:T(8,128)(2,1)}, u32[]{:S(2)}, u32[]{:S(2)}) %collective-permute-start.22) | collective-permute-done | bytes 442400 | tf_op jit(solution)/shard_map/ppermute | solution.py:21
  92.3 9.4 %collective-permute-done.23.refs_12_ = bf16[2,288,384]{2,1,0:T(8,128)(2,1)} collective-permute-done((bf16[2,288,384]{2,1,0:T(8,128)(2,1)}, bf16[2,288,384]{2,1,0:T(8,128)(2,1)}, u32[]{:S(2)}, u32[]{:S(2)}) %collective-permute-start.23) | collective-permute-done | bytes 442400 | tf_op jit(solution)/shard_map/ppermute | solution.py:21
  101.8 18.5 %pairs.1 = (f32[2,288,768]{2,1,0:T(8,128)S(1)}, f32[2,288,768]{2,1,0:T(8,128)S(1)}, f32[2,288,768]{2,1,0:T(8,128)S(1)}, f32[2,288,768]{2,1,0:T(8,128)S(1)}, f32[...) custom-call(s32[25]{0:T(128)S(1)} %concatenate.9.place_ref, f32[16]{0:T(128)S(1)} %concatenate.10.scal_ref, ...), custom_call_target="tpu_custom_call" | custom-call | flops 11800000512 | bytes 18000000 | tf_op jit(solution)/shard_map/pairs/pallas_call | solution.py:252
  122.3 5.8 %collective-permute-done.32 = f32[192,384]{1,0:T(8,128)S(1)} collective-permute-done((f32[192,384]{1,0:T(8,128)S(1)}, f32[192,384]{1,0:T(8,128)S(1)}, u32[]{:S(2)}, u32[]{:S(2)}) %collective-permute-start.32) | collective-permute-done | bytes 294944 | tf_op jit(solution)/shard_map/ppermute | solution.py:25
  134.8 3.2 %collective-permute-done.36 = f32[48,384]{1,0:T(8,128)S(1)} collective-permute-done((f32[48,384]{1,0:T(8,128)S(1)}, f32[48,384]{1,0:T(8,128)S(1)}, u32[]{:S(2)}, u32[]{:S(2)}) %collective-permute-start.36) | collective-permute-done | bytes 73760 | tf_op jit(solution)/shard_map/ppermute | solution.py:170
  138.1 4.4 %collective-permute-done.37 = f32[48,384]{1,0:T(8,128)S(1)} collective-permute-done((f32[48,384]{1,0:T(8,128)S(1)}, f32[48,384]{1,0:T(8,128)S(1)}, u32[]{:S(2)}, u32[]{:S(2)}) %collective-permute-start.37) | collective-permute-done | bytes 73760 | tf_op jit(solution)/shard_map/ppermute | solution.py:170
  142.8 3.3 %collective-permute-done.38 = f32[48,384]{1,0:T(8,128)S(1)} collective-permute-done((f32[48,384]{1,0:T(8,128)S(1)}, f32[48,384]{1,0:T(8,128)S(1)}, u32[]{:S(2)}, u32[]{:S(2)}) %collective-permute-start.38) | collective-permute-done | bytes 73760 | tf_op jit(solution)/shard_map/ppermute | solution.py:170
  152.1 6.0 %collective-permute-start.43 = (f32[48,384]{1,0:T(8,128)S(1)}, f32[48,384]{1,0:T(8,128)S(1)}, u32[]{:S(2)}, u32[]{:S(2)}) collective-permute-start(f32[48,384]{1,0:T(8,128)S(1)} %add_multiply_fusion.refs_0_), channel_id=1, source_target_pairs={{0,1},{1,0},{2,3},{3,2},{4,5},{5,4},{6,7},{7,6},{8,9},{9,8},{10,11... | collective-permute-start | bytes 221192 | tf_op jit(solution)/shard_map/ppermute | solution.py:25
  161.9 6.0 %collective-permute-done.42.refs_3_ = f32[48,384]{1,0:T(8,128)S(1)} collective-permute-done((f32[48,384]{1,0:T(8,128)S(1)}, f32[48,384]{1,0:T(8,128)S(1)}, u32[]{:S(2)}, u32[]{:S(2)}) %collective-permute-start.42) | collective-permute-done | bytes 73760 | tf_op jit(solution)/shard_map/ppermute | solution.py:170
  167.9 8.8 %collective-permute-start.46 = (f32[48,384]{1,0:T(8,128)S(1)}, f32[48,384]{1,0:T(8,128)S(1)}, u32[]{:S(2)}, u32[]{:S(2)}) collective-permute-start(f32[48,384]{1,0:T(8,128)S(1)} %collective-permute-done.42.refs_3_), channel_id=1, source_target_pairs={{0,1},{1,0},{2,3},{3,2},{4,5},{5,4},{6,7},{7,6},{8,9},{9,8},{10,11... | collective-permute-start | bytes 221192 | tf_op jit(solution)/shard_map/ppermute | solution.py:25
  176.7 2.8 %collective-permute-start.45 = (f32[48,384]{1,0:T(8,128)S(1)}, f32[48,384]{1,0:T(8,128)S(1)}, u32[]{:S(2)}, u32[]{:S(2)}) collective-permute-start(f32[48,384]{1,0:T(8,128)S(1)} %collective-permute-done.41.refs_2_), channel_id=1, source_target_pairs={{0,1},{1,0},{2,3},{3,2},{4,5},{5,4},{6,7},{7,6},{8,9},{9,8},{10,11... | collective-permute-start | bytes 221192 | tf_op jit(solution)/shard_map/ppermute | solution.py:25
  (157 shorter events, 57.7 us)
Async XLA Ops:
  1.8 48.8 %collective-permute-start.3 = (bf16[2,288,384]{2,1,0:T(8,128)(2,1)S(1)}, bf16[2,288,384]{2,1,0:T(8,128)(2,1)S(1)}, u32[]{:S(2)}, u32[]{:S(2)}) collective-permute-start(bf16[2,288,384]{2,1,0:T(8,128)(2,1)S(1)} %bitcast.39), channel_id=1, source_target_pairs={{0,1},{1,0},{2,3},{3,2},{4,5},{5,4},{6,7},{7,6},{8,9},{9,8},{10,11... | collective-permute-start | bytes 1327112 | tf_op jit(solution)/shard_map/ppermute | solution.py:25
  12.4 13.0 %collective-permute-start.20 = (bf16[288,384]{1,0:T(8,128)(2,1)S(1)}, bf16[288,384]{1,0:T(8,128)(2,1)S(1)}, u32[]{:S(2)}, u32[]{:S(2)}) collective-permute-start(bf16[288,384]{1,0:T(8,128)(2,1)S(1)} %collective-permute-done.17), channel_id=1, source_target_pairs={{0,96},{32,0},{64,32},{96,64},{1,97},{33,1},{65,33},{97,65},{2,98}... | collective-permute-start | bytes 663560 | tf_op jit(solution)/shard_map/ppermute | solution.py:21
  12.4 15.5 %collective-permute-start.18 = (bf16[288,384]{1,0:T(8,128)(2,1)S(1)}, bf16[288,384]{1,0:T(8,128)(2,1)S(1)}, u32[]{:S(2)}, u32[]{:S(2)}) collective-permute-start(bf16[288,384]{1,0:T(8,128)(2,1)S(1)} %collective-permute-done.17), channel_id=1, source_target_pairs={{0,32},{32,64},{64,96},{96,0},{1,33},{33,65},{65,97},{97,1},{2,34}... | collective-permute-start | bytes 663560 | tf_op jit(solution)/shard_map/ppermute | solution.py:21
  14.1 20.2 %collective-permute-start.10 = (bf16[288,384]{1,0:T(8,128)(2,1)S(1)}, bf16[288,384]{1,0:T(8,128)(2,1)S(1)}, u32[]{:S(2)}, u32[]{:S(2)}) collective-permute-start(bf16[288,384]{1,0:T(8,128)(2,1)S(1)} %collective-permute-done.7), channel_id=1, source_target_pairs={{0,24},{8,0},{16,8},{24,16},{1,25},{9,1},{17,9},{25,17},{2,26},{10... | collective-permute-start | bytes 663560 | tf_op jit(solution)/shard_map/ppermute | solution.py:21
  25.4 26.7 %collective-permute-start.2 = (bf16[2,288,384]{2,1,0:T(8,128)(2,1)S(1)}, bf16[2,288,384]{2,1,0:T(8,128)(2,1)S(1)}, u32[]{:S(2)}, u32[]{:S(2)}) collective-permute-start(bf16[2,288,384]{2,1,0:T(8,128)(2,1)S(1)} %bitcast.41), channel_id=1, source_target_pairs={{0,6},{2,0},{4,2},{6,4},{1,7},{3,1},{5,3},{7,5},{8,14},{10,8},{12,... | collective-permute-start | bytes 1327112 | tf_op jit(solution)/shard_map/ppermute | solution.py:21
  27.9 25.7 %collective-permute-start.1 = (bf16[2,288,384]{2,1,0:T(8,128)(2,1)S(1)}, bf16[2,288,384]{2,1,0:T(8,128)(2,1)S(1)}, u32[]{:S(2)}, u32[]{:S(2)}) collective-permute-start(bf16[2,288,384]{2,1,0:T(8,128)(2,1)S(1)} %bitcast.42), channel_id=1, source_target_pairs={{0,4},{2,6},{4,0},{6,2},{1,5},{3,7},{5,1},{7,3},{8,12},{10,14},{12... | collective-permute-start | bytes 1327112 | tf_op jit(solution)/shard_map/ppermute | solution.py:21
  34.3 19.3 %collective-permute-start = (bf16[2,288,384]{2,1,0:T(8,128)(2,1)S(1)}, bf16[2,288,384]{2,1,0:T(8,128)(2,1)S(1)}, u32[]{:S(2)}, u32[]{:S(2)}) collective-permute-start(bf16[2,288,384]{2,1,0:T(8,128)(2,1)S(1)} %bitcast.43), channel_id=1, source_target_pairs={{0,2},{2,4},{4,6},{6,0},{1,3},{3,5},{5,7},{7,1},{8,10},{10,12},{12... | collective-permute-start | bytes 1327112 | tf_op jit(solution)/shard_map/ppermute | solution.py:21
  50.6 10.9 %collective-permute-start.11 = (bf16[2,288,384]{2,1,0:T(8,128)(2,1)S(1)}, bf16[2,288,384]{2,1,0:T(8,128)(2,1)S(1)}, u32[]{:S(2)}, u32[]{:S(2)}) collective-permute-start(bf16[2,288,384]{2,1,0:T(8,128)(2,1)S(1)} %pad_maximum_fusion.refs_0_), channel_id=1, source_target_pairs={{0,32},{32,64},{64,96},{96,0},{1,33},{33,65},{65,97},{97,1},{2,34}... | collective-permute-start | bytes 1327112 | tf_op jit(solution)/shard_map/ppermute | solution.py:21
  52.1 17.7 %collective-permute-start.14 = (bf16[2,288,384]{2,1,0:T(8,128)(2,1)S(1)}, bf16[2,288,384]{2,1,0:T(8,128)(2,1)S(1)}, u32[]{:S(2)}, u32[]{:S(2)}) collective-permute-start(bf16[2,288,384]{2,1,0:T(8,128)(2,1)S(1)} %pad_maximum_fusion.1.refs_1_), channel_id=1, source_target_pairs={{0,96},{32,0},{64,32},{96,64},{1,97},{33,1},{65,33},{97,65},{2,98}... | collective-permute-start | bytes 1327112 | tf_op jit(solution)/shard_map/ppermute | solution.py:21
  53.6 19.0 %collective-permute-start.12 = (bf16[2,288,384]{2,1,0:T(8,128)(2,1)S(1)}, bf16[2,288,384]{2,1,0:T(8,128)(2,1)S(1)}, u32[]{:S(2)}, u32[]{:S(2)}) collective-permute-start(bf16[2,288,384]{2,1,0:T(8,128)(2,1)S(1)} %pad_maximum_fusion.1.refs_1_), channel_id=1, source_target_pairs={{0,32},{32,64},{64,96},{96,0},{1,33},{33,65},{65,97},{97,1},{2,34}... | collective-permute-start | bytes 1327112 | tf_op jit(solution)/shard_map/ppermute | solution.py:21
  53.7 21.3 %collective-permute-start.26 = (bf16[2,288,384]{2,1,0:T(8,128)(2,1)}, bf16[2,288,384]{2,1,0:T(8,128)(2,1)S(1)}, u32[]{:S(2)}, u32[]{:S(2)}) collective-permute-start(bf16[2,288,384]{2,1,0:T(8,128)(2,1)} %pad_maximum_fusion.2.refs_8_), channel_id=1, source_target_pairs={{0,24},{8,0},{16,8},{24,16},{1,25},{9,1},{17,9},{25,17},{2,26},{10... | collective-permute-start | bytes 1327112 | tf_op jit(solution)/shard_map/ppermute | solution.py:21
  61.1 18.4 %collective-permute-start.21 = (bf16[2,288,384]{2,1,0:T(8,128)(2,1)}, bf16[2,288,384]{2,1,0:T(8,128)(2,1)}, u32[]{:S(2)}, u32[]{:S(2)}) collective-permute-start(bf16[2,288,384]{2,1,0:T(8,128)(2,1)} %pad_maximum_fusion.2.refs_8_), channel_id=1, source_target_pairs={{0,8},{8,16},{16,24},{24,0},{1,9},{9,17},{17,25},{25,1},{2,10},{10... | collective-permute-start | bytes 1327112 | tf_op jit(solution)/shard_map/ppermute | solution.py:21
  61.5 18.0 %collective-permute-start.24 = (bf16[2,288,384]{2,1,0:T(8,128)(2,1)}, bf16[2,288,384]{2,1,0:T(8,128)(2,1)}, u32[]{:S(2)}, u32[]{:S(2)}) collective-permute-start(bf16[2,288,384]{2,1,0:T(8,128)(2,1)} %pad_maximum_fusion.3.refs_9_), channel_id=1, source_target_pairs={{0,24},{8,0},{16,8},{24,16},{1,25},{9,1},{17,9},{25,17},{2,26},{10... | collective-permute-start | bytes 1327112 | tf_op jit(solution)/shard_map/ppermute | solution.py:21
  79.5 12.8 %collective-permute-start.22 = (bf16[2,288,384]{2,1,0:T(8,128)(2,1)}, bf16[2,288,384]{2,1,0:T(8,128)(2,1)}, u32[]{:S(2)}, u32[]{:S(2)}) collective-permute-start(bf16[2,288,384]{2,1,0:T(8,128)(2,1)} %pad_maximum_fusion.3.refs_9_), channel_id=1, source_target_pairs={{0,8},{8,16},{16,24},{24,0},{1,9},{9,17},{17,25},{25,1},{2,10},{10... | collective-permute-start | bytes 1327112 | tf_op jit(solution)/shard_map/ppermute | solution.py:21
  79.5 12.8 %collective-permute-start.13 = (bf16[2,288,384]{2,1,0:T(8,128)(2,1)}, bf16[2,288,384]{2,1,0:T(8,128)(2,1)}, u32[]{:S(2)}, u32[]{:S(2)}) collective-permute-start(bf16[2,288,384]{2,1,0:T(8,128)(2,1)} %copy-done.7), channel_id=1, source_target_pairs={{0,32},{32,64},{64,96},{96,0},{1,33},{33,65},{65,97},{97,1},{2,34}... | collective-permute-start | bytes 1327112 | tf_op jit(solution)/shard_map/ppermute | solution.py:21
  79.6 12.7 %collective-permute-start.15 = (bf16[2,288,384]{2,1,0:T(8,128)(2,1)}, bf16[2,288,384]{2,1,0:T(8,128)(2,1)}, u32[]{:S(2)}, u32[]{:S(2)}) collective-permute-start(bf16[2,288,384]{2,1,0:T(8,128)(2,1)} %copy-done.9), channel_id=1, source_target_pairs={{0,96},{32,0},{64,32},{96,64},{1,97},{33,1},{65,33},{97,65},{2,98}... | collective-permute-start | bytes 1327112 | tf_op jit(solution)/shard_map/ppermute | solution.py:21
  82.3 19.5 %collective-permute-start.23 = (bf16[2,288,384]{2,1,0:T(8,128)(2,1)}, bf16[2,288,384]{2,1,0:T(8,128)(2,1)}, u32[]{:S(2)}, u32[]{:S(2)}) collective-permute-start(bf16[2,288,384]{2,1,0:T(8,128)(2,1)} %collective-permute-done.21.refs_10_), channel_id=1, source_target_pairs={{0,8},{8,16},{16,24},{24,0},{1,9},{9,17},{17,25},{25,1},{2,10},{10... | collective-permute-start | bytes 1327112 | tf_op jit(solution)/shard_map/ppermute | solution.py:21
  82.6 19.2 %collective-permute-start.25 = (bf16[2,288,384]{2,1,0:T(8,128)(2,1)}, bf16[2,288,384]{2,1,0:T(8,128)(2,1)}, u32[]{:S(2)}, u32[]{:S(2)}) collective-permute-start(bf16[2,288,384]{2,1,0:T(8,128)(2,1)} %collective-permute-done.24.refs_15_), channel_id=1, source_target_pairs={{0,24},{8,0},{16,8},{24,16},{1,25},{9,1},{17,9},{25,17},{2,26},{10... | collective-permute-start | bytes 1327112 | tf_op jit(solution)/shard_map/ppermute | solution.py:21
  120.3 27.7 %collective-permute-start.27 = (f32[2,288,768]{2,1,0:T(8,128)S(1)}, f32[2,288,768]{2,1,0:T(8,128)S(1)}, u32[]{:S(2)}, u32[]{:S(2)}) collective-permute-start(f32[2,288,768]{2,1,0:T(8,128)S(1)} %get-tuple-element.9), channel_id=1, source_target_pairs={{0,1},{1,0},{2,3},{3,2},{4,5},{5,4},{6,7},{7,6},{8,9},{9,8},{10,11... | collective-permute-start | bytes 5308424 | tf_op jit(solution)/shard_map/ppermute | solution.py:25
  121.7 28.1 %collective-permute-start.28 = (f32[2,288,768]{2,1,0:T(8,128)S(1)}, f32[2,288,768]{2,1,0:T(8,128)S(1)}, u32[]{:S(2)}, u32[]{:S(2)}) collective-permute-start(f32[2,288,768]{2,1,0:T(8,128)S(1)} %get-tuple-element.11), channel_id=1, source_target_pairs={{0,1},{1,0},{2,3},{3,2},{4,5},{5,4},{6,7},{7,6},{8,9},{9,8},{10,11... | collective-permute-start | bytes 5308424 | tf_op jit(solution)/shard_map/ppermute | solution.py:25
  148.1 34.1 %collective-permute-start.30 = (bf16[288,768]{1,0:T(8,128)(2,1)S(1)}, bf16[288,768]{1,0:T(8,128)(2,1)S(1)}, u32[]{:S(2)}, u32[]{:S(2)}) collective-permute-start(bf16[288,768]{1,0:T(8,128)(2,1)S(1)} %fusion.8), channel_id=1, source_target_pairs={{0,6},{2,0},{4,2},{6,4},{1,7},{3,1},{5,3},{7,5},{8,14},{10,8},{12,... | collective-permute-start | bytes 1327112 | tf_op jit(solution)/shard_map/ppermute | solution.py:21
  150.2 32.0 %collective-permute-start.29 = (bf16[288,768]{1,0:T(8,128)(2,1)S(1)}, bf16[288,768]{1,0:T(8,128)(2,1)S(1)}, u32[]{:S(2)}, u32[]{:S(2)}) collective-permute-start(bf16[288,768]{1,0:T(8,128)(2,1)S(1)} %get-tuple-element.16), channel_id=1, source_target_pairs={{0,2},{2,4},{4,6},{6,0},{1,3},{3,5},{5,7},{7,1},{8,10},{10,12},{12... | collective-permute-start | bytes 1327112 | tf_op jit(solution)/shard_map/ppermute | solution.py:21
  150.2 31.9 %collective-permute-start.31 = (bf16[288,768]{1,0:T(8,128)(2,1)S(1)}, bf16[288,768]{1,0:T(8,128)(2,1)S(1)}, u32[]{:S(2)}, u32[]{:S(2)}) collective-permute-start(bf16[288,768]{1,0:T(8,128)(2,1)S(1)} %get-tuple-element.17), channel_id=1, source_target_pairs={{0,4},{2,6},{4,0},{6,2},{1,5},{3,7},{5,1},{7,3},{8,12},{10,14},{12... | collective-permute-start | bytes 1327112 | tf_op jit(solution)/shard_map/ppermute | solution.py:21
  167.9 11.6 %collective-permute-start.46 = (f32[48,384]{1,0:T(8,128)S(1)}, f32[48,384]{1,0:T(8,128)S(1)}, u32[]{:S(2)}, u32[]{:S(2)}) collective-permute-start(f32[48,384]{1,0:T(8,128)S(1)} %collective-permute-done.42.refs_3_), channel_id=1, source_target_pairs={{0,1},{1,0},{2,3},{3,2},{4,5},{5,4},{6,7},{7,6},{8,9},{9,8},{10,11... | collective-permute-start | bytes 221192 | tf_op jit(solution)/shard_map/ppermute | solution.py:25
  (44 other events, 434.8 us)

commit v6 on v5

--- a/solution.py
+++ b/solution.py
@@ -289,10 +289,13 @@
     for bits in (2, 3, 1):
         others[bits] = swap_bits(others[bits], "y", bits)
     own = (mine + others[1]) + (others[2] + others[3])
-    for axis in ("x", "z"):
-        for bits in (1, 3):
-            got = swap_bits(own, axis, bits)
-            own = own + got
+    for bits in (1, 3):
+        got = swap_bits(own, "x", bits)
+        own = own + got
+    got = {}
+    for bits in (2, 3, 1):
+        got[bits] = swap_bits(own, "z", bits)
+    own = (own + got[2]) + (got[1] + got[3])
     own = own / task_iblock.shape[0]
     chunks_of = [own]
     for bits in (2, 3, 1):

time: 184 us -> 183 us (level)
    ppermute x10 -> x11, waiting for transfers between devices: 20.2 us -> 18.2 us  [swap_bits(): lax.ppermute(x, axis, [(i, i ^ bits) for i in range(lax.axis_size(axis))])]
    ppermute x10 -> x11, starting transfers between devices: 9.37 us -> 11.2 us  [swap_bits(): lax.ppermute(x, axis, [(i, i ^ bits) for i in range(lax.axis_size(axis))])]
  transfers between devices with their start and end apart: 47 -> 48, of which waited for: 18 -> 17; matrix products, arithmetic and copies ran while one was open for 7% -> 7% of each run, Pallas kernels for 2% -> 2%
where the time goes in v6:
time: 183 us
  starting transfers between devices  79.1 us (43%)
  waiting for transfers between devices  62.5 us (34%)
  Pallas kernels  22.6 us (12%)
  local copies, waits for them, and re-layouts  10.9 us (6%)
  other arithmetic  6.5 us (4%)
    ppermute x24, starting transfers between devices, move(): return lax.ppermute(x, axis, [(i, (i + s) % n) for i in range(n)])  38.3 us
    ppermute x24, waiting for transfers between devices, move(): return lax.ppermute(x, axis, [(i, (i + s) % n) for i in range(n)])  36.9 us
    ppermute x11, starting transfers between devices, swap(): return lax.ppermute(x, 'c', [(0, 1), (1, 0)])  24 us
    pallas_call x1, Pallas kernels, local(): pl.pallas_call(pair_kernel, in_specs=[SMEM, SMEM, vmem, vmem, vmem] + [AN...  18.5 us
    ppermute x11, waiting for transfers between devices, swap_bits(): lax.ppermute(x, axis, [(i, i ^ bits) for i in range(lax.axis_size(axis))])  18.2 us
    ppermute x11, starting transfers between devices, swap_bits(): lax.ppermute(x, axis, [(i, i ^ bits) for i in range(lax.axis_size(axis))])  11.2 us
    ppermute x11, waiting for transfers between devices, swap(): return lax.ppermute(x, 'c', [(0, 1), (1, 0)])  7.04 us
  transfers between devices with their start and end apart: 48, of which 17 were waited for; matrix products, arithmetic and copies ran while one was open for 7% of the time, Pallas kernels for 2%

profile of v6, /device:TPU:1, one launch (start us, length us, event | category | flops | bytes accessed | tf_op | source)
XLA Modules:
  0.0 182.6 jit_solution(8504310372796378084)
XLA Ops:
  3.3 3.6 %collective-permute-start.17 = (bf16[288,384]{1,0:T(8,128)(2,1)S(1)}, bf16[288,384]{1,0:T(8,128)(2,1)S(1)}, u32[]{:S(2)}, u32[]{:S(2)}) collective-permute-start(bf16[288,384]{1,0:T(8,128)(2,1)S(1)} %get-tuple-element.18), channel_id=1, source_target_pairs={{0,0},{1,32},{2,24},{3,56},{4,16},{5,48},{6,8},{7,40},{8,10},{9,42... | collective-permute-start | bytes 663560 | tf_op jit(solution)/shard_map/ppermute | solution.py:181
  14.1 10.2 %collective-permute-start.10 = (bf16[288,384]{1,0:T(8,128)(2,1)S(1)}, bf16[288,384]{1,0:T(8,128)(2,1)S(1)}, u32[]{:S(2)}, u32[]{:S(2)}) collective-permute-start(bf16[288,384]{1,0:T(8,128)(2,1)S(1)} %collective-permute-done.7), channel_id=1, source_target_pairs={{0,24},{8,0},{16,8},{24,16},{1,25},{9,1},{17,9},{25,17},{2,26},{10... | collective-permute-start | bytes 663560 | tf_op jit(solution)/shard_map/ppermute | solution.py:21
  25.4 2.5 %collective-permute-start.2 = (bf16[2,288,384]{2,1,0:T(8,128)(2,1)S(1)}, bf16[2,288,384]{2,1,0:T(8,128)(2,1)S(1)}, u32[]{:S(2)}, u32[]{:S(2)}) collective-permute-start(bf16[2,288,384]{2,1,0:T(8,128)(2,1)S(1)} %bitcast.41), channel_id=1, source_target_pairs={{0,6},{2,0},{4,2},{6,4},{1,7},{3,1},{5,3},{7,5},{8,14},{10,8},{12,... | collective-permute-start | bytes 1327112 | tf_op jit(solution)/shard_map/ppermute | solution.py:21
  29.5 4.8 %collective-permute-done.10 = bf16[288,384]{1,0:T(8,128)(2,1)S(1)} collective-permute-done((bf16[288,384]{1,0:T(8,128)(2,1)S(1)}, bf16[288,384]{1,0:T(8,128)(2,1)S(1)}, u32[]{:S(2)}, u32[]{:S(2)}) %collective-permute-start.10) | collective-permute-done | bytes 221216 | tf_op jit(solution)/shard_map/ppermute | solution.py:21
  38.0 5.2 %collective-permute-done.8 = bf16[288,384]{1,0:T(8,128)(2,1)S(1)} collective-permute-done((bf16[288,384]{1,0:T(8,128)(2,1)S(1)}, bf16[288,384]{1,0:T(8,128)(2,1)S(1)}, u32[]{:S(2)}, u32[]{:S(2)}) %collective-permute-start.8) | collective-permute-done | bytes 221216 | tf_op jit(solution)/shard_map/ppermute | solution.py:21
  43.2 3.1 %collective-permute-start.19 = (bf16[288,384]{1,0:T(8,128)(2,1)S(1)}, bf16[288,384]{1,0:T(8,128)(2,1)S(1)}, u32[]{:S(2)}, u32[]{:S(2)}) collective-permute-start(bf16[288,384]{1,0:T(8,128)(2,1)S(1)} %collective-permute-done.17), channel_id=1, source_target_pairs={{0,64},{32,96},{64,0},{96,32},{1,65},{33,97},{65,1},{97,33},{2,66}... | collective-permute-start | bytes 663560 | tf_op jit(solution)/shard_map/ppermute | solution.py:21
  46.4 4.2 %collective-permute-done.19 = bf16[288,384]{1,0:T(8,128)(2,1)S(1)} collective-permute-done((bf16[288,384]{1,0:T(8,128)(2,1)S(1)}, bf16[288,384]{1,0:T(8,128)(2,1)S(1)}, u32[]{:S(2)}, u32[]{:S(2)}) %collective-permute-start.19) | collective-permute-done | bytes 221216 | tf_op jit(solution)/shard_map/ppermute | solution.py:21
  56.0 4.3 %collective-permute-done.16.refs_6_ = bf16[2,288,384]{2,1,0:T(8,128)(2,1)S(1)} collective-permute-done((bf16[2,288,384]{2,1,0:T(8,128)(2,1)S(1)}, bf16[2,288,384]{2,1,0:T(8,128)(2,1)S(1)}, u32[]{:S(2)}, u32[]{:S(2)}) %collective-permute-start.16) | collective-permute-done | bytes 442400 | tf_op jit(solution)/shard_map/ppermute | solution.py:21
  63.8 6.0 %collective-permute-done.14.refs_7_ = bf16[2,288,384]{2,1,0:T(8,128)(2,1)S(1)} collective-permute-done((bf16[2,288,384]{2,1,0:T(8,128)(2,1)S(1)}, bf16[2,288,384]{2,1,0:T(8,128)(2,1)S(1)}, u32[]{:S(2)}, u32[]{:S(2)}) %collective-permute-start.14) | collective-permute-done | bytes 442400 | tf_op jit(solution)/shard_map/ppermute | solution.py:21
  69.8 2.9 %collective-permute-start.6 = (bf16[2,288,384]{2,1,0:T(8,128)(2,1)S(1)}, bf16[2,288,384]{2,1,0:T(8,128)(2,1)S(1)}, u32[]{:S(2)}, u32[]{:S(2)}) collective-permute-start(bf16[2,288,384]{2,1,0:T(8,128)(2,1)S(1)} %collective-permute-done.2.refs_3_), channel_id=1, source_target_pairs={{0,1},{1,0},{2,3},{3,2},{4,5},{5,4},{6,7},{7,6},{8,9},{9,8},{10,11... | collective-permute-start | bytes 1327112 | tf_op jit(solution)/shard_map/ppermute | solution.py:25
  79.6 2.7 %collective-permute-start.15 = (bf16[2,288,384]{2,1,0:T(8,128)(2,1)}, bf16[2,288,384]{2,1,0:T(8,128)(2,1)}, u32[]{:S(2)}, u32[]{:S(2)}) collective-permute-start(bf16[2,288,384]{2,1,0:T(8,128)(2,1)} %copy-done.9), channel_id=1, source_target_pairs={{0,96},{32,0},{64,32},{96,64},{1,97},{33,1},{65,33},{97,65},{2,98}... | collective-permute-start | bytes 1327112 | tf_op jit(solution)/shard_map/ppermute | solution.py:21
  82.6 2.4 %collective-permute-start.25 = (bf16[2,288,384]{2,1,0:T(8,128)(2,1)}, bf16[2,288,384]{2,1,0:T(8,128)(2,1)}, u32[]{:S(2)}, u32[]{:S(2)}) collective-permute-start(bf16[2,288,384]{2,1,0:T(8,128)(2,1)} %collective-permute-done.24.refs_15_), channel_id=1, source_target_pairs={{0,24},{8,0},{16,8},{24,16},{1,25},{9,1},{17,9},{25,17},{2,26},{10... | collective-permute-start | bytes 1327112 | tf_op jit(solution)/shard_map/ppermute | solution.py:21
  87.1 2.7 %turn.1.left_ref = bf16[768,2304]{1,0:T(8,128)(2,1)S(1)} custom-call(s32[8]{0:T(128)S(1)} %pad_add_fusion.slot_ref, bf16[2,288,384]{2,1,0:T(8,128)(2,1)S(1)} %bitcast.44, bf16[2,288,384]{2,1,0:T(8,128)(2,1)S(1)} %collective-permute-done.refs_1_, bf16[2,288,384]{2,1,0:T(8,128)(2,1)S(1)} %collective-permute-done.1.refs_2_, ...), custom_call_target="tpu_custom_call" | custom-call | bytes 7000000 | tf_op jit(solution)/shard_map/turn/pallas_call | solution.py:239
  89.8 2.5 %collective-permute-done.22.refs_11_ = bf16[2,288,384]{2,1,0:T(8,128)(2,1)} collective-permute-done((bf16[2,288,384]{2,1,0:T(8,128)(2,1)}, bf16[2,288,384]{2,1,0:T(8,128)(2,1)}, u32[]{:S(2)}, u32[]{:S(2)}) %collective-permute-start.22) | collective-permute-done | bytes 442400 | tf_op jit(solution)/shard_map/ppermute | solution.py:21
  92.3 9.4 %collective-permute-done.23.refs_12_ = bf16[2,288,384]{2,1,0:T(8,128)(2,1)} collective-permute-done((bf16[2,288,384]{2,1,0:T(8,128)(2,1)}, bf16[2,288,384]{2,1,0:T(8,128)(2,1)}, u32[]{:S(2)}, u32[]{:S(2)}) %collective-permute-start.23) | collective-permute-done | bytes 442400 | tf_op jit(solution)/shard_map/ppermute | solution.py:21
  101.8 18.5 %pairs.1 = (f32[2,288,768]{2,1,0:T(8,128)S(1)}, f32[2,288,768]{2,1,0:T(8,128)S(1)}, f32[2,288,768]{2,1,0:T(8,128)S(1)}, f32[2,288,768]{2,1,0:T(8,128)S(1)}, f32[...) custom-call(s32[25]{0:T(128)S(1)} %concatenate.9.place_ref, f32[16]{0:T(128)S(1)} %concatenate.10.scal_ref, ...), custom_call_target="tpu_custom_call" | custom-call | flops 11800000512 | bytes 18000000 | tf_op jit(solution)/shard_map/pairs/pallas_call | solution.py:252
  122.3 5.8 %collective-permute-done.32 = f32[192,384]{1,0:T(8,128)S(1)} collective-permute-done((f32[192,384]{1,0:T(8,128)S(1)}, f32[192,384]{1,0:T(8,128)S(1)}, u32[]{:S(2)}, u32[]{:S(2)}) %collective-permute-start.32) | collective-permute-done | bytes 294944 | tf_op jit(solution)/shard_map/ppermute | solution.py:25
  134.8 3.2 %collective-permute-done.36 = f32[48,384]{1,0:T(8,128)S(1)} collective-permute-done((f32[48,384]{1,0:T(8,128)S(1)}, f32[48,384]{1,0:T(8,128)S(1)}, u32[]{:S(2)}, u32[]{:S(2)}) %collective-permute-start.36) | collective-permute-done | bytes 73760 | tf_op jit(solution)/shard_map/ppermute | solution.py:170
  138.1 4.4 %collective-permute-done.37 = f32[48,384]{1,0:T(8,128)S(1)} collective-permute-done((f32[48,384]{1,0:T(8,128)S(1)}, f32[48,384]{1,0:T(8,128)S(1)}, u32[]{:S(2)}, u32[]{:S(2)}) %collective-permute-start.37) | collective-permute-done | bytes 73760 | tf_op jit(solution)/shard_map/ppermute | solution.py:170
  151.0 5.4 %collective-permute-start.44 = (f32[48,384]{1,0:T(8,128)S(1)}, f32[48,384]{1,0:T(8,128)S(1)}, u32[]{:S(2)}, u32[]{:S(2)}) collective-permute-start(f32[48,384]{1,0:T(8,128)S(1)} %add_multiply_fusion.refs_0_), channel_id=1, source_target_pairs={{0,1},{1,0},{2,3},{3,2},{4,5},{5,4},{6,7},{7,6},{8,9},{9,8},{10,11... | collective-permute-start | bytes 221192 | tf_op jit(solution)/shard_map/ppermute | solution.py:25
  157.9 2.3 %collective-permute-start.42 = (f32[48,384]{1,0:T(8,128)S(1)}, f32[48,384]{1,0:T(8,128)S(1)}, u32[]{:S(2)}, u32[]{:S(2)}) collective-permute-start(f32[48,384]{1,0:T(8,128)S(1)} %add_multiply_fusion.refs_0_), channel_id=1, source_target_pairs={{0,6},{2,4},{4,2},{6,0},{1,7},{3,5},{5,3},{7,1},{8,14},{10,12},{12... | collective-permute-start | bytes 221192 | tf_op jit(solution)/shard_map/ppermute | solution.py:170
  160.2 7.3 %collective-permute-done.43.refs_3_ = f32[48,384]{1,0:T(8,128)S(1)} collective-permute-done((f32[48,384]{1,0:T(8,128)S(1)}, f32[48,384]{1,0:T(8,128)S(1)}, u32[]{:S(2)}, u32[]{:S(2)}) %collective-permute-start.43) | collective-permute-done | bytes 73760 | tf_op jit(solution)/shard_map/ppermute | solution.py:170
  167.5 7.8 %collective-permute-start.47 = (f32[48,384]{1,0:T(8,128)S(1)}, f32[48,384]{1,0:T(8,128)S(1)}, u32[]{:S(2)}, u32[]{:S(2)}) collective-permute-start(f32[48,384]{1,0:T(8,128)S(1)} %collective-permute-done.43.refs_3_), channel_id=1, source_target_pairs={{0,1},{1,0},{2,3},{3,2},{4,5},{5,4},{6,7},{7,6},{8,9},{9,8},{10,11... | collective-permute-start | bytes 221192 | tf_op jit(solution)/shard_map/ppermute | solution.py:25
  175.4 2.9 %collective-permute-start.46 = (f32[48,384]{1,0:T(8,128)S(1)}, f32[48,384]{1,0:T(8,128)S(1)}, u32[]{:S(2)}, u32[]{:S(2)}) collective-permute-start(f32[48,384]{1,0:T(8,128)S(1)} %collective-permute-done.42.refs_2_), channel_id=1, source_target_pairs={{0,1},{1,0},{2,3},{3,2},{4,5},{5,4},{6,7},{7,6},{8,9},{9,8},{10,11... | collective-permute-start | bytes 221192 | tf_op jit(solution)/shard_map/ppermute | solution.py:25
  (158 shorter events, 57.5 us)
Async XLA Ops:
  1.8 48.8 %collective-permute-start.3 = (bf16[2,288,384]{2,1,0:T(8,128)(2,1)S(1)}, bf16[2,288,384]{2,1,0:T(8,128)(2,1)S(1)}, u32[]{:S(2)}, u32[]{:S(2)}) collective-permute-start(bf16[2,288,384]{2,1,0:T(8,128)(2,1)S(1)} %bitcast.39), channel_id=1, source_target_pairs={{0,1},{1,0},{2,3},{3,2},{4,5},{5,4},{6,7},{7,6},{8,9},{9,8},{10,11... | collective-permute-start | bytes 1327112 | tf_op jit(solution)/shard_map/ppermute | solution.py:25
  12.3 13.1 %collective-permute-start.20 = (bf16[288,384]{1,0:T(8,128)(2,1)S(1)}, bf16[288,384]{1,0:T(8,128)(2,1)S(1)}, u32[]{:S(2)}, u32[]{:S(2)}) collective-permute-start(bf16[288,384]{1,0:T(8,128)(2,1)S(1)} %collective-permute-done.17), channel_id=1, source_target_pairs={{0,96},{32,0},{64,32},{96,64},{1,97},{33,1},{65,33},{97,65},{2,98}... | collective-permute-start | bytes 663560 | tf_op jit(solution)/shard_map/ppermute | solution.py:21
  12.4 15.6 %collective-permute-start.18 = (bf16[288,384]{1,0:T(8,128)(2,1)S(1)}, bf16[288,384]{1,0:T(8,128)(2,1)S(1)}, u32[]{:S(2)}, u32[]{:S(2)}) collective-permute-start(bf16[288,384]{1,0:T(8,128)(2,1)S(1)} %collective-permute-done.17), channel_id=1, source_target_pairs={{0,32},{32,64},{64,96},{96,0},{1,33},{33,65},{65,97},{97,1},{2,34}... | collective-permute-start | bytes 663560 | tf_op jit(solution)/shard_map/ppermute | solution.py:21
  14.1 20.2 %collective-permute-start.10 = (bf16[288,384]{1,0:T(8,128)(2,1)S(1)}, bf16[288,384]{1,0:T(8,128)(2,1)S(1)}, u32[]{:S(2)}, u32[]{:S(2)}) collective-permute-start(bf16[288,384]{1,0:T(8,128)(2,1)S(1)} %collective-permute-done.7), channel_id=1, source_target_pairs={{0,24},{8,0},{16,8},{24,16},{1,25},{9,1},{17,9},{25,17},{2,26},{10... | collective-permute-start | bytes 663560 | tf_op jit(solution)/shard_map/ppermute | solution.py:21
  25.4 26.7 %collective-permute-start.2 = (bf16[2,288,384]{2,1,0:T(8,128)(2,1)S(1)}, bf16[2,288,384]{2,1,0:T(8,128)(2,1)S(1)}, u32[]{:S(2)}, u32[]{:S(2)}) collective-permute-start(bf16[2,288,384]{2,1,0:T(8,128)(2,1)S(1)} %bitcast.41), channel_id=1, source_target_pairs={{0,6},{2,0},{4,2},{6,4},{1,7},{3,1},{5,3},{7,5},{8,14},{10,8},{12,... | collective-permute-start | bytes 1327112 | tf_op jit(solution)/shard_map/ppermute | solution.py:21
  27.9 25.7 %collective-permute-start.1 = (bf16[2,288,384]{2,1,0:T(8,128)(2,1)S(1)}, bf16[2,288,384]{2,1,0:T(8,128)(2,1)S(1)}, u32[]{:S(2)}, u32[]{:S(2)}) collective-permute-start(bf16[2,288,384]{2,1,0:T(8,128)(2,1)S(1)} %bitcast.42), channel_id=1, source_target_pairs={{0,4},{2,6},{4,0},{6,2},{1,5},{3,7},{5,1},{7,3},{8,12},{10,14},{12... | collective-permute-start | bytes 1327112 | tf_op jit(solution)/shard_map/ppermute | solution.py:21
  34.3 19.3 %collective-permute-start = (bf16[2,288,384]{2,1,0:T(8,128)(2,1)S(1)}, bf16[2,288,384]{2,1,0:T(8,128)(2,1)S(1)}, u32[]{:S(2)}, u32[]{:S(2)}) collective-permute-start(bf16[2,288,384]{2,1,0:T(8,128)(2,1)S(1)} %bitcast.43), channel_id=1, source_target_pairs={{0,2},{2,4},{4,6},{6,0},{1,3},{3,5},{5,7},{7,1},{8,10},{10,12},{12... | collective-permute-start | bytes 1327112 | tf_op jit(solution)/shard_map/ppermute | solution.py:21
  50.6 10.9 %collective-permute-start.11 = (bf16[2,288,384]{2,1,0:T(8,128)(2,1)S(1)}, bf16[2,288,384]{2,1,0:T(8,128)(2,1)S(1)}, u32[]{:S(2)}, u32[]{:S(2)}) collective-permute-start(bf16[2,288,384]{2,1,0:T(8,128)(2,1)S(1)} %pad_maximum_fusion.refs_0_), channel_id=1, source_target_pairs={{0,32},{32,64},{64,96},{96,0},{1,33},{33,65},{65,97},{97,1},{2,34}... | collective-permute-start | bytes 1327112 | tf_op jit(solution)/shard_map/ppermute | solution.py:21
  52.1 17.7 %collective-permute-start.14 = (bf16[2,288,384]{2,1,0:T(8,128)(2,1)S(1)}, bf16[2,288,384]{2,1,0:T(8,128)(2,1)S(1)}, u32[]{:S(2)}, u32[]{:S(2)}) collective-permute-start(bf16[2,288,384]{2,1,0:T(8,128)(2,1)S(1)} %pad_maximum_fusion.1.refs_1_), channel_id=1, source_target_pairs={{0,96},{32,0},{64,32},{96,64},{1,97},{33,1},{65,33},{97,65},{2,98}... | collective-permute-start | bytes 1327112 | tf_op jit(solution)/shard_map/ppermute | solution.py:21
  53.6 19.0 %collective-permute-start.12 = (bf16[2,288,384]{2,1,0:T(8,128)(2,1)S(1)}, bf16[2,288,384]{2,1,0:T(8,128)(2,1)S(1)}, u32[]{:S(2)}, u32[]{:S(2)}) collective-permute-start(bf16[2,288,384]{2,1,0:T(8,128)(2,1)S(1)} %pad_maximum_fusion.1.refs_1_), channel_id=1, source_target_pairs={{0,32},{32,64},{64,96},{96,0},{1,33},{33,65},{65,97},{97,1},{2,34}... | collective-permute-start | bytes 1327112 | tf_op jit(solution)/shard_map/ppermute | solution.py:21
  53.7 21.3 %collective-permute-start.26 = (bf16[2,288,384]{2,1,0:T(8,128)(2,1)}, bf16[2,288,384]{2,1,0:T(8,128)(2,1)S(1)}, u32[]{:S(2)}, u32[]{:S(2)}) collective-permute-start(bf16[2,288,384]{2,1,0:T(8,128)(2,1)} %pad_maximum_fusion.2.refs_8_), channel_id=1, source_target_pairs={{0,24},{8,0},{16,8},{24,16},{1,25},{9,1},{17,9},{25,17},{2,26},{10... | collective-permute-start | bytes 1327112 | tf_op jit(solution)/shard_map/ppermute | solution.py:21
  61.1 18.5 %collective-permute-start.21 = (bf16[2,288,384]{2,1,0:T(8,128)(2,1)}, bf16[2,288,384]{2,1,0:T(8,128)(2,1)}, u32[]{:S(2)}, u32[]{:S(2)}) collective-permute-start(bf16[2,288,384]{2,1,0:T(8,128)(2,1)} %pad_maximum_fusion.2.refs_8_), channel_id=1, source_target_pairs={{0,8},{8,16},{16,24},{24,0},{1,9},{9,17},{17,25},{25,1},{2,10},{10... | collective-permute-start | bytes 1327112 | tf_op jit(solution)/shard_map/ppermute | solution.py:21
  61.5 18.0 %collective-permute-start.24 = (bf16[2,288,384]{2,1,0:T(8,128)(2,1)}, bf16[2,288,384]{2,1,0:T(8,128)(2,1)}, u32[]{:S(2)}, u32[]{:S(2)}) collective-permute-start(bf16[2,288,384]{2,1,0:T(8,128)(2,1)} %pad_maximum_fusion.3.refs_9_), channel_id=1, source_target_pairs={{0,24},{8,0},{16,8},{24,16},{1,25},{9,1},{17,9},{25,17},{2,26},{10... | collective-permute-start | bytes 1327112 | tf_op jit(solution)/shard_map/ppermute | solution.py:21
  79.5 12.8 %collective-permute-start.22 = (bf16[2,288,384]{2,1,0:T(8,128)(2,1)}, bf16[2,288,384]{2,1,0:T(8,128)(2,1)}, u32[]{:S(2)}, u32[]{:S(2)}) collective-permute-start(bf16[2,288,384]{2,1,0:T(8,128)(2,1)} %pad_maximum_fusion.3.refs_9_), channel_id=1, source_target_pairs={{0,8},{8,16},{16,24},{24,0},{1,9},{9,17},{17,25},{25,1},{2,10},{10... | collective-permute-start | bytes 1327112 | tf_op jit(solution)/shard_map/ppermute | solution.py:21
  79.5 12.8 %collective-permute-start.13 = (bf16[2,288,384]{2,1,0:T(8,128)(2,1)}, bf16[2,288,384]{2,1,0:T(8,128)(2,1)}, u32[]{:S(2)}, u32[]{:S(2)}) collective-permute-start(bf16[2,288,384]{2,1,0:T(8,128)(2,1)} %copy-done.7), channel_id=1, source_target_pairs={{0,32},{32,64},{64,96},{96,0},{1,33},{33,65},{65,97},{97,1},{2,34}... | collective-permute-start | bytes 1327112 | tf_op jit(solution)/shard_map/ppermute | solution.py:21
  79.6 12.7 %collective-permute-start.15 = (bf16[2,288,384]{2,1,0:T(8,128)(2,1)}, bf16[2,288,384]{2,1,0:T(8,128)(2,1)}, u32[]{:S(2)}, u32[]{:S(2)}) collective-permute-start(bf16[2,288,384]{2,1,0:T(8,128)(2,1)} %copy-done.9), channel_id=1, source_target_pairs={{0,96},{32,0},{64,32},{96,64},{1,97},{33,1},{65,33},{97,65},{2,98}... | collective-permute-start | bytes 1327112 | tf_op jit(solution)/shard_map/ppermute | solution.py:21
  82.3 19.5 %collective-permute-start.23 = (bf16[2,288,384]{2,1,0:T(8,128)(2,1)}, bf16[2,288,384]{2,1,0:T(8,128)(2,1)}, u32[]{:S(2)}, u32[]{:S(2)}) collective-permute-start(bf16[2,288,384]{2,1,0:T(8,128)(2,1)} %collective-permute-done.21.refs_10_), channel_id=1, source_target_pairs={{0,8},{8,16},{16,24},{24,0},{1,9},{9,17},{17,25},{25,1},{2,10},{10... | collective-permute-start | bytes 1327112 | tf_op jit(solution)/shard_map/ppermute | solution.py:21
  82.6 19.2 %collective-permute-start.25 = (bf16[2,288,384]{2,1,0:T(8,128)(2,1)}, bf16[2,288,384]{2,1,0:T(8,128)(2,1)}, u32[]{:S(2)}, u32[]{:S(2)}) collective-permute-start(bf16[2,288,384]{2,1,0:T(8,128)(2,1)} %collective-permute-done.24.refs_15_), channel_id=1, source_target_pairs={{0,24},{8,0},{16,8},{24,16},{1,25},{9,1},{17,9},{25,17},{2,26},{10... | collective-permute-start | bytes 1327112 | tf_op jit(solution)/shard_map/ppermute | solution.py:21
  120.3 26.2 %collective-permute-start.27 = (f32[2,288,768]{2,1,0:T(8,128)S(1)}, f32[2,288,768]{2,1,0:T(8,128)S(1)}, u32[]{:S(2)}, u32[]{:S(2)}) collective-permute-start(f32[2,288,768]{2,1,0:T(8,128)S(1)} %get-tuple-element.9), channel_id=1, source_target_pairs={{0,1},{1,0},{2,3},{3,2},{4,5},{5,4},{6,7},{7,6},{8,9},{9,8},{10,11... | collective-permute-start | bytes 5308424 | tf_op jit(solution)/shard_map/ppermute | solution.py:25
  121.8 26.8 %collective-permute-start.28 = (f32[2,288,768]{2,1,0:T(8,128)S(1)}, f32[2,288,768]{2,1,0:T(8,128)S(1)}, u32[]{:S(2)}, u32[]{:S(2)}) collective-permute-start(f32[2,288,768]{2,1,0:T(8,128)S(1)} %get-tuple-element.11), channel_id=1, source_target_pairs={{0,1},{1,0},{2,3},{3,2},{4,5},{5,4},{6,7},{7,6},{8,9},{9,8},{10,11... | collective-permute-start | bytes 5308424 | tf_op jit(solution)/shard_map/ppermute | solution.py:25
  146.6 34.3 %collective-permute-start.30 = (bf16[288,768]{1,0:T(8,128)(2,1)S(1)}, bf16[288,768]{1,0:T(8,128)(2,1)S(1)}, u32[]{:S(2)}, u32[]{:S(2)}) collective-permute-start(bf16[288,768]{1,0:T(8,128)(2,1)S(1)} %fusion.8), channel_id=1, source_target_pairs={{0,6},{2,0},{4,2},{6,4},{1,7},{3,1},{5,3},{7,5},{8,14},{10,8},{12,... | collective-permute-start | bytes 1327112 | tf_op jit(solution)/shard_map/ppermute | solution.py:21
  148.8 32.1 %collective-permute-start.29 = (bf16[288,768]{1,0:T(8,128)(2,1)S(1)}, bf16[288,768]{1,0:T(8,128)(2,1)S(1)}, u32[]{:S(2)}, u32[]{:S(2)}) collective-permute-start(bf16[288,768]{1,0:T(8,128)(2,1)S(1)} %get-tuple-element.16), channel_id=1, source_target_pairs={{0,2},{2,4},{4,6},{6,0},{1,3},{3,5},{5,7},{7,1},{8,10},{10,12},{12... | collective-permute-start | bytes 1327112 | tf_op jit(solution)/shard_map/ppermute | solution.py:21
  148.9 32.0 %collective-permute-start.31 = (bf16[288,768]{1,0:T(8,128)(2,1)S(1)}, bf16[288,768]{1,0:T(8,128)(2,1)S(1)}, u32[]{:S(2)}, u32[]{:S(2)}) collective-permute-start(bf16[288,768]{1,0:T(8,128)(2,1)S(1)} %get-tuple-element.17), channel_id=1, source_target_pairs={{0,4},{2,6},{4,0},{6,2},{1,5},{3,7},{5,1},{7,3},{8,12},{10,14},{12... | collective-permute-start | bytes 1327112 | tf_op jit(solution)/shard_map/ppermute | solution.py:21
  156.4 11.1 %collective-permute-start.43 = (f32[48,384]{1,0:T(8,128)S(1)}, f32[48,384]{1,0:T(8,128)S(1)}, u32[]{:S(2)}, u32[]{:S(2)}) collective-permute-start(f32[48,384]{1,0:T(8,128)S(1)} %add_multiply_fusion.refs_0_), channel_id=1, source_target_pairs={{0,4},{2,6},{4,0},{6,2},{1,5},{3,7},{5,1},{7,3},{8,12},{10,14},{12... | collective-permute-start | bytes 221192 | tf_op jit(solution)/shard_map/ppermute | solution.py:170
  (45 other events, 445.7 us)
